TPU v7x, 32 devices: a whole 2x2x4 slice. The times are simulated.
32 devices in a mesh: dp: 8 (over z, x), tensor: 4 (over y, core).
Axes of the slice: x: 2, y: 2, z: 4, core: 2. Of those that a mesh axis runs over, the one named last changes fastest.
Arguments:
- clips: bfloat16 [16, 16, 196, 768], P('dp', 'tensor'), may hold values from -6 to 6
- cotangent: bfloat16 [16, 16, 196, 768], P('dp', 'tensor'), may hold values from -6 to 6
- ln_gain: float32 [3, 768], replicated, may hold values from 0.5 to 1.5
- ln_shift: float32 [3, 768], replicated, may hold values from -2 to 2
- attn_qkv: bfloat16 [2, 3, 768, 768], P(None, None, None, 'tensor'), may hold values from -0.21875 to 0.21875
- attn_qv_bias: float32 [2, 2, 768], P(None, None, 'tensor'), may hold values from -2 to 2
- attn_out: bfloat16 [2, 768, 768], P(None, 'tensor'), may hold values from -0.875 to 0.875
- attn_out_bias: float32 [2, 768], replicated, may hold values from -2 to 2
- mlp_in: bfloat16 [768, 3072], P(None, 'tensor'), may hold values from -0.21875 to 0.21875
- mlp_in_bias: float32 [3072], P('tensor'), may hold values from -2 to 2
- mlp_out: bfloat16 [3072, 768], P('tensor'), may hold values from -0.109375 to 0.109375
- mlp_out_bias: float32 [768], replicated, may hold values from -2 to 2
Outputs:
- output: float32 [16, 16, 196, 768], P('dp', 'tensor')
- input_grad: float32 [16, 16, 196, 768], P('dp', 'tensor')
- grad_ln_gain: float32 [3, 768], replicated
- grad_ln_shift: float32 [3, 768], replicated
- grad_attn_qkv: float32 [2, 3, 768, 768], P(None, None, None, 'tensor')
- grad_attn_qv_bias: float32 [2, 2, 768], P(None, None, 'tensor')
- grad_attn_out: float32 [2, 768, 768], P(None, 'tensor')
- grad_attn_out_bias: float32 [2, 768], replicated
- grad_mlp_in: float32 [768, 3072], P(None, 'tensor')
- grad_mlp_in_bias: float32 [3072], P('tensor')
- grad_mlp_out: float32 [3072, 768], P('tensor')
- grad_mlp_out_bias: float32 [768], replicated
All inputs are finite; a program needn't handle non-finite values.
Results may differ from a plain program's by a relative error of at most 0.025.
Values may be sent and summed in bfloat16 or wider, within the bound.
A program may use at most 256 MiB of HBM per device.

v0:
```python
import jax
import jax.numpy as jnp
from jax import lax
from jax.sharding import PartitionSpec as P

HEAD_DIM = 64


norm_epsilon = 1e-06


def norm_layer(values, norm_gain, norm_shift):
    row_mean = jnp.mean(values, axis=-1, keepdims=True)
    centered = values - row_mean
    variance = jnp.mean(centered * centered, axis=-1, keepdims=True)
    return centered * lax.rsqrt(variance + norm_epsilon) * norm_gain + norm_shift


def exact_gelu(values):
    return jax.nn.gelu(values, approximate=False)


def pair_scores(first_side, second_side, temporal):
    if temporal:
        return jnp.einsum(
            "fphe,gphe->phfg", first_side, second_side, preferred_element_type=jnp.float32
        )
    return jnp.einsum(
        "fphe,fqhe->fhpq", first_side, second_side, preferred_element_type=jnp.float32
    )


def weigh_rows(shares, values, temporal):
    if temporal:
        return jnp.einsum("phfg,gphe->fphe", shares, values, preferred_element_type=jnp.float32)
    return jnp.einsum("fhpq,fqhe->fphe", shares, values, preferred_element_type=jnp.float32)


def weigh_cols(shares, values, temporal):
    if temporal:
        return jnp.einsum("phfg,fphe->gphe", shares, values, preferred_element_type=jnp.float32)
    return jnp.einsum("fhpq,fphe->fqhe", shares, values, preferred_element_type=jnp.float32)


def whole_inputs(shard):
    return lax.all_gather(shard, "tensor", axis=0, tiled=True)


def whole_grads(shard):
    return lax.all_gather(shard, "tensor", axis=0, tiled=True)


def branch_sum(values, weight):
    return lax.psum_scatter(
        jnp.einsum("fpe,ed->fpd", values, weight, preferred_element_type=jnp.float32),
        "tensor",
        scatter_dimension=0,
        tiled=True,
    )


def input_sum(grad_stack, weight_stack):
    return lax.psum_scatter(
        jnp.einsum(
            "cfpe,cde->fpd", grad_stack, weight_stack, preferred_element_type=jnp.float32
        ).astype(jnp.bfloat16),
        "tensor",
        scatter_dimension=0,
        tiled=True,
    ).astype(jnp.float32)


def attention_forward(gathered, w_qkv, b_qv, temporal):
    frames, places = (gathered.shape[0], gathered.shape[1])
    head_count = w_qkv.shape[2] // HEAD_DIM
    projected = jnp.einsum("fpd,cde->cfpe", gathered, w_qkv, preferred_element_type=jnp.float32)
    queries = (
        (projected[0] + b_qv[0]).astype(jnp.bfloat16).reshape(frames, places, head_count, HEAD_DIM)
    )
    key_vecs = projected[1].astype(jnp.bfloat16).reshape(frames, places, head_count, HEAD_DIM)
    value_vecs = (
        (projected[2] + b_qv[1]).astype(jnp.bfloat16).reshape(frames, places, head_count, HEAD_DIM)
    )
    scores = pair_scores(queries, key_vecs, temporal) * HEAD_DIM ** (-0.5)
    row_max = jnp.max(scores, axis=-1, keepdims=True)
    exponent = jnp.exp(scores - row_max)
    row_total = jnp.sum(exponent, axis=-1, keepdims=True)
    shares = (exponent / row_total).astype(jnp.bfloat16)
    log_total = row_max + jnp.log(row_total)
    context = (
        weigh_rows(shares, value_vecs, temporal)
        .astype(jnp.bfloat16)
        .reshape(frames, places, head_count * HEAD_DIM)
    )
    return (queries, key_vecs, value_vecs, log_total, context)


def attention_backward(gathered, forward_kept, w_out, grad_full, temporal):
    queries, key_vecs, value_vecs, log_total, context = forward_kept
    frames, places, head_count = (queries.shape[0], queries.shape[1], queries.shape[2])
    scale = HEAD_DIM ** (-0.5)
    grad_context = jnp.einsum("fpd,ed->fpe", grad_full, w_out, preferred_element_type=jnp.float32)
    grad_context = grad_context.astype(jnp.bfloat16).reshape(frames, places, head_count, HEAD_DIM)
    grad_wout = jnp.einsum("fpe,fpd->ed", context, grad_full, preferred_element_type=jnp.float32)
    shares = jnp.exp(pair_scores(queries, key_vecs, temporal) * scale - log_total)
    grad_shares = pair_scores(grad_context, value_vecs, temporal)
    grad_scores = shares * (grad_shares - jnp.sum(shares * grad_shares, axis=-1, keepdims=True))
    grad_scores = grad_scores.astype(jnp.bfloat16)
    grad_query = weigh_rows(grad_scores, key_vecs, temporal) * scale
    grad_key = weigh_cols(grad_scores, queries, temporal) * scale
    grad_value = weigh_cols(shares.astype(jnp.bfloat16), grad_context, temporal)
    grad_stack = jnp.stack([grad_query, grad_key, grad_value]).astype(jnp.bfloat16)
    grad_stack = grad_stack.reshape(3, frames, places, head_count * HEAD_DIM)
    grad_wqkv = jnp.einsum(
        "fpd,cfpe->cde", gathered, grad_stack, preferred_element_type=jnp.float32
    )
    grad_bias = jnp.stack(
        [
            jnp.sum(grad_stack[0], axis=(0, 1), dtype=jnp.float32),
            jnp.sum(grad_stack[2], axis=(0, 1), dtype=jnp.float32),
        ]
    )
    return (grad_stack, grad_wqkv, grad_bias, grad_wout)


def feed_forward(gathered, w_in, b_in):
    raised = jnp.einsum("fpd,dh->fph", gathered, w_in, preferred_element_type=jnp.float32) + b_in
    return (raised, exact_gelu(raised).astype(jnp.bfloat16))


def feed_backward(gathered, forward_kept, w_down, grad_full):
    raised, hidden = forward_kept
    grad_hidden = jnp.einsum("fpd,hd->fph", grad_full, w_down, preferred_element_type=jnp.float32)
    grad_raised = jax.vjp(exact_gelu, raised)[1](grad_hidden)[0].astype(jnp.bfloat16)
    grad_wdown = jnp.einsum("fph,fpd->hd", hidden, grad_full, preferred_element_type=jnp.float32)
    grad_win = jnp.einsum("fpd,fph->dh", gathered, grad_raised, preferred_element_type=jnp.float32)
    grad_bin = jnp.sum(grad_raised, axis=(0, 1), dtype=jnp.float32)
    return (grad_raised[None], grad_win, grad_bin, grad_wdown)


def norm_backward(stream, norm_gain, norm_shift, grad_normed):
    pull_back = jax.vjp(norm_layer, stream, norm_gain, norm_shift)[1]
    return pull_back(grad_normed)


def clip_pass(clip_in, clip_cot, params):
    gains, shifts, w_qkv, b_qv, w_out, b_out, w_in, b_in, w_down, b_down = params
    stream_zero = clip_in.astype(jnp.float32)
    normed_zero = norm_layer(stream_zero, gains[0], shifts[0]).astype(jnp.bfloat16)
    gathered_zero = whole_inputs(normed_zero)
    kept_zero = attention_forward(gathered_zero, w_qkv[0], b_qv[0], False)
    stream_one = stream_zero + (branch_sum(kept_zero[4], w_out[0]) + b_out[0])
    normed_one = norm_layer(stream_one, gains[1], shifts[1]).astype(jnp.bfloat16)
    gathered_one = whole_inputs(normed_one)
    kept_one = attention_forward(gathered_one, w_qkv[1], b_qv[1], True)
    stream_two = stream_one + (branch_sum(kept_one[4], w_out[1]) + b_out[1])
    normed_two = norm_layer(stream_two, gains[2], shifts[2]).astype(jnp.bfloat16)
    gathered_two = whole_inputs(normed_two)
    kept_two = feed_forward(gathered_two, w_in, b_in)
    result = stream_two + (branch_sum(kept_two[1], w_down) + b_down)
    grad_three = clip_cot.astype(jnp.float32)
    grad_full = whole_grads(grad_three.astype(jnp.bfloat16))
    grad_mlp, grad_win, grad_bin, grad_wdown = feed_backward(
        gathered_two, kept_two, w_down, grad_full
    )
    grad_bdown = jnp.sum(grad_three, axis=(0, 1))
    grad_normed = input_sum(grad_mlp, w_in[None])
    grad_stream, gain_two, shift_two = norm_backward(stream_two, gains[2], shifts[2], grad_normed)
    grad_two = grad_three + grad_stream
    grad_full = whole_grads(grad_two.astype(jnp.bfloat16))
    grad_mix_one, grad_wqkv_one, grad_bqv_one, grad_wout_one = attention_backward(
        gathered_one, kept_one, w_out[1], grad_full, True
    )
    grad_bout_one = jnp.sum(grad_two, axis=(0, 1))
    grad_normed = input_sum(grad_mix_one, w_qkv[1])
    grad_stream, gain_one, shift_one = norm_backward(stream_one, gains[1], shifts[1], grad_normed)
    grad_one = grad_two + grad_stream
    grad_full = whole_grads(grad_one.astype(jnp.bfloat16))
    grad_mix_zero, grad_wqkv_zero, grad_bqv_zero, grad_wout_zero = attention_backward(
        gathered_zero, kept_zero, w_out[0], grad_full, False
    )
    grad_bout_zero = jnp.sum(grad_one, axis=(0, 1))
    grad_normed = input_sum(grad_mix_zero, w_qkv[0])
    grad_stream, gain_zero, shift_zero = norm_backward(
        stream_zero, gains[0], shifts[0], grad_normed
    )
    grad_input = grad_one + grad_stream
    grads_clip = (
        jnp.stack([gain_zero, gain_one, gain_two]),
        jnp.stack([shift_zero, shift_one, shift_two]),
        jnp.stack([grad_wqkv_zero, grad_wqkv_one]),
        jnp.stack([grad_bqv_zero, grad_bqv_one]),
        jnp.stack([grad_wout_zero, grad_wout_one]),
        jnp.stack([grad_bout_zero, grad_bout_one]),
        grad_win,
        grad_bin,
        grad_wdown,
        grad_bdown,
    )
    return (result, grad_input, grads_clip)


def reduce_all(grads_in):
    split_sums = lax.psum(
        (grads_in[2], grads_in[3], grads_in[4], grads_in[6], grads_in[7], grads_in[8]), "dp"
    )
    shared_sums = lax.psum((grads_in[0], grads_in[1], grads_in[5], grads_in[9]), ("dp", "tensor"))
    return (
        shared_sums[0],
        shared_sums[1],
        split_sums[0],
        split_sums[1],
        split_sums[2],
        shared_sums[2],
        split_sums[3],
        split_sums[4],
        split_sums[5],
        shared_sums[3],
    )


def shards(
    clips,
    cotangent,
    ln_gain,
    ln_shift,
    attn_qkv,
    attn_qv_bias,
    attn_out,
    attn_out_bias,
    mlp_in,
    mlp_in_bias,
    mlp_out,
    mlp_out_bias,
):
    params = (
        ln_gain,
        ln_shift,
        attn_qkv,
        attn_qv_bias,
        attn_out,
        attn_out_bias,
        mlp_in,
        mlp_in_bias,
        mlp_out,
        mlp_out_bias,
    )
    zero_grads = jax.tree.map(lambda weight_arr: jnp.zeros(weight_arr.shape, jnp.float32), params)

    def per_clip(accum, clip_pair):
        result, grad_input, grads_clip = clip_pass(clip_pair[0], clip_pair[1], params)
        accum = jax.tree.map(jnp.add, accum, grads_clip)
        return (accum, (result, grad_input))

    accum, (results, input_grads) = lax.scan(per_clip, zero_grads, (clips, cotangent))
    accum = reduce_all(accum)
    return (
        results,
        input_grads,
        accum[0],
        accum[1],
        accum[2],
        accum[3],
        accum[4],
        accum[5],
        accum[6],
        accum[7],
        accum[8],
        accum[9],
    )


def solution(mesh):
    placed = (
        P("dp", "tensor", None, None),
        P("dp", "tensor", None, None),
        P(),
        P(),
        P(None, None, None, "tensor"),
        P(None, None, "tensor"),
        P(None, "tensor", None),
        P(),
        P(None, "tensor"),
        P("tensor"),
        P("tensor", None),
        P(),
    )
    return jax.shard_map(
        shards,
        mesh=mesh,
        in_specs=placed,
        out_specs=(
            P("dp", "tensor", None, None),
            P("dp", "tensor", None, None),
            P(),
            P(),
            P(None, None, None, "tensor"),
            P(None, None, "tensor"),
            P(None, "tensor", None),
            P(),
            P(None, "tensor"),
            P("tensor"),
            P("tensor", None),
            P(),
        ),
        check_vma=False,
    )
```

profile of v0, /device:TPU:0, one launch (start us, length us, event | category | flops | bytes accessed | tf_op | source)
XLA Modules:
  0.0 2050.7 jit_solution(5915735920981022298)
XLA Ops:
  8.1 1720.2 %while.33 = (s32[]{:T(128)}, f32[3,768]{1,0:T(4,128)}, f32[3,768]{1,0:T(4,128)}, f32[2,3,768,192]{2,3,1,0:T(8,128)}, f32[2,2,192]{2,1,0:T(2,128)}, /*index=5*/f3...) while((s32[]{:T(128)}, f32[3,768]{1,0:T(4,128)}, ...), condition=%wide.region_39.0_spmd.clone, body=%wide.region_0.39_spmd.clone.sunk | while | flops 46337245184 | bytes 1286530048 | solution.py:255
  14.9 41.2 %all-gather.11.cloned.1.call-done = bf16[16,196,768]{2,1,0:T(8,128)(2,1)} async-done(((bf16[4,196,768]{2,1,0:T(8,128)(2,1)}), bf16[16,196,768]{2,1,0:T(8,128)(2,1)}) %all-gather.11.cloned.1.call-update) | async-done | bytes 4816912 | tf_op jit(solution)/shard_map/while/body/eval_jaxpr/all_gather | solution.py:46
  79.0 80.5 %reduce-scatter.7.cloned.1.call-done = f32[4,196,768]{2,1,0:T(8,128)} async-done(((f32[16,196,768]{2,1,0:T(8,128)}), f32[4,196,768]{2,1,0:T(8,128)}) %reduce-scatter.7.cloned.1.call-update) | async-done | bytes 2408464 | tf_op jit(solution)/shard_map/while/body/eval_jaxpr/reduce_scatter | solution.py:54
  164.2 38.3 %all-gather.13.cloned.1.call-done = bf16[16,196,768]{2,1,0:T(8,128)(2,1)} async-done(((bf16[4,196,768]{2,1,0:T(8,128)(2,1)}), bf16[16,196,768]{2,1,0:T(8,128)(2,1)}) %all-gather.13.cloned.1.call-update) | async-done | bytes 4816912 | tf_op jit(solution)/shard_map/while/body/eval_jaxpr/all_gather | solution.py:46
  245.7 6.7 fusion.276
  252.5 81.1 %reduce-scatter.9.cloned.1.call-done = f32[4,196,768]{2,1,0:T(8,128)} async-done(((f32[16,196,768]{2,1,0:T(8,128)}), f32[4,196,768]{2,1,0:T(8,128)}) %reduce-scatter.9.cloned.1.call-update) | async-done | bytes 2408464 | tf_op jit(solution)/shard_map/while/body/eval_jaxpr/reduce_scatter | solution.py:54
  343.0 34.3 %all-gather.15.cloned.1.call-done = bf16[16,196,768]{2,1,0:T(8,128)(2,1)} async-done(((bf16[4,196,768]{2,1,0:T(8,128)(2,1)}), bf16[16,196,768]{2,1,0:T(8,128)(2,1)}) %all-gather.15.cloned.1.call-update) | async-done | bytes 4816912 | tf_op jit(solution)/shard_map/while/body/eval_jaxpr/all_gather | solution.py:46
  377.3 9.5 fusion.279
  390.9 23.7 %multiply_convert_fusion.11 = (bf16[16,196,768]{2,1,0:T(8,128)(2,1)}, f32[16,196,768]{2,1,0:T(8,128)}) fusion(f32[16,196,768]{2,1,0:T(8,128)S(1)} %get-tuple-element.708, f32[768]{0:T(1024)S(1)} %copy-done.87, u16[196,768]{1,0:T(8,128)(2,1)S(1)} %get-tuple-element.709, u16[196,768]{1,0:T(8,128)(2,1)S(1)} %get-tuple-element.710), kind=kLoop, calls=%fused_computation.9.clone.1 | loop fusion | flops 170999808 | bytes 24689664 | tf_op jit(solution)/shard_map/while/body/eval_jaxpr/convert_element_type | solution.py:128
  417.4 13.9 convert_reduce_fusion.20
  439.7 11.6 fusion.280
  451.4 37.3 %reduce-scatter.11.cloned.1.call-done = bf16[4,196,768]{2,1,0:T(8,128)(2,1)} async-done(((bf16[16,196,768]{2,1,0:T(8,128)(2,1)}), bf16[4,196,768]{2,1,0:T(8,128)(2,1)}) %reduce-scatter.11.cloned.1.call-update) | async-done | bytes 1204240 | tf_op jit(solution)/shard_map/while/body/eval_jaxpr/reduce_scatter | solution.py:63
  488.6 83.8 %reduce-scatter.13.cloned.1.call-done = f32[4,196,768]{2,1,0:T(8,128)} async-done(((f32[16,196,768]{2,1,0:T(8,128)}), f32[4,196,768]{2,1,0:T(8,128)}) %reduce-scatter.13.cloned.1.call-update) | async-done | bytes 2408464 | tf_op jit(solution)/shard_map/while/body/eval_jaxpr/reduce_scatter | solution.py:54
  584.4 37.4 %all-gather.19.cloned.1.call-done = bf16[16,196,768]{2,1,0:T(8,128)(2,1)} async-done(((bf16[4,196,768]{2,1,0:T(8,128)(2,1)}), bf16[16,196,768]{2,1,0:T(8,128)(2,1)}) %all-gather.19.cloned.1.call-update) | async-done | bytes 4816912 | tf_op jit(solution)/shard_map/while/body/eval_jaxpr/all_gather | solution.py:50
  631.7 6.8 multiply_reduce_fusion.16
  662.2 9.1 bitcast_convert_fusion.4
  671.3 49.3 %reduce-scatter.15.cloned.1.call-done = bf16[4,196,768]{2,1,0:T(8,128)(2,1)} async-done(((bf16[16,196,768]{2,1,0:T(8,128)(2,1)}), bf16[4,196,768]{2,1,0:T(8,128)(2,1)}) %reduce-scatter.15.cloned.1.call-update) | async-done | bytes 1204240 | tf_op jit(solution)/shard_map/while/body/eval_jaxpr/reduce_scatter | solution.py:63
  728.1 38.6 %all-gather.21.cloned.1.call-done = bf16[16,196,768]{2,1,0:T(8,128)(2,1)} async-done(((bf16[4,196,768]{2,1,0:T(8,128)(2,1)}), bf16[16,196,768]{2,1,0:T(8,128)(2,1)}) %all-gather.21.cloned.1.call-update) | async-done | bytes 4816912 | tf_op jit(solution)/shard_map/while/body/eval_jaxpr/all_gather | solution.py:50
  770.8 7.2 convert_reduce_fusion.25
  783.7 11.4 multiply_convert_fusion.13
  810.2 9.7 bitcast_add_fusion.5
  819.9 7.5 bitcast_add_fusion.4
  836.0 6.3 fusion.288
  873.6 38.5 %all-gather.11.cloned.1.call-done = bf16[16,196,768]{2,1,0:T(8,128)(2,1)} async-done(((bf16[4,196,768]{2,1,0:T(8,128)(2,1)}), bf16[16,196,768]{2,1,0:T(8,128)(2,1)}) %all-gather.11.cloned.1.call-update) | async-done | bytes 4816912 | tf_op jit(solution)/shard_map/while/body/eval_jaxpr/all_gather | solution.py:46
  934.9 80.5 %reduce-scatter.7.cloned.1.call-done = f32[4,196,768]{2,1,0:T(8,128)} async-done(((f32[16,196,768]{2,1,0:T(8,128)}), f32[4,196,768]{2,1,0:T(8,128)}) %reduce-scatter.7.cloned.1.call-update) | async-done | bytes 2408464 | tf_op jit(solution)/shard_map/while/body/eval_jaxpr/reduce_scatter | solution.py:54
  1020.2 38.3 %all-gather.13.cloned.1.call-done = bf16[16,196,768]{2,1,0:T(8,128)(2,1)} async-done(((bf16[4,196,768]{2,1,0:T(8,128)(2,1)}), bf16[16,196,768]{2,1,0:T(8,128)(2,1)}) %all-gather.13.cloned.1.call-update) | async-done | bytes 4816912 | tf_op jit(solution)/shard_map/while/body/eval_jaxpr/all_gather | solution.py:46
  1101.7 6.7 fusion.276
  1108.5 81.1 %reduce-scatter.9.cloned.1.call-done = f32[4,196,768]{2,1,0:T(8,128)} async-done(((f32[16,196,768]{2,1,0:T(8,128)}), f32[4,196,768]{2,1,0:T(8,128)}) %reduce-scatter.9.cloned.1.call-update) | async-done | bytes 2408464 | tf_op jit(solution)/shard_map/while/body/eval_jaxpr/reduce_scatter | solution.py:54
  1199.0 34.3 %all-gather.15.cloned.1.call-done = bf16[16,196,768]{2,1,0:T(8,128)(2,1)} async-done(((bf16[4,196,768]{2,1,0:T(8,128)(2,1)}), bf16[16,196,768]{2,1,0:T(8,128)(2,1)}) %all-gather.15.cloned.1.call-update) | async-done | bytes 4816912 | tf_op jit(solution)/shard_map/while/body/eval_jaxpr/all_gather | solution.py:46
  1233.3 9.5 fusion.279
  1246.8 23.7 %multiply_convert_fusion.11 = (bf16[16,196,768]{2,1,0:T(8,128)(2,1)}, f32[16,196,768]{2,1,0:T(8,128)}) fusion(f32[16,196,768]{2,1,0:T(8,128)S(1)} %get-tuple-element.708, f32[768]{0:T(1024)S(1)} %copy-done.87, u16[196,768]{1,0:T(8,128)(2,1)S(1)} %get-tuple-element.709, u16[196,768]{1,0:T(8,128)(2,1)S(1)} %get-tuple-element.710), kind=kLoop, calls=%fused_computation.9.clone.1 | loop fusion | flops 170999808 | bytes 24689664 | tf_op jit(solution)/shard_map/while/body/eval_jaxpr/convert_element_type | solution.py:128
  1273.3 13.9 convert_reduce_fusion.20
  1295.7 11.6 fusion.280
  1307.3 37.3 %reduce-scatter.11.cloned.1.call-done = bf16[4,196,768]{2,1,0:T(8,128)(2,1)} async-done(((bf16[16,196,768]{2,1,0:T(8,128)(2,1)}), bf16[4,196,768]{2,1,0:T(8,128)(2,1)}) %reduce-scatter.11.cloned.1.call-update) | async-done | bytes 1204240 | tf_op jit(solution)/shard_map/while/body/eval_jaxpr/reduce_scatter | solution.py:63
  1344.6 83.7 %reduce-scatter.13.cloned.1.call-done = f32[4,196,768]{2,1,0:T(8,128)} async-done(((f32[16,196,768]{2,1,0:T(8,128)}), f32[4,196,768]{2,1,0:T(8,128)}) %reduce-scatter.13.cloned.1.call-update) | async-done | bytes 2408464 | tf_op jit(solution)/shard_map/while/body/eval_jaxpr/reduce_scatter | solution.py:54
  1440.2 37.4 %all-gather.19.cloned.1.call-done = bf16[16,196,768]{2,1,0:T(8,128)(2,1)} async-done(((bf16[4,196,768]{2,1,0:T(8,128)(2,1)}), bf16[16,196,768]{2,1,0:T(8,128)(2,1)}) %all-gather.19.cloned.1.call-update) | async-done | bytes 4816912 | tf_op jit(solution)/shard_map/while/body/eval_jaxpr/all_gather | solution.py:50
  1487.5 6.8 multiply_reduce_fusion.16
  1518.0 9.1 bitcast_convert_fusion.4
  1527.1 49.3 %reduce-scatter.15.cloned.1.call-done = bf16[4,196,768]{2,1,0:T(8,128)(2,1)} async-done(((bf16[16,196,768]{2,1,0:T(8,128)(2,1)}), bf16[4,196,768]{2,1,0:T(8,128)(2,1)}) %reduce-scatter.15.cloned.1.call-update) | async-done | bytes 1204240 | tf_op jit(solution)/shard_map/while/body/eval_jaxpr/reduce_scatter | solution.py:63
  1583.9 38.6 %all-gather.21.cloned.1.call-done = bf16[16,196,768]{2,1,0:T(8,128)(2,1)} async-done(((bf16[4,196,768]{2,1,0:T(8,128)(2,1)}), bf16[16,196,768]{2,1,0:T(8,128)(2,1)}) %all-gather.21.cloned.1.call-update) | async-done | bytes 4816912 | tf_op jit(solution)/shard_map/while/body/eval_jaxpr/all_gather | solution.py:50
  1626.6 7.2 convert_reduce_fusion.25
  1639.5 11.4 multiply_convert_fusion.13
  1666.0 11.0 bitcast_add_fusion.5
  1677.0 7.4 bitcast_add_fusion.4
  1692.9 6.4 fusion.288
  1729.1 22.3 %all-reduce.1 = (f32[2,2,192]{2,1,0:T(2,128)}, f32[768]{0:T(1024)}) all-reduce(f32[2,2,192]{2,1,0:T(2,128)S(1)} %copy-done.84, f32[768]{0:T(1024)S(1)} %copy-done.81), channel_id=1, replica_groups=mesh['dp'=8,'tensor'=4] {'dp'}, use_global_device_ids=true, to_apply=%region_43.0 | all-reduce | flops 1536 | bytes 12288 | tf_op jit(solution)/shard_map/psum | solution.py:204
  1751.4 43.4 %all-reduce = (f32[3,768]{1,0:T(4,128)}, f32[3,768]{1,0:T(4,128)}, f32[2,768]{1,0:T(2,128)}, f32[768]{0:T(1024)}) all-reduce(f32[3,768]{1,0:T(4,128)S(1)} %copy-done.69, f32[3,768]{1,0:T(4,128)S(1)} %copy-done.66, f32[2,768]{1,0:T(2,128)S(1)} %copy-done.72, f32[768]{0:T(1024)S(1)} %copy-done.78), channel_id=1, replica_groups=mesh['dp'=8,'tensor'=4] {'dp','tensor'}, use_global_device_ids=true, to_apply=%region_40.0 | all-reduce | flops 6912 | bytes 55296 | tf_op jit(solution)/shard_map/psum | solution.py:207
  1794.8 240.1 %all-reduce.5.cloned.1.call-done = (f32[2,3,768,192]{2,3,1,0:T(8,128)}, f32[2,192,768]{2,1,0:T(8,128)}, f32[768,768]{1,0:T(8,128)}, f32[768,768]{1,0:T(8,128)}) async-done(((f32[2,3,768,192]{2,3,1,0:T(8,128)}, f32[2,192,768]{2,1,0:T(8,128)}, f32[768,768]{1,0:T(8,128)}, f32[768,768]{1,0:T(8,128)}), (f32[2,3,768,192]{2,3,1,0:T(8,128)}, f32[2,192,768]{2,1,0:T(8,128)}, f32[768,768]{1,0:T(8,128)}, ...) | async-done | bytes 9437200 | tf_op jit(solution)/shard_map/psum | solution.py:204
  (696 shorter events, 434.8 us)
Async XLA Ops:
  8.6 47.5 %all-gather.11.cloned.1.call-start = ((), (), s32[]{:S(2)}) async-start(), calls=%async_computation.7 | async-start | bytes 6144000 | tf_op jit(solution)/shard_map/while/body/eval_jaxpr/all_gather | solution.py:46
  12.1 44.0 %copy-start.89 = (bf16[2,3,768,192]{2,3,1,0:T(8,128)(2,1)S(1)}, bf16[2,3,768,192]{2,3,1,0:T(8,128)(2,1)}, u32[]{:S(2)}) copy-start(bf16[2,3,768,192]{2,3,1,0:T(8,128)(2,1)} %get-tuple-element.815) | copy-start | bytes 5308420 | tf_op jit(solution)/shard_map/while
  12.8 49.0 %copy-start.60 = (f32[4,196]{1,0:T(4,128)}, f32[4,196]{1,0:T(4,128)S(1)}, u32[]{:S(2)}) copy-start(f32[4,196]{1,0:T(4,128)S(1)} %fusion.263) | copy-start | bytes 9412 | tf_op jit(solution)/shard_map/while
  12.8 49.0 %copy-start.57 = (f32[4,196]{1,0:T(4,128)}, f32[4,196]{1,0:T(4,128)S(1)}, u32[]{:S(2)}) copy-start(f32[4,196]{1,0:T(4,128)S(1)} %fusion.264) | copy-start | bytes 9412 | tf_op jit(solution)/shard_map/while
  14.7 144.7 %reduce-scatter.7.cloned.1.call-start = ((), (), s32[]{:S(2)}) async-start(), calls=%async_computation.8 | async-start | bytes 12288000 | tf_op jit(solution)/shard_map/while/body/eval_jaxpr/reduce_scatter | solution.py:54
  14.9 48.0 %copy-start.62 = (f32[3,64]{1,0:T(4,128)}, f32[3,64]{1,0:T(4,128)S(1)}, u32[]{:S(2)}) copy-start(f32[3,64]{1,0:T(4,128)S(1)} %add.536) | copy-start | bytes 2308 | tf_op jit(solution)/shard_map/while
  14.9 52.4 %copy-start.73 = (f32[3,64]{1,0:T(4,128)}, f32[3,64]{1,0:T(4,128)S(1)}, u32[]{:S(2)}) copy-start(f32[3,64]{1,0:T(4,128)S(1)} %add.537) | copy-start | bytes 2308 | tf_op jit(solution)/shard_map/while
  78.3 124.3 %all-gather.13.cloned.1.call-start = ((), (), s32[]{:S(2)}) async-start(), calls=%async_computation.9 | async-start | bytes 6144000 | tf_op jit(solution)/shard_map/while/body/eval_jaxpr/all_gather | solution.py:46
  163.8 169.8 %reduce-scatter.9.cloned.1.call-start = ((), (), s32[]{:S(2)}) async-start(), calls=%async_computation.10 | async-start | bytes 12288000 | tf_op jit(solution)/shard_map/while/body/eval_jaxpr/reduce_scatter | solution.py:54
  252.4 124.9 %all-gather.15.cloned.1.call-start = ((), (), s32[]{:S(2)}) async-start(), calls=%async_computation.11 | async-start | bytes 6144000 | tf_op jit(solution)/shard_map/while/body/eval_jaxpr/all_gather | solution.py:46
  338.6 38.7 %copy-start.87 = (f32[768]{0:T(1024)S(1)}, f32[768]{0:T(1024)}, u32[]{:S(2)}) copy-start(f32[768]{0:T(1024)} %get-tuple-element.821) | copy-start | bytes 9220 | tf_op jit(solution)/shard_map/while
  338.6 78.7 %all-gather.17.cloned.1.call-start = ((), (), s32[]{:S(2)}) async-start(), calls=%async_computation.12 | async-start | bytes 6144000 | tf_op jit(solution)/shard_map/while/body/eval_jaxpr/all_gather | solution.py:50
  342.7 145.9 %reduce-scatter.11.cloned.1.call-start = ((), (), s32[]{:S(2)}) async-start(), calls=%async_computation.13 | async-start | bytes 6144000 | tf_op jit(solution)/shard_map/while/body/eval_jaxpr/reduce_scatter | solution.py:63
  417.4 16.1 copy-start.91
  439.3 133.2 %reduce-scatter.13.cloned.1.call-start = ((), (), s32[]{:S(2)}) async-start(), calls=%async_computation.14 | async-start | bytes 12288000 | tf_op jit(solution)/shard_map/while/body/eval_jaxpr/reduce_scatter | solution.py:54
  451.3 121.2 %copy-start.85 = (f32[768]{0:T(1024)S(1)}, f32[768]{0:T(1024)}, u32[]{:S(2)}) copy-start(f32[768]{0:T(1024)} %get-tuple-element.823) | copy-start | bytes 9220 | tf_op jit(solution)/shard_map/while
  451.3 170.5 %all-gather.19.cloned.1.call-start = ((), (), s32[]{:S(2)}) async-start(), calls=%async_computation.15 | async-start | bytes 6144000 | tf_op jit(solution)/shard_map/while/body/eval_jaxpr/all_gather | solution.py:50
  583.0 137.6 %reduce-scatter.15.cloned.1.call-start = ((), (), s32[]{:S(2)}) async-start(), calls=%async_computation.16 | async-start | bytes 6144000 | tf_op jit(solution)/shard_map/while/body/eval_jaxpr/reduce_scatter | solution.py:63
  671.3 95.4 %all-gather.21.cloned.1.call-start = ((), (), s32[]{:S(2)}) async-start(), calls=%async_computation.17 | async-start | bytes 6144000 | tf_op jit(solution)/shard_map/while/body/eval_jaxpr/all_gather | solution.py:50
  725.4 41.3 %copy-start.45 = (bf16[2,192,768]{2,1,0:T(8,128)(2,1)S(1)}, bf16[2,192,768]{2,1,0:T(8,128)(2,1)}, u32[]{:S(2)}) copy-start(bf16[2,192,768]{2,1,0:T(8,128)(2,1)} %get-tuple-element.818) | copy-start | bytes 1769476 | tf_op jit(solution)/shard_map/while
  728.0 130.1 %reduce-scatter.17.cloned.1.call-start = ((), (), s32[]{:S(2)}) async-start(), calls=%async_computation.18 | async-start | bytes 6144000 | tf_op jit(solution)/shard_map/while/body/eval_jaxpr/reduce_scatter | solution.py:63
  810.2 17.3 slice-start.11
  867.3 44.8 %all-gather.11.cloned.1.call-start = ((), (), s32[]{:S(2)}) async-start(), calls=%async_computation.7 | async-start | bytes 6144000 | tf_op jit(solution)/shard_map/while/body/eval_jaxpr/all_gather | solution.py:46
  870.8 41.3 %copy-start.89 = (bf16[2,3,768,192]{2,3,1,0:T(8,128)(2,1)S(1)}, bf16[2,3,768,192]{2,3,1,0:T(8,128)(2,1)}, u32[]{:S(2)}) copy-start(bf16[2,3,768,192]{2,3,1,0:T(8,128)(2,1)} %get-tuple-element.815) | copy-start | bytes 5308420 | tf_op jit(solution)/shard_map/while
  871.5 46.3 %copy-start.60 = (f32[4,196]{1,0:T(4,128)}, f32[4,196]{1,0:T(4,128)S(1)}, u32[]{:S(2)}) copy-start(f32[4,196]{1,0:T(4,128)S(1)} %fusion.263) | copy-start | bytes 9412 | tf_op jit(solution)/shard_map/while
  871.5 46.3 %copy-start.57 = (f32[4,196]{1,0:T(4,128)}, f32[4,196]{1,0:T(4,128)S(1)}, u32[]{:S(2)}) copy-start(f32[4,196]{1,0:T(4,128)S(1)} %fusion.264) | copy-start | bytes 9412 | tf_op jit(solution)/shard_map/while
  873.4 142.0 %reduce-scatter.7.cloned.1.call-start = ((), (), s32[]{:S(2)}) async-start(), calls=%async_computation.8 | async-start | bytes 12288000 | tf_op jit(solution)/shard_map/while/body/eval_jaxpr/reduce_scatter | solution.py:54
  873.5 45.3 %copy-start.62 = (f32[3,64]{1,0:T(4,128)}, f32[3,64]{1,0:T(4,128)S(1)}, u32[]{:S(2)}) copy-start(f32[3,64]{1,0:T(4,128)S(1)} %add.536) | copy-start | bytes 2308 | tf_op jit(solution)/shard_map/while
  873.6 49.7 %copy-start.73 = (f32[3,64]{1,0:T(4,128)}, f32[3,64]{1,0:T(4,128)S(1)}, u32[]{:S(2)}) copy-start(f32[3,64]{1,0:T(4,128)S(1)} %add.537) | copy-start | bytes 2308 | tf_op jit(solution)/shard_map/while
  934.2 124.3 %all-gather.13.cloned.1.call-start = ((), (), s32[]{:S(2)}) async-start(), calls=%async_computation.9 | async-start | bytes 6144000 | tf_op jit(solution)/shard_map/while/body/eval_jaxpr/all_gather | solution.py:46
  1019.8 169.8 %reduce-scatter.9.cloned.1.call-start = ((), (), s32[]{:S(2)}) async-start(), calls=%async_computation.10 | async-start | bytes 12288000 | tf_op jit(solution)/shard_map/while/body/eval_jaxpr/reduce_scatter | solution.py:54
  1108.4 124.9 %all-gather.15.cloned.1.call-start = ((), (), s32[]{:S(2)}) async-start(), calls=%async_computation.11 | async-start | bytes 6144000 | tf_op jit(solution)/shard_map/while/body/eval_jaxpr/all_gather | solution.py:46
  1194.6 38.7 %copy-start.87 = (f32[768]{0:T(1024)S(1)}, f32[768]{0:T(1024)}, u32[]{:S(2)}) copy-start(f32[768]{0:T(1024)} %get-tuple-element.821) | copy-start | bytes 9220 | tf_op jit(solution)/shard_map/while
  1194.6 78.7 %all-gather.17.cloned.1.call-start = ((), (), s32[]{:S(2)}) async-start(), calls=%async_computation.12 | async-start | bytes 6144000 | tf_op jit(solution)/shard_map/while/body/eval_jaxpr/all_gather | solution.py:50
  1198.7 145.9 %reduce-scatter.11.cloned.1.call-start = ((), (), s32[]{:S(2)}) async-start(), calls=%async_computation.13 | async-start | bytes 6144000 | tf_op jit(solution)/shard_map/while/body/eval_jaxpr/reduce_scatter | solution.py:63
  1295.2 133.1 %reduce-scatter.13.cloned.1.call-start = ((), (), s32[]{:S(2)}) async-start(), calls=%async_computation.14 | async-start | bytes 12288000 | tf_op jit(solution)/shard_map/while/body/eval_jaxpr/reduce_scatter | solution.py:54
  1307.3 121.0 %copy-start.85 = (f32[768]{0:T(1024)S(1)}, f32[768]{0:T(1024)}, u32[]{:S(2)}) copy-start(f32[768]{0:T(1024)} %get-tuple-element.823) | copy-start | bytes 9220 | tf_op jit(solution)/shard_map/while
  1307.3 170.3 %all-gather.19.cloned.1.call-start = ((), (), s32[]{:S(2)}) async-start(), calls=%async_computation.15 | async-start | bytes 6144000 | tf_op jit(solution)/shard_map/while/body/eval_jaxpr/all_gather | solution.py:50
  1438.9 137.6 %reduce-scatter.15.cloned.1.call-start = ((), (), s32[]{:S(2)}) async-start(), calls=%async_computation.16 | async-start | bytes 6144000 | tf_op jit(solution)/shard_map/while/body/eval_jaxpr/reduce_scatter | solution.py:63
  1527.1 95.4 %all-gather.21.cloned.1.call-start = ((), (), s32[]{:S(2)}) async-start(), calls=%async_computation.17 | async-start | bytes 6144000 | tf_op jit(solution)/shard_map/while/body/eval_jaxpr/all_gather | solution.py:50
  1581.3 41.3 %copy-start.45 = (bf16[2,192,768]{2,1,0:T(8,128)(2,1)S(1)}, bf16[2,192,768]{2,1,0:T(8,128)(2,1)}, u32[]{:S(2)}) copy-start(bf16[2,192,768]{2,1,0:T(8,128)(2,1)} %get-tuple-element.818) | copy-start | bytes 1769476 | tf_op jit(solution)/shard_map/while
  1583.8 133.6 %reduce-scatter.17.cloned.1.call-start = ((), (), s32[]{:S(2)}) async-start(), calls=%async_computation.18 | async-start | bytes 6144000 | tf_op jit(solution)/shard_map/while/body/eval_jaxpr/reduce_scatter | solution.py:63
  1666.0 18.5 slice-start.11
  1728.4 306.5 %all-reduce.5.cloned.1.call-start = ((), (), s32[]{:S(2)}) async-start(), calls=%async_computation.6 | async-start | bytes 18874368 | tf_op jit(solution)/shard_map/psum | solution.py:204
  1728.4 22.9 %copy-start.66 = (f32[3,768]{1,0:T(4,128)S(1)}, f32[3,768]{1,0:T(4,128)}, u32[]{:S(2)}) copy-start(f32[3,768]{1,0:T(4,128)} %get-tuple-element.153) | copy-start | bytes 27652
  1728.4 22.9 %copy-start.69 = (f32[3,768]{1,0:T(4,128)S(1)}, f32[3,768]{1,0:T(4,128)}, u32[]{:S(2)}) copy-start(f32[3,768]{1,0:T(4,128)} %get-tuple-element.152) | copy-start | bytes 27652
  1728.5 22.9 %copy-start.72 = (f32[2,768]{1,0:T(2,128)S(1)}, f32[2,768]{1,0:T(2,128)}, u32[]{:S(2)}) copy-start(f32[2,768]{1,0:T(2,128)} %get-tuple-element.157) | copy-start | bytes 18436
  1728.5 22.9 %copy-start.78 = (f32[768]{0:T(1024)S(1)}, f32[768]{0:T(1024)}, u32[]{:S(2)}) copy-start(f32[768]{0:T(1024)} %get-tuple-element.161) | copy-start | bytes 9220
  (180 other events, 812.9 us)
Sparse Core Ops, SparseCore 0:
  14.8 41.2 all-gather.10
  78.4 80.9 reduce-scatter.6
  163.9 38.5 all-gather.12
  252.6 80.9 reduce-scatter.8
  338.7 38.5 all-gather.14
  378.7 38.5 all-gather.16
  439.4 49.2 reduce-scatter.10
  491.5 80.9 reduce-scatter.12
  583.2 38.5 all-gather.18
  671.4 49.1 reduce-scatter.14
  728.1 38.5 all-gather.20
  808.8 49.1 reduce-scatter.16
  873.5 38.5 all-gather.10
  934.4 80.9 reduce-scatter.6
  1019.9 38.5 all-gather.12
  1108.5 80.9 reduce-scatter.8
  1194.7 38.5 all-gather.14
  1234.7 38.5 all-gather.16
  1295.3 49.2 reduce-scatter.10
  1347.3 80.9 reduce-scatter.12
  1439.0 38.5 all-gather.18
  1527.2 49.1 reduce-scatter.14
  1583.9 38.5 all-gather.20
  1664.6 49.1 reduce-scatter.16
Sparse Core Ops, SparseCore 1:
  1734.4 300.4 all-reduce.4
where the time goes:
time: 2050 us
  waiting for transfers between devices  1290 us (63%)
  matrix products  346 us (17%)
  local copies, waits for them, and re-layouts  170 us (8%)
  other arithmetic  157 us (8%)
  blocking collectives  65.6 us (3%)
    reduce_scatter x6, waiting for transfers between devices, branch_sum(): lax.psum_scatter(jnp.einsum('fpe,ed->fpd', values, weight, preferred_elem...  491 us
    psum x1, waiting for transfers between devices, reduce_all(): lax.psum((grads_in[2], grads_in[3], grads_in[4], grads_in[6], grads_in[7]...  240 us
    all_gather x6, waiting for transfers between devices, whole_inputs(): return lax.all_gather(shard, 'tensor', axis=0, tiled=True)  225 us
    reduce_scatter x6, waiting for transfers between devices, input_sum(): lax.psum_scatter(jnp.einsum('cfpe,cde->fpd', grad_stack, weight_stack, pr...  173 us
    all_gather x6, waiting for transfers between devices, whole_grads(): return lax.all_gather(shard, 'tensor', axis=0, tiled=True)  158 us
    while x388, local copies, waits for them, and re-layouts  48.1 us
    convert_element_type x2, other arithmetic, feed_forward(): return (raised, exact_gelu(raised).astype(jnp.bfloat16))  47.4 us
    dot_general x6, matrix products, branch_sum(): jnp.einsum('fpe,ed->fpd', values, weight, preferred_element_type=jnp.floa...  47.1 us
  transfers between devices with their start and end apart: 25, of which 24 were waited for; matrix products, arithmetic and copies ran while one was open for 9% of the time, Pallas kernels for 0%

commit v1 on v0

v1 whole, which is shorter than its diff:
```python
import jax
import jax.numpy as jnp
from jax import lax
from jax.sharding import PartitionSpec as P

HEAD_DIM = 64
norm_epsilon = 1e-06
ROWS = 200
HALF = 104
STEP = 96
BF = jnp.bfloat16
F32 = jnp.float32


def dot(spec, a, b):
    return jnp.einsum(spec, a, b, preferred_element_type=F32)


def norm_stats(values):
    mean = jnp.mean(values, axis=-1, keepdims=True)
    centered = values - mean
    inv = lax.rsqrt(jnp.mean(centered * centered, axis=-1, keepdims=True) + norm_epsilon)
    return centered * inv, inv


def norm_back(values, gain, grad):
    hat, inv = norm_stats(values)
    e = grad * gain
    dv = inv * (
        e - jnp.mean(e, axis=-1, keepdims=True) - hat * jnp.mean(e * hat, axis=-1, keepdims=True)
    )
    dims = tuple(range(grad.ndim - 1))
    return dv, jnp.sum(grad * hat, axis=dims), jnp.sum(grad, axis=dims)


def heads(v):
    return v.reshape(v.shape[:-1] + (v.shape[-1] // HEAD_DIM, HEAD_DIM))


def attention(normed, w, mask):
    wq, wk, wv, wo, bq, bv = w
    q = (dot("grd,ed->gre", normed, wq) + bq).astype(BF)
    k = dot("grd,ed->gre", normed, wk).astype(BF)
    v = (dot("grd,ed->gre", normed, wv) + bv).astype(BF)
    s = dot("gqhe,gkhe->ghqk", heads(q), heads(k)) * HEAD_DIM**-0.5
    s = jnp.where(mask, s, -1e30)
    top = jnp.max(s, axis=-1, keepdims=True)
    ex = jnp.exp(s - top)
    total = jnp.sum(ex, axis=-1, keepdims=True)
    p = (ex / total).astype(BF)
    o = dot("ghqk,gkhe->gqhe", p, heads(v)).astype(BF).reshape(normed.shape)
    return q, k, v, o, top + jnp.log(total)


def attention_back(normed, kept, w, mask, grad):
    wq, wk, wv, wo, bq, bv = w
    q, k, v, o, lse = kept
    shape = normed.shape
    do = dot("grd,ed->gre", grad, wo).astype(BF)
    gwo = dot("gre,grd->ed", o, grad)
    s = dot("gqhe,gkhe->ghqk", heads(q), heads(k)) * HEAD_DIM**-0.5
    p = jnp.where(mask, jnp.exp(s - lse), 0.0)
    dp = dot("gqhe,gkhe->ghqk", heads(do), heads(v))
    ds = (p * (dp - jnp.sum(p * dp, axis=-1, keepdims=True))).astype(BF)
    dq = (dot("ghqk,gkhe->gqhe", ds, heads(k)) * HEAD_DIM**-0.5).astype(BF).reshape(shape)
    dk = (dot("ghqk,gqhe->gkhe", ds, heads(q)) * HEAD_DIM**-0.5).astype(BF).reshape(shape)
    dv = dot("ghqk,gqhe->gkhe", p.astype(BF), heads(do)).astype(BF).reshape(shape)
    gq = dot("gre,grd->ed", dq, normed)
    gk = dot("gre,grd->ed", dk, normed)
    gv = dot("gre,grd->ed", dv, normed)
    dn = dot("gre,ed->grd", dq, wq) + dot("gre,ed->grd", dk, wk) + dot("gre,ed->grd", dv, wv)
    bias = (jnp.sum(dq, axis=(0, 1), dtype=F32), jnp.sum(dv, axis=(0, 1), dtype=F32))
    return dn.astype(BF), (gq, gk, gv, gwo), bias


def shards(clips, cot, gain, shift, qkv, qvb, wout, bout, win, b_in, wdown, bdown):
    tensor = lax.axis_index("tensor")
    y, core = tensor // 2, tensor % 2
    x = lax.axis_index("dp") % 2
    dp = lax.axis_size("dp")
    width = clips.shape[-1]
    places = clips.shape[2]

    def over_tensor(v, bit):
        return lax.ppermute(v, "tensor", [(i, i ^ bit) for i in range(4)])

    def over_dp(v, bit):
        return lax.ppermute(v, "dp", [(i, i ^ bit) for i in range(dp)])

    def pad(v):
        return jnp.pad(v, ((0, 0), (0, ROWS - places), (0, 0)))

    def split(a, b):
        return jnp.where(x == 0, a, b), jnp.where(x == 0, b, a)

    def whole_clip(v):
        mine = pad(lax.dynamic_index_in_dim(v, y, 0, False))
        other = pad(lax.dynamic_index_in_dim(v, 1 - y, 0, False))
        return jnp.concatenate([mine, over_tensor(other, 2)])

    def back(v):
        n = v.shape[0] // 2
        v = v[:, :places]
        got = over_tensor(v[n:], 2)
        a, b = v[:n], got
        first = jnp.where(y == 0, a, b)
        second = jnp.where(y == 0, b, a)
        return jnp.stack([first, second]).astype(F32)

    def hi_lo(v):
        hi = v.astype(BF)
        return hi, (v - hi.astype(F32)).astype(BF)

    def gather(halves):
        send, keep = split(*halves)
        gy = over_tensor(send, 2)
        gx = over_dp(gy, 1)
        two = split(gy, gx)
        three = tuple(over_tensor(v, 1) for v in two)
        one = tuple(over_tensor(v, 1) for v in halves)
        return [halves, one, two, three]

    e = qkv.shape[-1]

    def attn_weights(i):
        hi, lo = hi_lo(qvb[i].reshape(1, -1))
        rows = jnp.concatenate([hi, lo], axis=1)
        rows = jnp.concatenate([rows, jnp.zeros((7, width), BF)])
        a = jnp.concatenate([qkv[i, 0].T, qkv[i, 1].T, rows])
        b = jnp.concatenate([qkv[i, 2].T, wout[i], jnp.zeros((8, width), BF)])
        got = gather((a, b))
        wq = jnp.concatenate([g[0][:e] for g in got])
        wk = jnp.concatenate([g[0][e : 2 * e] for g in got])
        wv = jnp.concatenate([g[1][:e] for g in got])
        wo = jnp.concatenate([g[1][e : 2 * e] for g in got])
        bias = [g[0][2 * e].astype(F32) for g in got]
        bias = [v[: 2 * e] + v[2 * e :] for v in bias]
        bq = jnp.concatenate([v[:e] for v in bias])
        bv = jnp.concatenate([v[e:] for v in bias])
        return wq, wk, wv, wo, bq, bv

    def mlp_weights():
        h = win.shape[1] // 2
        wt = win.T
        out = []
        for k in range(2):
            hi, lo = hi_lo(b_in[k * h : (k + 1) * h].reshape(1, -1))
            rows = jnp.concatenate([jnp.concatenate([hi, lo], axis=1), jnp.zeros((7, width), BF)])
            out.append(
                jnp.concatenate([wt[k * h : (k + 1) * h], wdown[k * h : (k + 1) * h], rows])
            )
        got = gather(tuple(out))
        res = []
        for g in got:
            bias = [v[2 * h].astype(F32) for v in g]
            bias = jnp.concatenate([v[:h] + v[h:] for v in bias])
            res.append(
                (
                    jnp.concatenate([v[:h] for v in g]),
                    jnp.concatenate([v[h : 2 * h] for v in g]),
                    bias,
                )
            )
        return res

    def to_places(v):
        own = lax.dynamic_slice_in_dim(v, STEP * core, HALF, 1)
        send = lax.dynamic_slice_in_dim(v, STEP * (1 - core), HALF, 1)
        both = jnp.concatenate([own, over_tensor(send, 1)])
        f = both.shape[0]
        both = both.reshape(f, HALF // 8, 8, width).transpose(1, 0, 2, 3)
        return both.reshape(HALF // 8, f * 8, width)

    def to_frames(v, flip=False):
        f = v.shape[1] // 8
        v = v.reshape(HALF // 8, f, 8, width).transpose(1, 0, 2, 3).reshape(f, HALF, width)
        own = v[: f // 2]
        got = over_tensor(v[f // 2 :], 1)
        if flip:
            got = jnp.concatenate([got[..., i * e : (i + 1) * e] for i in (1, 0, 3, 2)], axis=-1)
        cut = 2 * HALF - ROWS
        a = jnp.concatenate([own, got[:, cut:]], axis=1)
        b = jnp.concatenate([got, own[:, cut:]], axis=1)
        return jnp.where(core == 0, a, b)

    stream0 = whole_clip(clips).astype(F32)
    w0 = attn_weights(0)
    w1 = attn_weights(1)
    wm = mlp_weights()
    grad3b = whole_clip(cot)
    row = lax.broadcasted_iota(jnp.int32, (ROWS, ROWS), 1)
    mask0 = row < places
    frames = 2 * stream0.shape[0]
    r0 = lax.broadcasted_iota(jnp.int32, (frames * 8, frames * 8), 0) % 8
    r1 = lax.broadcasted_iota(jnp.int32, (frames * 8, frames * 8), 1) % 8
    mask1 = r0 == r1

    n0 = (norm_stats(stream0)[0] * gain[0] + shift[0]).astype(BF)
    kept0 = attention(n0, w0, mask0)
    stream1 = stream0 + (dot("gre,ed->grd", kept0[3], w0[3]) + bout[0])
    n1 = (norm_stats(stream1)[0] * gain[1] + shift[1]).astype(BF)
    n1p = to_places(n1)
    kept1 = attention(n1p, w1, mask1)
    o1 = to_frames(kept1[3], True)
    stream2 = stream1 + (dot("gre,ed->grd", o1, w1[3]) + bout[1])
    n2 = (norm_stats(stream2)[0] * gain[2] + shift[2]).astype(BF)

    branch = 0.0
    dn2 = 0.0
    gmlp = [None] * 4
    grad3 = grad3b.astype(F32)
    for r in (3, 1, 2, 0):
        wt, wd, b = wm[r]
        raised = dot("grd,hd->grh", n2, wt) + b
        hidden, pull = jax.vjp(lambda u: jax.nn.gelu(u, approximate=False), raised)
        hidden = hidden.astype(BF)
        branch = branch + dot("grh,hd->grd", hidden, wd)
        dh = dot("grd,hd->grh", grad3b, wd)
        dr = pull(dh)[0].astype(BF)
        gmlp[r] = (
            dot("grh,grd->hd", dr, n2),
            dot("grh,grd->hd", hidden, grad3b),
            jnp.sum(dr, axis=(0, 1), dtype=F32),
        )
        dn2 = dn2 + dot("grh,hd->grd", dr, wt)
    output = back((stream2 + (branch + bdown)).astype(BF))
    gbdown = jnp.sum(grad3, axis=(0, 1))
    dv, gg2, gs2 = norm_back(stream2, gain[2], dn2)
    grad2 = grad3 + dv
    gbo1 = jnp.sum(grad2, axis=(0, 1))
    g2p = to_places(grad2.astype(BF))
    place = STEP * core + 8 * lax.broadcasted_iota(jnp.int32, (HALF // 8, 1, 1), 0)
    g2p = jnp.where((core == 1) & (place < HALF), jnp.zeros_like(g2p), g2p)
    dn1p, gw1, gb1 = attention_back(n1p, kept1, w1, mask1, g2p)
    dv, gg1, gs1 = norm_back(stream1, gain[1], to_frames(dn1p).astype(F32))
    grad1 = grad2 + dv
    gbo0 = jnp.sum(grad1, axis=(0, 1))
    dn0, gw0, gb0 = attention_back(n0, kept0, w0, mask0, grad1.astype(BF))
    dv, gg0, gs0 = norm_back(stream0, gain[0], dn0.astype(F32))
    input_grad = back((grad1 + dv).astype(BF))

    def row_of(v):
        return jnp.zeros((8, width), F32).at[0, : v.shape[0]].set(v)

    def attn_pieces(gw, gb):
        out = []
        for r in range(4):
            s = slice(r * e, (r + 1) * e)
            a = jnp.concatenate([gw[0][s], gw[1][s], row_of(gb[0][s])])
            b = jnp.concatenate([gw[2][s], gw[3][s], row_of(gb[1][s])])
            out.append(split(a.astype(BF), b.astype(BF)))
        return out

    def mlp_pieces():
        h = win.shape[1] // 2
        out = []
        for r in range(4):
            ga, gd, gb = gmlp[r]
            pair = []
            for k in range(2):
                s = slice(k * h, (k + 1) * h)
                pair.append(jnp.concatenate([ga[s], gd[s], row_of(gb[s])]).astype(BF))
            out.append(split(*pair))
        return out

    small = jnp.stack([gg0, gg1, gg2, gs0, gs1, gs2, gbo0, gbo1, gbdown]).astype(BF)
    small = jnp.pad(small, ((0, 7), (0, 0)))

    def reduce_piece(p, extra):
        def both(a, b, swap):
            got = swap(a)
            return b + got

        c1 = over_tensor(jnp.stack([p[1][0], p[3][0]]), 1)
        c2 = over_tensor(jnp.stack([p[1][1], p[3][1]]), 1)
        keep = [p[0][0] + c1[0], p[2][0] + c1[1]]
        send = [p[0][1] + c2[0], p[2][1] + c2[1]]
        got = over_dp(jnp.stack(send), 1)
        keep = [keep[0] + got[0], keep[1] + got[1]]
        total = keep[0] + over_tensor(keep[1], 2)
        if extra is not None:
            extra = extra + over_tensor(extra, 1)
            extra = extra + over_dp(extra, 1)
            extra = extra + over_tensor(extra, 2)
            rows = extra.shape[0]
            total = jnp.concatenate([total, extra])
        bit = 2
        while bit < dp:
            total = total + over_dp(total, bit)
            bit *= 2
        if extra is not None:
            total, extra = total[:-rows], total[-rows:]
        return split(total, over_dp(total, 1)), extra

    (ma, mb), _ = reduce_piece(mlp_pieces(), None)
    (a1, b1), _ = reduce_piece(attn_pieces(gw1, gb1), None)
    (a0, b0), small = reduce_piece(attn_pieces(gw0, gb0), small)
    small = small.astype(F32)

    gqkv = jnp.stack(
        [jnp.stack([a[:e].T, a[e : 2 * e].T, b[:e].T]) for a, b in ((a0, b0), (a1, b1))]
    ).astype(F32)
    gout = jnp.stack([b0[e : 2 * e], b1[e : 2 * e]]).astype(F32)
    gqv = jnp.stack(
        [jnp.stack([a[2 * e, :e], b[2 * e, :e]]) for a, b in ((a0, b0), (a1, b1))]
    ).astype(F32)
    h = win.shape[1] // 2
    gwin = jnp.concatenate([ma[:h], mb[:h]]).T.astype(F32)
    gwd = jnp.concatenate([ma[h : 2 * h], mb[h : 2 * h]]).astype(F32)
    gbin = jnp.concatenate([ma[2 * h, :h], mb[2 * h, :h]]).astype(F32)
    return (
        output,
        input_grad,
        small[0:3],
        small[3:6],
        gqkv,
        gqv,
        gout,
        small[6:8],
        gwin,
        gbin,
        gwd,
        small[8],
    )


def solution(mesh):
    placed = (
        P("dp", "tensor", None, None),
        P("dp", "tensor", None, None),
        P(),
        P(),
        P(None, None, None, "tensor"),
        P(None, None, "tensor"),
        P(None, "tensor", None),
        P(),
        P(None, "tensor"),
        P("tensor"),
        P("tensor", None),
        P(),
    )
    return jax.shard_map(
        shards,
        mesh=mesh,
        in_specs=placed,
        out_specs=(
            P("dp", "tensor", None, None),
            P("dp", "tensor", None, None),
            P(),
            P(),
            P(None, None, None, "tensor"),
            P(None, None, "tensor"),
            P(None, "tensor", None),
            P(),
            P(None, "tensor"),
            P("tensor"),
            P("tensor", None),
            P(),
        ),
        check_vma=False,
    )
```

time: 2050 us -> 968 us (0.47)
  waiting for transfers between devices: 1290 us -> 263 us
  blocking collectives: 65.6 us -> 0 us
  matrix products: 346 us -> 307 us
  starting transfers between devices: 3.01 us -> 40.4 us
  other arithmetic: 157 us -> 181 us
    reduce_scatter x12 -> x0, waiting for transfers between devices: 664 us -> none  [the longest x6 491 us: branch_sum(): lax.psum_scatter(jnp.einsum('fpe,ed->fpd', values, weight, preferred_elem...]
    all_gather x12 -> x0, waiting for transfers between devices: 383 us -> none  [the longest x6 225 us: whole_inputs(): return lax.all_gather(shard, 'tensor', axis=0, tiled=True)]
    ppermute x0 -> x50, waiting for transfers between devices: none -> 263 us  [the longest x16 144 us: over_dp(): return lax.ppermute(v, 'dp', [(i, i ^ bit) for i in range(dp)])]
    psum x1 -> x0, waiting for transfers between devices: 240 us -> none  [reduce_all(): lax.psum((grads_in[2], grads_in[3], grads_in[4], grads_in[6], grads_in[7]...]
    psum x2 -> x0, blocking collectives: 65.6 us -> none  [the longest x1 43.4 us: reduce_all(): lax.psum((grads_in[0], grads_in[1], grads_in[5], grads_in[9]), ('dp', 'te...]
    while x388 -> x0, local copies, waits for them, and re-layouts: 48.1 us -> none
    slice x16 -> x75, local copies, waits for them, and re-layouts: 14.6 us -> 58.5 us  [the longest x6 11.5 us: attn_weights(): wo = jnp.concatenate([g[1][e:2 * e] for g in got])]
    ppermute x0 -> x50, starting transfers between devices: none -> 40.4 us  [the longest x16 20.2 us: over_dp(): return lax.ppermute(v, 'dp', [(i, i ^ bit) for i in range(dp)])]
  transfers between devices with their start and end apart: 25 -> 50, of which waited for: 24 -> 14; matrix products, arithmetic and copies ran while one was open for 9% -> 51% of each run, Pallas kernels for 0% -> 0%
where the time goes in v1:
time: 968 us; the launch traced here: 962 us
  matrix products  307 us (32%)
  waiting for transfers between devices  263 us (27%)
  other arithmetic  181 us (19%)
  local copies, waits for them, and re-layouts  166 us (17%)
  starting transfers between devices  40.4 us (4%)
    dot_general x60, matrix products, dot(): return jnp.einsum(spec, a, b, preferred_element_type=F32)  307 us
    ppermute x16, waiting for transfers between devices, over_dp(): return lax.ppermute(v, 'dp', [(i, i ^ bit) for i in range(dp)])  144 us
    ppermute x34, waiting for transfers between devices, over_tensor(): return lax.ppermute(v, 'tensor', [(i, i ^ bit) for i in range(4)])  119 us
    convert_element_type x4, other arithmetic, shards(): hidden = hidden.astype(BF)  46.3 us
    unnamed x506, local copies, waits for them, and re-layouts  34.8 us
    convert_element_type x2, other arithmetic, attention_back(): ds = (p * (dp - jnp.sum(p * dp, axis=-1, keepdims=True))).astype(BF)  21 us
    ppermute x16, starting transfers between devices, over_dp(): return lax.ppermute(v, 'dp', [(i, i ^ bit) for i in range(dp)])  20.2 us
    ppermute x34, starting transfers between devices, over_tensor(): return lax.ppermute(v, 'tensor', [(i, i ^ bit) for i in range(4)])  20.2 us
  transfers between devices with their start and end apart: 50, of which 14 were waited for; matrix products, arithmetic and copies ran while one was open for 51% of the time, Pallas kernels for 0%

profile of v1, /device:TPU:0, one launch (start us, length us, event | category | flops | bytes accessed | tf_op | source)
XLA Modules:
  0.0 962.4 jit_solution(5697742869693299777)
XLA Ops:
  10.1 5.0 constant_dynamic-slice_fusion.3
  42.6 33.1 %collective-permute-done.9 = bf16[392,768]{1,0:T(8,128)(2,1)S(1)} collective-permute-done((bf16[392,768]{1,0:T(8,128)(2,1)S(1)}, bf16[392,768]{1,0:T(8,128)(2,1)S(1)}, u32[]{:S(2)}, u32[]{:S(2)}) %collective-permute-start.9) | collective-permute-done | bytes 602144 | tf_op jit(solution)/shard_map/ppermute | solution.py:85
  82.2 10.2 %collective-permute-done.3 = bf16[392,768]{1,0:T(8,128)(2,1)S(1)} collective-permute-done((bf16[392,768]{1,0:T(8,128)(2,1)}, bf16[392,768]{1,0:T(8,128)(2,1)S(1)}, u32[]{:S(2)}, u32[]{:S(2)}) %collective-permute-start.3) | collective-permute-done | bytes 602144 | tf_op jit(solution)/shard_map/ppermute | solution.py:88
  94.5 10.8 %collective-permute-done.10 = bf16[392,768]{1,0:T(8,128)(2,1)S(1)} collective-permute-done((bf16[392,768]{1,0:T(8,128)(2,1)S(1)}, bf16[392,768]{1,0:T(8,128)(2,1)S(1)}, u32[]{:S(2)}, u32[]{:S(2)}) %collective-permute-start.10) | collective-permute-done | bytes 602144 | tf_op jit(solution)/shard_map/ppermute | solution.py:88
  114.9 12.6 %collective-permute-done.22 = bf16[4,200,768]{2,1,0:T(8,128)(2,1)} collective-permute-done((bf16[4,200,768]{2,1,0:T(8,128)(2,1)S(1)}, bf16[4,200,768]{2,1,0:T(8,128)(2,1)}, u32[]{:S(2)}, u32[]{:S(2)}) %collective-permute-start.22) | collective-permute-done | bytes 1228832 | tf_op jit(solution)/shard_map/ppermute | solution.py:85
  142.0 6.3 add_convert_fusion.11
  148.3 4.6 copy.117
  155.6 6.1 add_convert_fusion.12
  166.1 14.1 %select_reduce_fusion = (f32[8,12,200]{2,1,0:T(8,128)}, f32[8,12,200,200]{2,3,1,0:T(8,128)}) fusion(pred[200]{0:T(512)(128)(4,1)S(1)} %iota_compare_fusion.2, bf16[8,200,12,64]{1,3,2,0:T(8,128)(2,1)} %bitcast.593, bf16[8,200,12,64]{1,3,2,0:T(8,128)(2,1)S(1)} %bitcast.591), kind=kOutput, calls=%fused_computation.5 | convolution fusion | flops 503020800 | bytes 20352200 | tf_op jit(solution)/shard_map/gqhe,gkhe->ghqk/dot_general | solution.py:16
  180.2 12.3 %fusion = f32[8,12,200]{2,1,0:T(8,128)} fusion(f32[8,12,200,200]{2,3,1,0:T(8,128)} %get-tuple-element.624, f32[8,12,200]{2,1,0:T(8,128)} %get-tuple-element.623, pred[200]{0:T(512)(128)(4,1)S(1)} %iota_compare_fusion.2), kind=kLoop, calls=%fused_computation.6 | loop fusion | flops 15340800 | bytes 15513800 | tf_op jit(solution)/shard_map/reduce_sum | solution.py:49
  192.6 9.8 %fusion.118 = bf16[8,12,64,200]{3,2,1,0:T(8,128)(2,1)S(1)} fusion(bf16[8,200,12,64]{1,3,2,0:T(8,128)(2,1)S(1)} %bitcast.612, f32[8,12,200,200]{2,3,1,0:T(8,128)} %get-tuple-element.624, f32[8,12,200]{2,1,0:T(8,128)} %fusion, f32[8,12,200]{2,1,0:T(8,128)} %get-tuple-element.623, pred[200]{0:T(512)(128)(4,1)S(1)} %iota_compare_fusion.2), kind=kOutput, calls=%fused_computation.236 | convolution fusion | flops 511948800 | bytes 20429000 | tf_op jit(solution)/shard_map/ghqk,gkhe->gqhe/dot_general | solution.py:16
  231.8 5.4 add_convert_fusion.1
  241.2 6.3 add_convert_fusion.2
  265.0 7.0 copy.126
  272.0 8.3 reshape_reshape.3
  296.9 11.4 %multiply_convert_fusion.8 = (bf16[8,200,768]{2,1,0:T(8,128)(2,1)S(1)}, f32[8,200,768]{2,1,0:T(8,128)S(1)}) fusion(f32[8,200,768]{2,1,0:T(8,128)S(1)} %get-tuple-element.634, f32[768]{0:T(1024)S(1)} %copy-done.199, u8[200,768]{1,0:T(8,128)(4,1)S(1)} %get-tuple-element.346, u8[200,768]{1,0:T(8,128)(4,1)S(1)} %get-tuple-element.345), kind=kLoop, calls=%fused_computation.140 | loop fusion | flops 87244800 | bytes 12598272 | tf_op jit(solution)/shard_map/convert_element_type | solution.py:216
  308.4 5.2 fusion.336
  318.4 6.1 fusion.182
  328.1 12.4 %multiply_convert_fusion.7 = (bf16[8,200,768]{2,1,0:T(8,128)(2,1)}, f32[8,200,768]{2,1,0:T(8,128)S(1)}) fusion(f32[8,200,768]{2,1,0:T(8,128)S(1)} %get-tuple-element.640, f32[768]{0:T(1024)S(1)} %pad_maximum_fusion.33, u8[200,768]{1,0:T(8,128)(4,1)S(1)} %get-tuple-element.348, u8[200,768]{1,0:T(8,128)(4,1)S(1)} %get-tuple-element.347), kind=kLoop, calls=%fused_computation.127 | loop fusion | flops 87244800 | bytes 12598272 | tf_op jit(solution)/shard_map/convert_element_type | solution.py:216
  340.5 6.6 convert_reduce_fusion.5
  347.0 5.3 convolution_bitcast_fusion.5
  360.1 11.4 %multiply_convert_fusion.6 = (bf16[8,200,768]{2,1,0:T(8,128)(2,1)S(1)}, f32[8,200,768]{2,1,0:T(8,128)S(1)}) fusion(f32[8,200,768]{2,1,0:T(8,128)S(1)} %get-tuple-element.631, f32[768]{0:T(1024)S(1)} %copy-done.198, u8[200,768]{1,0:T(8,128)(4,1)S(1)} %get-tuple-element.350, u8[200,768]{1,0:T(8,128)(4,1)S(1)} %get-tuple-element.349), kind=kLoop, calls=%fused_computation.114 | loop fusion | flops 87244800 | bytes 12598272 | tf_op jit(solution)/shard_map/convert_element_type | solution.py:216
  371.5 6.6 convert_reduce_fusion.6
  378.1 5.3 convolution_bitcast_fusion.7
  401.2 11.2 %multiply_convert_fusion.9 = (bf16[8,200,768]{2,1,0:T(8,128)(2,1)S(1)}, f32[8,200,768]{2,1,0:T(8,128)S(1)}) fusion(f32[8,200,768]{2,1,0:T(8,128)S(1)} %get-tuple-element.637, f32[768]{0:T(1024)S(1)} %pad_maximum_fusion.31, u8[200,768]{1,0:T(8,128)(4,1)S(1)} %get-tuple-element.344, u8[200,768]{1,0:T(8,128)(4,1)S(1)} %get-tuple-element.343), kind=kLoop, calls=%fused_computation.153 | loop fusion | flops 87244800 | bytes 12598272 | tf_op jit(solution)/shard_map/convert_element_type | solution.py:216
  412.4 5.2 fusion.337
  433.4 7.5 multiply_reduce_fusion.2
  458.3 7.0 add_convert_fusion.8
  480.6 5.2 fusion.122
  489.4 9.2 convert_reduce_fusion.3
  498.6 8.3 multiply_reduce_fusion.1
  506.9 6.7 multiply_convert_fusion.1
  579.9 4.6 copy.144
  584.6 15.9 %multiply_reduce_fusion = (f32[8,12,200]{2,1,0:T(8,128)}, f32[8,12,200,200]{2,3,1,0:T(8,128)}) fusion(f32[8,12,200,200]{2,3,1,0:T(8,128)} %get-tuple-element.624, f32[8,12,200]{2,1,0:T(8,128)} %log_add_fusion, pred[200]{0:T(512)(128)(4,1)S(1)} %copy-done.209, bf16[8,200,12,64]{1,3,2,0:T(8,128)(2,1)} %bitcast.614, bf16[8,200,12,64]{1,3,2,0:T(8,128)(2,1)S(1)} %bitcast.613), kind=kOutput, calls=%fused_computation.1 | convolution fusion | flops 510700800 | bytes 35789000 | tf_op jit(solution)/shard_map/gqhe,gkhe->ghqk/dot_general | solution.py:16
  600.4 14.3 %multiply_convert_fusion = bf16[8,12,200,200]{2,3,1,0:T(8,128)(2,1)S(1)} fusion(f32[8,12,200,200]{2,3,1,0:T(8,128)} %get-tuple-element.647, f32[8,12,200,200]{2,3,1,0:T(8,128)} %get-tuple-element.624, f32[8,12,200]{2,1,0:T(8,128)} %get-tuple-element.646, f32[8,12,200]{2,1,0:T(8,128)} %log_add_fusion, pred[200]{0:T(512)(128)(4,1)S(1)} %copy-done.209), kind=kLoop, calls=%fused_computation | loop fusion | flops 23040000 | bytes 38553800 | tf_op jit(solution)/shard_map/convert_element_type | solution.py:64
  622.4 8.8 multiply_convert_fusion.2
  631.2 6.9 convolution_bitcast_fusion
  638.1 10.6 %convert_reduce_fusion.1 = (bf16[12,64]{1,0:T(8,128)(2,1)S(1)}, bf16[8,12,64,200]{3,2,1,0:T(8,128)(2,1)}) fusion(bf16[8,200,12,64]{1,3,2,0:T(8,128)(2,1)S(1)} %bitcast.615, f32[8,12,200,200]{2,3,1,0:T(8,128)} %get-tuple-element.624, f32[8,12,200]{2,1,0:T(8,128)} %log_add_fusion, pred[200]{0:T(512)(128)(4,1)S(1)} %copy-done.209), kind=kOutput, calls=%fused_computation.28 | convolution fusion | flops 510565632 | bytes 20353736 | tf_op jit(solution)/shard_map/ghqk,gqhe->gkhe/dot_general | solution.py:16
  648.7 6.7 fusion.198
  679.7 8.6 fusion.42
  703.8 32.6 %collective-permute-done.39 = bf16[392,768]{1,0:T(8,128)(2,1)} collective-permute-done((bf16[392,768]{1,0:T(8,128)(2,1)}, bf16[392,768]{1,0:T(8,128)(2,1)}, u32[]{:S(2)}, u32[]{:S(2)}) %collective-permute-start.39) | collective-permute-done | bytes 602144 | tf_op jit(solution)/shard_map/ppermute | solution.py:85
  758.3 6.1 collective-permute-done.28
  779.1 40.9 %collective-permute-done.32 = bf16[16,768]{1,0:T(8,128)(2,1)S(1)} collective-permute-done((bf16[16,768]{1,0:T(8,128)(2,1)S(1)}, bf16[16,768]{1,0:T(8,128)(2,1)S(1)}, u32[]{:S(2)}, u32[]{:S(2)}) %collective-permute-start.32) | collective-permute-done | bytes 24608 | tf_op jit(solution)/shard_map/ppermute | solution.py:85
  833.0 14.5 %collective-permute-done.33 = bf16[408,768]{1,0:T(8,128)(2,1)S(1)} collective-permute-done((bf16[408,768]{1,0:T(8,128)(2,1)S(1)}, bf16[408,768]{1,0:T(8,128)(2,1)S(1)}, u32[]{:S(2)}, u32[]{:S(2)}) %collective-permute-start.33) | collective-permute-done | bytes 626720 | tf_op jit(solution)/shard_map/ppermute | solution.py:88
  849.4 26.3 %collective-permute-done.47 = bf16[776,768]{1,0:T(8,128)(2,1)S(1)} collective-permute-done((bf16[776,768]{1,0:T(8,128)(2,1)S(1)}, bf16[776,768]{1,0:T(8,128)(2,1)S(1)}, u32[]{:S(2)}, u32[]{:S(2)}) %collective-permute-start.47) | collective-permute-done | bytes 1191968 | tf_op jit(solution)/shard_map/ppermute | solution.py:88
  880.6 8.9 collective-permute-done.35
  889.7 39.1 %collective-permute-done.48 = bf16[776,768]{1,0:T(8,128)(2,1)S(1)} collective-permute-done((bf16[776,768]{1,0:T(8,128)(2,1)S(1)}, bf16[776,768]{1,0:T(8,128)(2,1)S(1)}, u32[]{:S(2)}, u32[]{:S(2)}) %collective-permute-start.48) | collective-permute-done | bytes 1191968 | tf_op jit(solution)/shard_map/ppermute | solution.py:88
  933.6 23.8 %collective-permute-done.49 = bf16[776,768]{1,0:T(8,128)(2,1)S(1)} collective-permute-done((bf16[776,768]{1,0:T(8,128)(2,1)S(1)}, bf16[776,768]{1,0:T(8,128)(2,1)S(1)}, u32[]{:S(2)}, u32[]{:S(2)}) %collective-permute-start.49) | collective-permute-done | bytes 1191968 | tf_op jit(solution)/shard_map/ppermute | solution.py:88
  (939 shorter events, 406.7 us)
Async XLA Ops:
  4.3 36.3 %collective-permute-start.2 = (bf16[392,768]{1,0:T(8,128)(2,1)}, bf16[392,768]{1,0:T(8,128)(2,1)}, u32[]{:S(2)}, u32[]{:S(2)}) collective-permute-start(bf16[392,768]{1,0:T(8,128)(2,1)} %get-tuple-element.512), channel_id=1, source_target_pairs={{0,2},{1,3},{2,0},{3,1},{4,6},{5,7},{6,4},{7,5},{8,10},{9,11},{10,... | collective-permute-start | bytes 1806344 | tf_op jit(solution)/shard_map/ppermute | solution.py:85
  7.2 21.1 %collective-permute-start.5 = (bf16[392,768]{1,0:T(8,128)(2,1)}, bf16[392,768]{1,0:T(8,128)(2,1)}, u32[]{:S(2)}, u32[]{:S(2)}) collective-permute-start(bf16[392,768]{1,0:T(8,128)(2,1)} %get-tuple-element.511), channel_id=1, source_target_pairs={{0,1},{1,0},{2,3},{3,2},{4,5},{5,4},{6,7},{7,6},{8,9},{9,8},{10,11... | collective-permute-start | bytes 1806344 | tf_op jit(solution)/shard_map/ppermute | solution.py:85
  7.2 24.0 %collective-permute-start.1 = (bf16[392,768]{1,0:T(8,128)(2,1)}, bf16[392,768]{1,0:T(8,128)(2,1)}, u32[]{:S(2)}, u32[]{:S(2)}) collective-permute-start(bf16[392,768]{1,0:T(8,128)(2,1)} %get-tuple-element.545), channel_id=1, source_target_pairs={{0,1},{1,0},{2,3},{3,2},{4,5},{5,4},{6,7},{7,6},{8,9},{9,8},{10,11... | collective-permute-start | bytes 1806344 | tf_op jit(solution)/shard_map/ppermute | solution.py:85
  9.4 24.3 %collective-permute-start.12 = (bf16[392,768]{1,0:T(8,128)(2,1)}, bf16[392,768]{1,0:T(8,128)(2,1)}, u32[]{:S(2)}, u32[]{:S(2)}) collective-permute-start(bf16[392,768]{1,0:T(8,128)(2,1)} %get-tuple-element.509), channel_id=1, source_target_pairs={{0,1},{1,0},{2,3},{3,2},{4,5},{5,4},{6,7},{7,6},{8,9},{9,8},{10,11... | collective-permute-start | bytes 1806344 | tf_op jit(solution)/shard_map/ppermute | solution.py:85
  9.5 26.9 %collective-permute-start.8 = (bf16[392,768]{1,0:T(8,128)(2,1)}, bf16[392,768]{1,0:T(8,128)(2,1)}, u32[]{:S(2)}, u32[]{:S(2)}) collective-permute-start(bf16[392,768]{1,0:T(8,128)(2,1)} %get-tuple-element.546), channel_id=1, source_target_pairs={{0,1},{1,0},{2,3},{3,2},{4,5},{5,4},{6,7},{7,6},{8,9},{9,8},{10,11... | collective-permute-start | bytes 1806344 | tf_op jit(solution)/shard_map/ppermute | solution.py:85
  28.3 12.2 %collective-permute-start.20 = (bf16[776,768]{1,0:T(8,128)(2,1)S(1)}, bf16[776,768]{1,0:T(8,128)(2,1)S(1)}, u32[]{:S(2)}, u32[]{:S(2)}) collective-permute-start(bf16[776,768]{1,0:T(8,128)(2,1)S(1)} %get-tuple-element.440), channel_id=1, source_target_pairs={{0,1},{1,0},{2,3},{3,2},{4,5},{5,4},{6,7},{7,6},{8,9},{9,8},{10,11... | collective-permute-start | bytes 3575816 | tf_op jit(solution)/shard_map/ppermute | solution.py:85
  31.2 45.9 %collective-permute-start.19 = (bf16[776,768]{1,0:T(8,128)(2,1)S(1)}, bf16[776,768]{1,0:T(8,128)(2,1)S(1)}, u32[]{:S(2)}, u32[]{:S(2)}) collective-permute-start(bf16[776,768]{1,0:T(8,128)(2,1)S(1)} %get-tuple-element.438), channel_id=1, source_target_pairs={{0,1},{1,0},{2,3},{3,2},{4,5},{5,4},{6,7},{7,6},{8,9},{9,8},{10,11... | collective-permute-start | bytes 3575816 | tf_op jit(solution)/shard_map/ppermute | solution.py:85
  33.7 44.1 %collective-permute-start.15 = (bf16[776,768]{1,0:T(8,128)(2,1)S(1)}, bf16[776,768]{1,0:T(8,128)(2,1)}, u32[]{:S(2)}, u32[]{:S(2)}) collective-permute-start(bf16[776,768]{1,0:T(8,128)(2,1)S(1)} %get-tuple-element.439), channel_id=1, source_target_pairs={{0,2},{1,3},{2,0},{3,1},{4,6},{5,7},{6,4},{7,5},{8,10},{9,11},{10,... | collective-permute-start | bytes 3575816 | tf_op jit(solution)/shard_map/ppermute | solution.py:85
  36.4 39.3 %collective-permute-start.9 = (bf16[392,768]{1,0:T(8,128)(2,1)S(1)}, bf16[392,768]{1,0:T(8,128)(2,1)S(1)}, u32[]{:S(2)}, u32[]{:S(2)}) collective-permute-start(bf16[392,768]{1,0:T(8,128)(2,1)S(1)} %copy-done.134), channel_id=1, source_target_pairs={{0,2},{1,3},{2,0},{3,1},{4,6},{5,7},{6,4},{7,5},{8,10},{9,11},{10,... | collective-permute-start | bytes 1806344 | tf_op jit(solution)/shard_map/ppermute | solution.py:85
  40.4 73.5 %collective-permute-start = (bf16[4,200,768]{2,1,0:T(8,128)(2,1)S(1)}, bf16[4,200,768]{2,1,0:T(8,128)(2,1)S(1)}, u32[]{:S(2)}, u32[]{:S(2)}) collective-permute-start(bf16[4,200,768]{2,1,0:T(8,128)(2,1)S(1)} %copy-done.90), channel_id=1, source_target_pairs={{0,2},{1,3},{2,0},{3,1},{4,6},{5,7},{6,4},{7,5},{8,10},{9,11},{10,... | collective-permute-start | bytes 3686408 | tf_op jit(solution)/shard_map/ppermute | solution.py:85
  40.6 86.9 %collective-permute-start.22 = (bf16[4,200,768]{2,1,0:T(8,128)(2,1)S(1)}, bf16[4,200,768]{2,1,0:T(8,128)(2,1)}, u32[]{:S(2)}, u32[]{:S(2)}) collective-permute-start(bf16[4,200,768]{2,1,0:T(8,128)(2,1)S(1)} %copy-done.91), channel_id=1, source_target_pairs={{0,2},{1,3},{2,0},{3,1},{4,6},{5,7},{6,4},{7,5},{8,10},{9,11},{10,... | collective-permute-start | bytes 3686408 | tf_op jit(solution)/shard_map/ppermute | solution.py:85
  75.7 16.7 %collective-permute-start.3 = (bf16[392,768]{1,0:T(8,128)(2,1)}, bf16[392,768]{1,0:T(8,128)(2,1)S(1)}, u32[]{:S(2)}, u32[]{:S(2)}) collective-permute-start(bf16[392,768]{1,0:T(8,128)(2,1)} %collective-permute-done.2), channel_id=1, source_target_pairs={{0,4},{4,0},{8,12},{12,8},{16,20},{20,16},{24,28},{28,24},{1,5},{5... | collective-permute-start | bytes 1806344 | tf_op jit(solution)/shard_map/ppermute | solution.py:88
  77.2 28.1 %collective-permute-start.10 = (bf16[392,768]{1,0:T(8,128)(2,1)S(1)}, bf16[392,768]{1,0:T(8,128)(2,1)S(1)}, u32[]{:S(2)}, u32[]{:S(2)}) collective-permute-start(bf16[392,768]{1,0:T(8,128)(2,1)S(1)} %collective-permute-done.9), channel_id=1, source_target_pairs={{0,4},{4,0},{8,12},{12,8},{16,20},{20,16},{24,28},{28,24},{1,5},{5... | collective-permute-start | bytes 1806344 | tf_op jit(solution)/shard_map/ppermute | solution.py:88
  77.7 136.7 %collective-permute-start.16 = (bf16[776,768]{1,0:T(8,128)(2,1)}, bf16[776,768]{1,0:T(8,128)(2,1)}, u32[]{:S(2)}, u32[]{:S(2)}) collective-permute-start(bf16[776,768]{1,0:T(8,128)(2,1)} %collective-permute-done.15), channel_id=1, source_target_pairs={{0,4},{4,0},{8,12},{12,8},{16,20},{20,16},{24,28},{28,24},{1,5},{5... | collective-permute-start | bytes 3575816 | tf_op jit(solution)/shard_map/ppermute | solution.py:88
  94.4 36.9 %collective-permute-start.6 = (bf16[392,768]{1,0:T(8,128)(2,1)S(1)}, bf16[392,768]{1,0:T(8,128)(2,1)}, u32[]{:S(2)}, u32[]{:S(2)}) collective-permute-start(bf16[392,768]{1,0:T(8,128)(2,1)S(1)} %get-tuple-element.437), channel_id=1, source_target_pairs={{0,1},{1,0},{2,3},{3,2},{4,5},{5,4},{6,7},{7,6},{8,9},{9,8},{10,11... | collective-permute-start | bytes 1806344 | tf_op jit(solution)/shard_map/ppermute | solution.py:85
  105.3 47.7 %collective-permute-start.4 = (bf16[392,768]{1,0:T(8,128)(2,1)}, bf16[392,768]{1,0:T(8,128)(2,1)}, u32[]{:S(2)}, u32[]{:S(2)}) collective-permute-start(bf16[392,768]{1,0:T(8,128)(2,1)} %get-tuple-element.436), channel_id=1, source_target_pairs={{0,1},{1,0},{2,3},{3,2},{4,5},{5,4},{6,7},{7,6},{8,9},{9,8},{10,11... | collective-permute-start | bytes 1806344 | tf_op jit(solution)/shard_map/ppermute | solution.py:85
  113.9 95.0 %collective-permute-start.13 = (bf16[392,768]{1,0:T(8,128)(2,1)}, bf16[392,768]{1,0:T(8,128)(2,1)}, u32[]{:S(2)}, u32[]{:S(2)}) collective-permute-start(bf16[392,768]{1,0:T(8,128)(2,1)} %get-tuple-element.435), channel_id=1, source_target_pairs={{0,1},{1,0},{2,3},{3,2},{4,5},{5,4},{6,7},{7,6},{8,9},{9,8},{10,11... | collective-permute-start | bytes 1806344 | tf_op jit(solution)/shard_map/ppermute | solution.py:85
  127.5 84.9 %collective-permute-start.11 = (bf16[392,768]{1,0:T(8,128)(2,1)}, bf16[392,768]{1,0:T(8,128)(2,1)}, u32[]{:S(2)}, u32[]{:S(2)}) collective-permute-start(bf16[392,768]{1,0:T(8,128)(2,1)} %get-tuple-element.434), channel_id=1, source_target_pairs={{0,1},{1,0},{2,3},{3,2},{4,5},{5,4},{6,7},{7,6},{8,9},{9,8},{10,11... | collective-permute-start | bytes 1806344 | tf_op jit(solution)/shard_map/ppermute | solution.py:85
  208.4 16.0 %collective-permute-start.7 = (bf16[8,104,768]{2,1,0:T(8,128)(2,1)S(1)}, bf16[8,104,768]{2,1,0:T(8,128)(2,1)S(1)}, u32[]{:S(2)}, u32[]{:S(2)}) collective-permute-start(bf16[8,104,768]{2,1,0:T(8,128)(2,1)S(1)} %get-tuple-element.391), channel_id=1, source_target_pairs={{0,1},{1,0},{2,3},{3,2},{4,5},{5,4},{6,7},{7,6},{8,9},{9,8},{10,11... | collective-permute-start | bytes 3833864 | tf_op jit(solution)/shard_map/ppermute | solution.py:85
  217.6 64.1 %collective-permute-start.18 = (bf16[776,768]{1,0:T(8,128)(2,1)}, bf16[776,768]{1,0:T(8,128)(2,1)}, u32[]{:S(2)}, u32[]{:S(2)}) collective-permute-start(bf16[776,768]{1,0:T(8,128)(2,1)} %get-tuple-element.405), channel_id=1, source_target_pairs={{0,1},{1,0},{2,3},{3,2},{4,5},{5,4},{6,7},{7,6},{8,9},{9,8},{10,11... | collective-permute-start | bytes 3575816 | tf_op jit(solution)/shard_map/ppermute | solution.py:85
  217.7 65.2 %collective-permute-start.17 = (bf16[776,768]{1,0:T(8,128)(2,1)}, bf16[776,768]{1,0:T(8,128)(2,1)}, u32[]{:S(2)}, u32[]{:S(2)}) collective-permute-start(bf16[776,768]{1,0:T(8,128)(2,1)} %get-tuple-element.404), channel_id=1, source_target_pairs={{0,1},{1,0},{2,3},{3,2},{4,5},{5,4},{6,7},{7,6},{8,9},{9,8},{10,11... | collective-permute-start | bytes 3575816 | tf_op jit(solution)/shard_map/ppermute | solution.py:85
  427.7 312.5 %collective-permute-start.43 = (bf16[2,776,768]{2,1,0:T(8,128)(2,1)}, bf16[2,776,768]{2,1,0:T(8,128)(2,1)}, u32[]{:S(2)}, u32[]{:S(2)}) collective-permute-start(bf16[2,776,768]{2,1,0:T(8,128)(2,1)} %pad_maximum_fusion.1), channel_id=1, source_target_pairs={{0,1},{1,0},{2,3},{3,2},{4,5},{5,4},{6,7},{7,6},{8,9},{9,8},{10,11... | collective-permute-start | bytes 7151624 | tf_op jit(solution)/shard_map/ppermute | solution.py:85
  429.8 124.5 %collective-permute-start.44 = (bf16[2,776,768]{2,1,0:T(8,128)(2,1)}, bf16[2,776,768]{2,1,0:T(8,128)(2,1)}, u32[]{:S(2)}, u32[]{:S(2)}) collective-permute-start(bf16[2,776,768]{2,1,0:T(8,128)(2,1)} %pad_maximum_fusion.2), channel_id=1, source_target_pairs={{0,1},{1,0},{2,3},{3,2},{4,5},{5,4},{6,7},{7,6},{8,9},{9,8},{10,11... | collective-permute-start | bytes 7151624 | tf_op jit(solution)/shard_map/ppermute | solution.py:85
  448.3 32.3 %collective-permute-start.23 = (bf16[8,104,768]{2,1,0:T(8,128)(2,1)}, bf16[8,104,768]{2,1,0:T(8,128)(2,1)}, u32[]{:S(2)}, u32[]{:S(2)}) collective-permute-start(bf16[8,104,768]{2,1,0:T(8,128)(2,1)} %get-tuple-element.389), channel_id=1, source_target_pairs={{0,1},{1,0},{2,3},{3,2},{4,5},{5,4},{6,7},{7,6},{8,9},{9,8},{10,11... | collective-permute-start | bytes 3833864 | tf_op jit(solution)/shard_map/ppermute | solution.py:85
  528.3 35.7 %collective-permute-start.24 = (bf16[8,104,768]{2,1,0:T(8,128)(2,1)}, bf16[8,104,768]{2,1,0:T(8,128)(2,1)}, u32[]{:S(2)}, u32[]{:S(2)}) collective-permute-start(bf16[8,104,768]{2,1,0:T(8,128)(2,1)} %get-tuple-element.384), channel_id=1, source_target_pairs={{0,1},{1,0},{2,3},{3,2},{4,5},{5,4},{6,7},{7,6},{8,9},{9,8},{10,11... | collective-permute-start | bytes 3833864 | tf_op jit(solution)/shard_map/ppermute | solution.py:85
  548.5 11.9 %collective-permute-start.37 = (bf16[2,392,768]{2,1,0:T(8,128)(2,1)}, bf16[2,392,768]{2,1,0:T(8,128)(2,1)}, u32[]{:S(2)}, u32[]{:S(2)}) collective-permute-start(bf16[2,392,768]{2,1,0:T(8,128)(2,1)} %pad_maximum_fusion.10), channel_id=1, source_target_pairs={{0,1},{1,0},{2,3},{3,2},{4,5},{5,4},{6,7},{7,6},{8,9},{9,8},{10,11... | collective-permute-start | bytes 3612680 | tf_op jit(solution)/shard_map/ppermute | solution.py:85
  551.5 143.0 %collective-permute-start.36 = (bf16[2,392,768]{2,1,0:T(8,128)(2,1)}, bf16[2,392,768]{2,1,0:T(8,128)(2,1)}, u32[]{:S(2)}, u32[]{:S(2)}) collective-permute-start(bf16[2,392,768]{2,1,0:T(8,128)(2,1)} %pad_maximum_fusion.9), channel_id=1, source_target_pairs={{0,1},{1,0},{2,3},{3,2},{4,5},{5,4},{6,7},{7,6},{8,9},{9,8},{10,11... | collective-permute-start | bytes 3612680 | tf_op jit(solution)/shard_map/ppermute | solution.py:85
  558.9 190.0 %collective-permute-start.45 = (bf16[2,776,768]{2,1,0:T(8,128)(2,1)}, bf16[2,776,768]{2,1,0:T(8,128)(2,1)}, u32[]{:S(2)}, u32[]{:S(2)}) collective-permute-start(bf16[2,776,768]{2,1,0:T(8,128)(2,1)} %pad_maximum_fusion.3), channel_id=1, source_target_pairs={{0,4},{4,0},{8,12},{12,8},{16,20},{20,16},{24,28},{28,24},{1,5},{5... | collective-permute-start | bytes 7151624 | tf_op jit(solution)/shard_map/ppermute | solution.py:88
  563.5 131.5 %collective-permute-start.38 = (bf16[2,392,768]{2,1,0:T(8,128)(2,1)}, bf16[2,392,768]{2,1,0:T(8,128)(2,1)}, u32[]{:S(2)}, u32[]{:S(2)}) collective-permute-start(bf16[2,392,768]{2,1,0:T(8,128)(2,1)} %pad_maximum_fusion.11), channel_id=1, source_target_pairs={{0,4},{4,0},{8,12},{12,8},{16,20},{20,16},{24,28},{28,24},{1,5},{5... | collective-permute-start | bytes 3612680 | tf_op jit(solution)/shard_map/ppermute | solution.py:88
  679.0 20.8 %collective-permute-start.27 = (bf16[2,392,768]{2,1,0:T(8,128)(2,1)}, bf16[2,392,768]{2,1,0:T(8,128)(2,1)}, u32[]{:S(2)}, u32[]{:S(2)}) collective-permute-start(bf16[2,392,768]{2,1,0:T(8,128)(2,1)} %pad_maximum_fusion.7), channel_id=1, source_target_pairs={{0,1},{1,0},{2,3},{3,2},{4,5},{5,4},{6,7},{7,6},{8,9},{9,8},{10,11... | collective-permute-start | bytes 3612680 | tf_op jit(solution)/shard_map/ppermute | solution.py:85
  694.5 74.7 %collective-permute-start.21 = (bf16[4,196,768]{2,0,1:T(4,128)(2,1)}, bf16[4,196,768]{2,0,1:T(4,128)(2,1)}, u32[]{:S(2)}, u32[]{:S(2)}) collective-permute-start(bf16[4,196,768]{2,0,1:T(4,128)(2,1)} %copy.130), channel_id=1, source_target_pairs={{0,2},{1,3},{2,0},{3,1},{4,6},{5,7},{6,4},{7,5},{8,10},{9,11},{10,... | collective-permute-start | bytes 3612680 | tf_op jit(solution)/shard_map/ppermute | solution.py:85
  697.6 38.7 %collective-permute-start.39 = (bf16[392,768]{1,0:T(8,128)(2,1)}, bf16[392,768]{1,0:T(8,128)(2,1)}, u32[]{:S(2)}, u32[]{:S(2)}) collective-permute-start(bf16[392,768]{1,0:T(8,128)(2,1)} %fusion.185), channel_id=1, source_target_pairs={{0,2},{1,3},{2,0},{3,1},{4,6},{5,7},{6,4},{7,5},{8,10},{9,11},{10,... | collective-permute-start | bytes 1806344 | tf_op jit(solution)/shard_map/ppermute | solution.py:85
  699.9 56.8 %collective-permute-start.26 = (bf16[2,392,768]{2,1,0:T(8,128)(2,1)}, bf16[2,392,768]{2,1,0:T(8,128)(2,1)}, u32[]{:S(2)}, u32[]{:S(2)}) collective-permute-start(bf16[2,392,768]{2,1,0:T(8,128)(2,1)} %pad_maximum_fusion.6), channel_id=1, source_target_pairs={{0,1},{1,0},{2,3},{3,2},{4,5},{5,4},{6,7},{7,6},{8,9},{9,8},{10,11... | collective-permute-start | bytes 3612680 | tf_op jit(solution)/shard_map/ppermute | solution.py:85
  736.3 28.1 %collective-permute-start.28 = (bf16[2,392,768]{2,1,0:T(8,128)(2,1)}, bf16[2,392,768]{2,1,0:T(8,128)(2,1)}, u32[]{:S(2)}, u32[]{:S(2)}) collective-permute-start(bf16[2,392,768]{2,1,0:T(8,128)(2,1)} %pad_maximum_fusion.8), channel_id=1, source_target_pairs={{0,4},{4,0},{8,12},{12,8},{16,20},{20,16},{24,28},{28,24},{1,5},{5... | collective-permute-start | bytes 3612680 | tf_op jit(solution)/shard_map/ppermute | solution.py:88
  740.2 14.6 %collective-permute-start.40 = (bf16[392,768]{1,0:T(8,128)(2,1)}, bf16[392,768]{1,0:T(8,128)(2,1)}, u32[]{:S(2)}, u32[]{:S(2)}) collective-permute-start(bf16[392,768]{1,0:T(8,128)(2,1)} %fusion.188), channel_id=1, source_target_pairs={{0,8},{4,12},{8,0},{12,4},{16,24},{20,28},{24,16},{28,20},{1,9},{5... | collective-permute-start | bytes 1806344 | tf_op jit(solution)/shard_map/ppermute | solution.py:88
  748.9 19.7 %collective-permute-start.30 = (bf16[16,768]{1,0:T(8,128)(2,1)S(1)}, bf16[16,768]{1,0:T(8,128)(2,1)S(1)}, u32[]{:S(2)}, u32[]{:S(2)}) collective-permute-start(bf16[16,768]{1,0:T(8,128)(2,1)S(1)} %pad.130), channel_id=1, source_target_pairs={{0,1},{1,0},{2,3},{3,2},{4,5},{5,4},{6,7},{7,6},{8,9},{9,8},{10,11... | collective-permute-start | bytes 73736 | tf_op jit(solution)/shard_map/ppermute | solution.py:85
  754.8 73.4 %collective-permute-start.25 = (bf16[4,196,768]{2,0,1:T(4,128)(2,1)S(1)}, bf16[4,196,768]{2,0,1:T(4,128)(2,1)S(1)}, u32[]{:S(2)}, u32[]{:S(2)}) collective-permute-start(bf16[4,196,768]{2,0,1:T(4,128)(2,1)S(1)} %copy.151), channel_id=1, source_target_pairs={{0,2},{1,3},{2,0},{3,1},{4,6},{5,7},{6,4},{7,5},{8,10},{9,11},{10,... | collective-permute-start | bytes 3612680 | tf_op jit(solution)/shard_map/ppermute | solution.py:85
  756.7 68.5 %collective-permute-start.46 = (bf16[776,768]{1,0:T(8,128)(2,1)S(1)}, bf16[776,768]{1,0:T(8,128)(2,1)S(1)}, u32[]{:S(2)}, u32[]{:S(2)}) collective-permute-start(bf16[776,768]{1,0:T(8,128)(2,1)S(1)} %fusion.160), channel_id=1, source_target_pairs={{0,2},{1,3},{2,0},{3,1},{4,6},{5,7},{6,4},{7,5},{8,10},{9,11},{10,... | collective-permute-start | bytes 3575816 | tf_op jit(solution)/shard_map/ppermute | solution.py:85
  764.4 55.7 %collective-permute-start.41 = (bf16[392,768]{1,0:T(8,128)(2,1)S(1)}, bf16[392,768]{1,0:T(8,128)(2,1)S(1)}, u32[]{:S(2)}, u32[]{:S(2)}) collective-permute-start(bf16[392,768]{1,0:T(8,128)(2,1)S(1)} %add.650), channel_id=1, source_target_pairs={{0,16},{4,20},{8,24},{12,28},{16,0},{20,4},{24,8},{28,12},{1,17},{... | collective-permute-start | bytes 1806344 | tf_op jit(solution)/shard_map/ppermute | solution.py:88
  768.6 53.3 %collective-permute-start.29 = (bf16[392,768]{1,0:T(8,128)(2,1)S(1)}, bf16[392,768]{1,0:T(8,128)(2,1)S(1)}, u32[]{:S(2)}, u32[]{:S(2)}) collective-permute-start(bf16[392,768]{1,0:T(8,128)(2,1)S(1)} %fusion.190), channel_id=1, source_target_pairs={{0,2},{1,3},{2,0},{3,1},{4,6},{5,7},{6,4},{7,5},{8,10},{9,11},{10,... | collective-permute-start | bytes 1806344 | tf_op jit(solution)/shard_map/ppermute | solution.py:85
  773.1 47.0 %collective-permute-start.32 = (bf16[16,768]{1,0:T(8,128)(2,1)S(1)}, bf16[16,768]{1,0:T(8,128)(2,1)S(1)}, u32[]{:S(2)}, u32[]{:S(2)}) collective-permute-start(bf16[16,768]{1,0:T(8,128)(2,1)S(1)} %add.639), channel_id=1, source_target_pairs={{0,2},{1,3},{2,0},{3,1},{4,6},{5,7},{6,4},{7,5},{8,10},{9,11},{10,... | collective-permute-start | bytes 73736 | tf_op jit(solution)/shard_map/ppermute | solution.py:85
  820.3 12.6 %collective-permute-start.42 = (bf16[392,768]{1,0:T(8,128)(2,1)S(1)}, bf16[392,768]{1,0:T(8,128)(2,1)S(1)}, u32[]{:S(2)}, u32[]{:S(2)}) collective-permute-start(bf16[392,768]{1,0:T(8,128)(2,1)S(1)} %add.651), channel_id=1, source_target_pairs={{0,4},{4,0},{8,12},{12,8},{16,20},{20,16},{24,28},{28,24},{1,5},{5... | collective-permute-start | bytes 1806344 | tf_op jit(solution)/shard_map/ppermute | solution.py:88
  823.6 23.8 %collective-permute-start.33 = (bf16[408,768]{1,0:T(8,128)(2,1)S(1)}, bf16[408,768]{1,0:T(8,128)(2,1)S(1)}, u32[]{:S(2)}, u32[]{:S(2)}) collective-permute-start(bf16[408,768]{1,0:T(8,128)(2,1)S(1)} %pad_maximum_fusion.18), channel_id=1, source_target_pairs={{0,8},{4,12},{8,0},{12,4},{16,24},{20,28},{24,16},{28,20},{1,9},{5... | collective-permute-start | bytes 1880072 | tf_op jit(solution)/shard_map/ppermute | solution.py:88
  827.7 48.0 %collective-permute-start.47 = (bf16[776,768]{1,0:T(8,128)(2,1)S(1)}, bf16[776,768]{1,0:T(8,128)(2,1)S(1)}, u32[]{:S(2)}, u32[]{:S(2)}) collective-permute-start(bf16[776,768]{1,0:T(8,128)(2,1)S(1)} %fusion.163), channel_id=1, source_target_pairs={{0,8},{4,12},{8,0},{12,4},{16,24},{20,28},{24,16},{28,20},{1,9},{5... | collective-permute-start | bytes 3575816 | tf_op jit(solution)/shard_map/ppermute | solution.py:88
  847.6 30.3 %collective-permute-start.34 = (bf16[408,768]{1,0:T(8,128)(2,1)S(1)}, bf16[408,768]{1,0:T(8,128)(2,1)S(1)}, u32[]{:S(2)}, u32[]{:S(2)}) collective-permute-start(bf16[408,768]{1,0:T(8,128)(2,1)S(1)} %fusion.257), channel_id=1, source_target_pairs={{0,16},{4,20},{8,24},{12,28},{16,0},{20,4},{24,8},{28,12},{1,17},{... | collective-permute-start | bytes 1880072 | tf_op jit(solution)/shard_map/ppermute | solution.py:88
  876.0 52.8 %collective-permute-start.48 = (bf16[776,768]{1,0:T(8,128)(2,1)S(1)}, bf16[776,768]{1,0:T(8,128)(2,1)S(1)}, u32[]{:S(2)}, u32[]{:S(2)}) collective-permute-start(bf16[776,768]{1,0:T(8,128)(2,1)S(1)} %add.659), channel_id=1, source_target_pairs={{0,16},{4,20},{8,24},{12,28},{16,0},{20,4},{24,8},{28,12},{1,17},{... | collective-permute-start | bytes 3575816 | tf_op jit(solution)/shard_map/ppermute | solution.py:88
  878.2 11.4 %collective-permute-start.35 = (bf16[392,768]{1,0:T(8,128)(2,1)S(1)}, bf16[392,768]{1,0:T(8,128)(2,1)S(1)}, u32[]{:S(2)}, u32[]{:S(2)}) collective-permute-start(bf16[392,768]{1,0:T(8,128)(2,1)S(1)} %slice.1705), channel_id=1, source_target_pairs={{0,4},{4,0},{8,12},{12,8},{16,20},{20,16},{24,28},{28,24},{1,5},{5... | collective-permute-start | bytes 1806344 | tf_op jit(solution)/shard_map/ppermute | solution.py:88
  929.1 28.2 %collective-permute-start.49 = (bf16[776,768]{1,0:T(8,128)(2,1)S(1)}, bf16[776,768]{1,0:T(8,128)(2,1)S(1)}, u32[]{:S(2)}, u32[]{:S(2)}) collective-permute-start(bf16[776,768]{1,0:T(8,128)(2,1)S(1)} %add.660), channel_id=1, source_target_pairs={{0,4},{4,0},{8,12},{12,8},{16,20},{20,16},{24,28},{28,24},{1,5},{5... | collective-permute-start | bytes 3575816 | tf_op jit(solution)/shard_map/ppermute | solution.py:88
  (252 other events, 3620.0 us)

commit v2 on v1

v2 whole, which is shorter than its diff:
```python
import functools

import jax
import jax.numpy as jnp
from jax import lax
from jax.experimental import pallas as pl
from jax.experimental.pallas import tpu as pltpu
from jax.sharding import PartitionSpec as P

BF = jnp.bfloat16
F32 = jnp.float32
HEAD_DIM = 64
norm_epsilon = 1e-06
LIMIT = 60 << 20


def nn(a, b):
    return lax.dot_general(a, b, (((1,), (0,)), ((), ())), preferred_element_type=F32)


def nt(a, b):
    return lax.dot_general(a, b, (((1,), (1,)), ((), ())), preferred_element_type=F32)


def tn(a, b):
    return lax.dot_general(a, b, (((0,), (0,)), ((), ())), preferred_element_type=F32)


def hat_of(values):
    mean = jnp.mean(values, axis=-1, keepdims=True)
    centered = values - mean
    inv = lax.rsqrt(jnp.mean(centered * centered, axis=-1, keepdims=True) + norm_epsilon)
    return centered * inv, inv


def hat_back(hat, inv, gain, grad):
    e = grad * gain
    return inv * (
        e - jnp.mean(e, axis=-1, keepdims=True) - hat * jnp.mean(e * hat, axis=-1, keepdims=True)
    )


GROUP = 256
PER = GROUP // HEAD_DIM


def head_of_lane(rows):
    return lax.broadcasted_iota(jnp.int32, (rows, GROUP), 1) // HEAD_DIM


def stacked(v):
    lane = head_of_lane(v.shape[0])
    return jnp.concatenate([jnp.where(lane == h, v, jnp.zeros_like(v)) for h in range(PER)])


def unstacked(v):
    rows = v.shape[0] // PER
    lane = head_of_lane(rows)
    out = v[:rows]
    for h in range(1, PER):
        out = jnp.where(lane == h, v[h * rows : (h + 1) * rows], out)
    return out


def only_places(places):
    def mask(s):
        cut = places // 8 * 8
        row = lax.broadcasted_iota(jnp.int32, (s.shape[0] - cut, s.shape[1]), 0)
        return jnp.concatenate([s[:cut], jnp.where(row < places - cut, s[cut:], -1e30)])

    return mask


def same_place(bias):
    return lambda s: s + bias


def place_bias(rows):
    a = lax.broadcasted_iota(jnp.int32, (rows, PER * rows), 0) & 7
    b = lax.broadcasted_iota(jnp.int32, (rows, PER * rows), 1) & 7
    return jnp.where(a == b, 0.0, -1e30).astype(F32)


def attend(q_ref, k_ref, v_ref, o_ref, lse_ref, mask):
    for g in range(o_ref.shape[1] // GROUP):
        at = slice(GROUP * g, GROUP * g + GROUP)
        s = mask(nt(k_ref[:, at], stacked(q_ref[:, at])))
        top = jnp.max(s, axis=0, keepdims=True)
        ex = jnp.exp(s - top)
        total = jnp.sum(ex, axis=0, keepdims=True)
        p = (ex * (1.0 / total)).astype(BF)
        o_ref[:, at] = unstacked(tn(p, v_ref[:, at])).astype(BF)
        lse_ref[g : g + 1] = top + jnp.log(total)


def attend_back(q_ref, k_ref, v_ref, do_ref, lse_ref, dq_ref, dk_ref, dv_ref, mask):
    for g in range(do_ref.shape[1] // GROUP):
        at = slice(GROUP * g, GROUP * g + GROUP)
        qs, dos = stacked(q_ref[:, at]), stacked(do_ref[:, at])
        k = k_ref[:, at]
        p = jnp.exp(mask(nt(k, qs)) - lse_ref[g : g + 1])
        dp = nt(v_ref[:, at], dos)
        ds = (p * (dp - jnp.sum(p * dp, axis=0, keepdims=True))).astype(BF)
        dv_ref[:, at] = nn(p.astype(BF), dos).astype(BF)
        dk_ref[:, at] = nn(ds, qs).astype(BF)
        dq_ref[:, at] = (unstacked(tn(ds, k)) * HEAD_DIM**-0.5).astype(BF)


def whole(shape):
    return pl.BlockSpec(shape, lambda *_: (0,) * len(shape), pipeline_mode=pl.Buffered(1))


def params(n=1):
    return pltpu.CompilerParams(
        dimension_semantics=("arbitrary",) * n, vmem_limit_bytes=LIMIT
    )


def spatial_body(places, x, w, wo, vec, stream, n1, q, k, v, o, lse):
    xv = x[0].astype(F32)
    d = xv.shape[1]
    n0 = (hat_of(xv)[0] * vec[0:1] + vec[1:2]).astype(BF)
    q[0] = ((nt(n0, w[0:d]) + vec[2:3]) * HEAD_DIM**-0.5).astype(BF)
    k[0] = nt(n0, w[d : 2 * d]).astype(BF)
    v[0] = (nt(n0, w[2 * d : 3 * d]) + vec[3:4]).astype(BF)
    attend(q.at[0], k.at[0], v.at[0], o.at[0], lse.at[0], only_places(places))
    s1 = xv + (nn(o[0], wo[...]) + vec[4:5])
    stream[0] = s1
    n1[0] = (hat_of(s1)[0] * vec[5:6] + vec[6:7]).astype(BF)


def spatial(x, w, wo, vec, places):
    f, r, d = x.shape
    blk = pl.BlockSpec((1, r, d), lambda i: (i, 0, 0))
    big = jax.ShapeDtypeStruct((f, r, d), BF)
    return pl.pallas_call(
        functools.partial(spatial_body, places),
        grid=(f,),
        in_specs=[blk, whole(w.shape), whole(wo.shape), whole(vec.shape)],
        out_specs=[blk] * 6 + [pl.BlockSpec((1, d // GROUP, PER * r), lambda i: (i, 0, 0))],
        out_shape=[jax.ShapeDtypeStruct((f, r, d), F32)]
        + [big] * 5
        + [jax.ShapeDtypeStruct((f, d // GROUP, PER * r), F32)],
        compiler_params=params(),
        name="spatial",
    )(x, w, wo, vec)


def temporal_body(n1, w, vec, q, k, v, o, lse):
    n = n1[0]
    d = n.shape[1]
    q[0] = ((nt(n, w[0:d]) + vec[0:1]) * HEAD_DIM**-0.5).astype(BF)
    k[0] = nt(n, w[d : 2 * d]).astype(BF)
    v[0] = (nt(n, w[2 * d : 3 * d]) + vec[1:2]).astype(BF)
    attend(q.at[0], k.at[0], v.at[0], o.at[0], lse.at[0], same_place(place_bias(n.shape[0])))


def temporal(n1, w, vec):
    b, r, d = n1.shape
    blk = pl.BlockSpec((1, r, d), lambda i: (i, 0, 0))
    return pl.pallas_call(
        temporal_body,
        grid=(b,),
        in_specs=[blk, whole(w.shape), whole(vec.shape)],
        out_specs=[blk] * 4 + [pl.BlockSpec((1, d // GROUP, PER * r), lambda i: (i, 0, 0))],
        out_shape=[jax.ShapeDtypeStruct((b, r, d), BF)] * 4
        + [jax.ShapeDtypeStruct((b, d // GROUP, PER * r), F32)],
        compiler_params=params(),
        name="temporal",
    )(n1, w, vec)


def temporal_back_body(g, n, q, k, v, o, lse, w, wo, dn, gw, gwo, sums, dqkv, do):
    i = pl.program_id(0)
    d = g.shape[-1]
    r = q.shape[1]
    do[...] = nt(g[pl.ds(i, 1)][0], wo[...]).astype(BF)
    attend_back(
        q.at[0], k.at[0], v.at[0], do, lse.at[0],
        dqkv.at[0, i], dqkv.at[1, i], dqkv.at[2, i], same_place(place_bias(r)),
    )

    @pl.when(i == pl.num_programs(0) - 1)
    def _():
        rows = g.shape[0] * r
        nv = n[...].reshape(rows, d)
        for c in range(3):
            dv = dqkv[c].reshape(rows, d)
            gw[c * d : (c + 1) * d] = tn(dv, nv).astype(BF)
            sums[c : c + 1] = jnp.sum(dv.astype(F32), axis=0, keepdims=True)
        gwo[...] = tn(o[...].reshape(rows, d), g[...].reshape(rows, d)).astype(BF)
        acc = nn(dqkv[0].reshape(rows, d), w[0:d])
        acc += nn(dqkv[1].reshape(rows, d), w[d : 2 * d])
        acc += nn(dqkv[2].reshape(rows, d), w[2 * d : 3 * d])
        dn[...] = acc.astype(BF).reshape(dn.shape)


def temporal_back(g, n, q, k, v, o, lse, w, wo):
    b, r, d = g.shape
    blk = pl.BlockSpec((1, r, d), lambda i: (i, 0, 0))
    return pl.pallas_call(
        temporal_back_body,
        grid=(b,),
        in_specs=[whole(g.shape), whole(n.shape), blk, blk, blk, whole(o.shape),
                  pl.BlockSpec((1, d // GROUP, PER * r), lambda i: (i, 0, 0)), whole(w.shape), whole(wo.shape)],
        out_specs=[whole(g.shape), whole(w.shape), whole(wo.shape), whole((8, d))],
        out_shape=[jax.ShapeDtypeStruct(g.shape, BF), jax.ShapeDtypeStruct(w.shape, BF),
                   jax.ShapeDtypeStruct(wo.shape, BF), jax.ShapeDtypeStruct((8, d), F32)],
        scratch_shapes=[pltpu.VMEM((3, b, r, d), BF), pltpu.VMEM((r, d), BF)],
        compiler_params=params(),
        name="temporal_back",
    )(g, n, q, k, v, o, lse, w, wo)


def spatial_back_body(places, x, s1, dn1, g2, q, k, v, o, lse, w, wo, vec,
                      g0, gw, gwo, sums, dqkv, n0s, gbs, os, do):
    i = pl.program_id(0)
    r, d = x.shape[1:]

    @pl.when(i == 0)
    def _():
        sums[...] = jnp.zeros_like(sums)

    def add(at, val):
        sums[at : at + 1] += jnp.sum(val, axis=0, keepdims=True)

    hat, inv = hat_of(s1[0])
    dn = dn1[0].astype(F32)
    add(2, dn * hat)
    add(3, dn)
    g1 = g2[0] + hat_back(hat, inv, vec[2:3], dn)
    add(4, g1)
    gb = g1.astype(BF)
    gbs[i] = gb
    os[i] = o[0]
    do[...] = nt(gb, wo[...]).astype(BF)
    attend_back(
        q.at[0], k.at[0], v.at[0], do, lse.at[0],
        dqkv.at[0, i], dqkv.at[1, i], dqkv.at[2, i], only_places(places),
    )
    hat, inv = hat_of(x[0].astype(F32))
    n0s[i] = (hat * vec[0:1] + vec[1:2]).astype(BF)
    dn = nn(dqkv[0, i], w[0:d]) + nn(dqkv[1, i], w[d : 2 * d]) + nn(dqkv[2, i], w[2 * d : 3 * d])
    add(0, dn * hat)
    add(1, dn)
    g0[0] = g1 + hat_back(hat, inv, vec[0:1], dn)

    @pl.when(i == pl.num_programs(0) - 1)
    def _():
        rows = n0s.shape[0] * r
        nv = n0s[...].reshape(rows, d)
        for c in range(3):
            dv = dqkv[c].reshape(rows, d)
            gw[c * d : (c + 1) * d] = tn(dv, nv).astype(BF)
            sums[5 + c : 6 + c] = jnp.sum(dv.astype(F32), axis=0, keepdims=True)
        gwo[...] = tn(os[...].reshape(rows, d), gbs[...].reshape(rows, d)).astype(BF)


def spatial_back(x, s1, dn1, g2, q, k, v, o, lse, w, wo, vec, places):
    f, r, d = x.shape
    blk = pl.BlockSpec((1, r, d), lambda i: (i, 0, 0))
    return pl.pallas_call(
        functools.partial(spatial_back_body, places),
        grid=(f,),
        in_specs=[blk] * 8 + [pl.BlockSpec((1, d // GROUP, PER * r), lambda i: (i, 0, 0)),
                  whole(w.shape), whole(wo.shape), whole(vec.shape)],
        out_specs=[blk, whole(w.shape), whole(wo.shape), whole((8, d))],
        out_shape=[jax.ShapeDtypeStruct(x.shape, F32), jax.ShapeDtypeStruct(w.shape, BF),
                   jax.ShapeDtypeStruct(wo.shape, BF), jax.ShapeDtypeStruct((8, d), F32)],
        scratch_shapes=[pltpu.VMEM((3, f, r, d), BF)] + [pltpu.VMEM((f, r, d), BF)] * 3
        + [pltpu.VMEM((r, d), BF)],
        compiler_params=params(),
        name="spatial_back",
    )(x, s1, dn1, g2, q, k, v, o, lse, w, wo, vec)


def gelu_parts(u):
    cdf = 0.5 + 0.5 * lax.erf(u * 0.7071067811865476)
    return u * cdf, cdf + u * (jnp.exp(-0.5 * u * u) * 0.3989422804014327)


def mlp_step(n2, gb, wt, wd, b, s, branch, dn, gwt, gwd, gbi):
    u = nt(n2, wt[s]) + b[s]
    h, slope = gelu_parts(u)
    h = h.astype(BF)
    branch[...] += nn(h, wd[s])
    dr = (nt(gb, wd[s]) * slope).astype(BF)
    dn[...] += nn(dr, wt[s])
    gwt[s] += tn(dr, n2)
    gwd[s] += tn(h, gb)
    gbi[s] += jnp.sum(dr.astype(F32), axis=0, keepdims=True)


def mlp_ends(i, s, gwt, gwd, gbi, gwt_o, gwd_o):
    @pl.when(i == pl.num_programs(0) - 1)
    def _():
        gwt_o[s] = gwt[s].astype(BF)
        gwd_o[s] = gwd[s].astype(BF)


def mlp_first_body(s1, o1, gb, wo, vec, wt, wd, b, s2, n2, branch, dn, gwt_o, gwd_o, gbi, gwt, gwd):
    i, s = pl.program_id(0), pl.program_id(1)

    @pl.when((i == 0) & (s == 0))
    def _():
        gwt[...] = jnp.zeros_like(gwt)
        gwd[...] = jnp.zeros_like(gwd)
        gbi[...] = jnp.zeros_like(gbi)

    @pl.when(s == 0)
    def _():
        v = s1[...] + (nn(o1[...], wo[...]) + vec[0:1])
        s2[...] = v
        n2[...] = (hat_of(v)[0] * vec[1:2] + vec[2:3]).astype(BF)
        branch[...] = jnp.zeros_like(branch)
        dn[...] = jnp.zeros_like(dn)

    mlp_step(n2[...], gb[...], wt, wd, b, s, branch, dn, gwt, gwd, gbi)
    mlp_ends(i, s, gwt, gwd, gbi, gwt_o, gwd_o)


def mlp_first(s1, o1, gb, wo, vec, wt, wd, b, tile):
    rows, d = s1.shape
    ns, h, _ = wt.shape
    blk = pl.BlockSpec((tile, d), lambda i, s: (i, 0))
    sh = lambda t: jax.ShapeDtypeStruct((rows, d), t)
    return pl.pallas_call(
        mlp_first_body,
        grid=(rows // tile, ns),
        in_specs=[blk, blk, blk, whole(wo.shape), whole(vec.shape), whole(wt.shape),
                  whole(wd.shape), whole(b.shape)],
        out_specs=[blk] * 4 + [whole(wt.shape), whole(wd.shape), whole(b.shape)],
        out_shape=[sh(F32), sh(BF), sh(F32), sh(F32), jax.ShapeDtypeStruct(wt.shape, BF),
                   jax.ShapeDtypeStruct(wd.shape, BF), jax.ShapeDtypeStruct(b.shape, F32)],
        scratch_shapes=[pltpu.VMEM(wt.shape, F32), pltpu.VMEM(wd.shape, F32)],
        compiler_params=params(2),
        name="mlp_first",
    )(s1, o1, gb, wo, vec, wt, wd, b)


def mlp_second_body(s2, n2, gb, br0, dn0, vec, wt, wd, b,
                    out, g2, g2b, gwt_o, gwd_o, gbi, sums, branch, dn, gwt, gwd):
    i, s = pl.program_id(0), pl.program_id(1)

    @pl.when((i == 0) & (s == 0))
    def _():
        gwt[...] = jnp.zeros_like(gwt)
        gwd[...] = jnp.zeros_like(gwd)
        gbi[...] = jnp.zeros_like(gbi)
        sums[...] = jnp.zeros_like(sums)

    @pl.when(s == 0)
    def _():
        branch[...] = br0[...]
        dn[...] = dn0[...]

    mlp_step(n2[...], gb[...], wt, wd, b, s, branch, dn, gwt, gwd, gbi)
    mlp_ends(i, s, gwt, gwd, gbi, gwt_o, gwd_o)

    @pl.when(s == pl.num_programs(1) - 1)
    def _():
        def add(at, val):
            sums[at : at + 1] += jnp.sum(val, axis=0, keepdims=True)

        v = s2[...]
        out[...] = (v + (branch[...] + vec[0:1])).astype(out.dtype)
        hat, inv = hat_of(v)
        dv = dn[...]
        add(0, dv * hat)
        add(1, dv)
        g3 = gb[...].astype(F32)
        add(3, g3)
        g = g3 + hat_back(hat, inv, vec[1:2], dv)
        add(2, g)
        g2[...] = g
        g2b[...] = g.astype(BF)


def mlp_second(s2, n2, gb, br0, dn0, vec, wt, wd, b, tile):
    rows, d = s2.shape
    ns, h, _ = wt.shape
    blk = pl.BlockSpec((tile, d), lambda i, s: (i, 0))
    sh = lambda t: jax.ShapeDtypeStruct((rows, d), t)
    return pl.pallas_call(
        mlp_second_body,
        grid=(rows // tile, ns),
        in_specs=[blk] * 5 + [whole(vec.shape), whole(wt.shape), whole(wd.shape), whole(b.shape)],
        out_specs=[blk] * 3 + [whole(wt.shape), whole(wd.shape), whole(b.shape), whole((8, d))],
        out_shape=[sh(F32), sh(F32), sh(BF), jax.ShapeDtypeStruct(wt.shape, BF),
                   jax.ShapeDtypeStruct(wd.shape, BF), jax.ShapeDtypeStruct(b.shape, F32),
                   jax.ShapeDtypeStruct((8, d), F32)],
        scratch_shapes=[pltpu.VMEM((tile, d), F32), pltpu.VMEM((tile, d), F32),
                        pltpu.VMEM(wt.shape, F32), pltpu.VMEM(wd.shape, F32)],
        compiler_params=params(2),
        name="mlp_second",
    )(s2, n2, gb, br0, dn0, vec, wt, wd, b)


ROWS = 208
HALF = ROWS // 2
TILE = 416


def shards(clips, cot, gain, shift, qkv, qvb, wout, bout, win, b_in, wdown, bdown):
    tensor = lax.axis_index("tensor")
    y, core = tensor // 2, tensor % 2
    x = lax.axis_index("dp") % 2
    dp = lax.axis_size("dp")
    width = clips.shape[-1]
    places = clips.shape[2]
    e = qkv.shape[-1]
    h = win.shape[1] // 2

    def over_tensor(v, bit):
        return lax.ppermute(v, "tensor", [(i, i ^ bit) for i in range(4)])

    def over_dp(v, bit):
        return lax.ppermute(v, "dp", [(i, i ^ bit) for i in range(dp)])

    def pad(v):
        return jnp.pad(v, ((0, 0), (0, ROWS - places), (0, 0)))

    def split(a, b):
        return jnp.where(x == 0, a, b), jnp.where(x == 0, b, a)

    def whole_clip(v):
        mine = lax.dynamic_index_in_dim(v, y, 0, False)
        other = lax.dynamic_index_in_dim(v, 1 - y, 0, False)
        return pad(jnp.concatenate([mine, over_tensor(other, 2)]))

    def back(v):
        n = v.shape[0] // 2
        v = v[:, :places]
        got = over_tensor(v[n:].astype(BF), 2).astype(F32)
        mine = v[:n]
        return jnp.stack([jnp.where(y == 0, mine, got), jnp.where(y == 0, got, mine)])

    def hi_lo(v):
        hi = v.astype(BF)
        return hi, (v - hi.astype(F32)).astype(BF)

    def gather(halves):
        send, keep = split(*halves)
        gy = over_tensor(send, 2)
        gx = over_dp(gy, 1)
        two = split(gy, gx)
        three = tuple(over_tensor(v, 1) for v in two)
        one = tuple(over_tensor(v, 1) for v in halves)
        return [halves, one, two, three]

    def attn_weights(i):
        hi, lo = hi_lo(qvb[i].reshape(1, -1))
        rows = jnp.concatenate([hi, lo], axis=1)
        rows = jnp.concatenate([rows, jnp.zeros((7, width), BF)])
        a = jnp.concatenate([qkv[i, 0].T, qkv[i, 1].T, rows])
        b = jnp.concatenate([qkv[i, 2].T, wout[i], jnp.zeros((8, width), BF)])
        got = gather((a, b))
        w = jnp.concatenate(
            [g[0][:e] for g in got] + [g[0][e : 2 * e] for g in got] + [g[1][:e] for g in got]
        )
        wo = jnp.concatenate([g[1][e : 2 * e] for g in got])
        bias = [g[0][2 * e].astype(F32) for g in got]
        bias = [v[: 2 * e] + v[2 * e :] for v in bias]
        return w, wo, jnp.concatenate([v[:e] for v in bias]), jnp.concatenate([v[e:] for v in bias])

    def mlp_weights():
        wt = win.T
        out = []
        for k in range(2):
            hi, lo = hi_lo(b_in[k * h : (k + 1) * h].reshape(1, -1))
            rows = jnp.concatenate([jnp.concatenate([hi, lo], axis=1), jnp.zeros((7, width), BF)])
            out.append(
                jnp.concatenate([wt[k * h : (k + 1) * h], wdown[k * h : (k + 1) * h], rows])
            )
        got = gather(tuple(out))

        def pair(rs):
            a = jnp.stack([jnp.concatenate([v[:h] for v in got[r]]) for r in rs])
            b = jnp.stack([jnp.concatenate([v[h : 2 * h] for v in got[r]]) for r in rs])
            rows = [[v[2 * h].astype(F32) for v in got[r]] for r in rs]
            bias = jnp.stack([jnp.concatenate([v[:h] + v[h:] for v in q]) for q in rows])
            return a, b, bias[:, None, :]

        return pair((3, 1)), pair((2, 0))

    def to_places(v):
        own = lax.dynamic_slice_in_dim(v, HALF * core, HALF, 1)
        send = lax.dynamic_slice_in_dim(v, HALF * (1 - core), HALF, 1)
        both = jnp.concatenate([own, over_tensor(send, 1)])
        f = both.shape[0]
        both = both.reshape(f, HALF // 8, 8, width).transpose(1, 0, 2, 3)
        return both.reshape(HALF // 8, f * 8, width)

    def to_frames(v, flip=False):
        f = v.shape[1] // 8
        v = v.reshape(HALF // 8, f, 8, width).transpose(1, 0, 2, 3).reshape(f, HALF, width)
        own = v[: f // 2]
        got = over_tensor(v[f // 2 :], 1)
        if flip:
            got = jnp.concatenate([got[..., i * e : (i + 1) * e] for i in (1, 0, 3, 2)], axis=-1)
        return jnp.concatenate(
            [jnp.where(core == 0, own, got), jnp.where(core == 0, got, own)], axis=1
        )

    def rows8(*vs):
        return jnp.pad(jnp.stack(vs), ((0, 8 - len(vs)), (0, 0)))

    x0 = whole_clip(clips)
    frames = x0.shape[0]
    flat = (frames * ROWS, width)
    w0, wo0, bq0, bv0 = attn_weights(0)
    w1, wo1, bq1, bv1 = attn_weights(1)
    ma, mb = mlp_weights()
    gb3 = whole_clip(cot).reshape(flat)

    vec = rows8(gain[0], shift[0], bq0, bv0, bout[0], gain[1], shift[1])
    s1, n1, q0, k0, v0, o0, lse0 = spatial(x0, w0, wo0, vec, places)
    n1p = to_places(n1)
    q1, k1, v1, o1p, lse1 = temporal(n1p, w1, rows8(bq1, bv1))
    o1 = to_frames(o1p, True)

    vec = rows8(bout[1], gain[2], shift[2])
    s2, n2, branch, dn2, gwt_a, gwd_a, gb_a = mlp_first(
        s1.reshape(flat), o1.reshape(flat), gb3, wo1, vec, *ma, TILE
    )
    out, g2, g2b, gwt_b, gwd_b, gb_b, sums2 = mlp_second(
        s2, n2, gb3, branch, dn2, rows8(bdown, gain[2]), *mb, TILE
    )
    output = back(out.reshape(x0.shape))

    dn1p, gw1, gwo1, sums1 = temporal_back(
        to_places(g2b.reshape(x0.shape)), n1p, q1, k1, v1, o1p, lse1, w1, wo1
    )
    dn1 = to_frames(dn1p)
    g0, gw0, gwo0, sums0 = spatial_back(
        x0, s1, dn1, g2.reshape(x0.shape), q0, k0, v0, o0, lse0, w0, wo0,
        rows8(gain[0], shift[0], gain[1]), places,
    )
    input_grad = back(g0)

    def row_of(v):
        return jnp.pad(v.astype(BF)[None], ((0, 7), (0, width - v.shape[0])))

    def attn_pieces(gw, gwo, bq, bv):
        out = []
        for r in range(4):
            s = slice(r * e, (r + 1) * e)
            a = jnp.concatenate([gw[:width][s], gw[width : 2 * width][s], row_of(bq[s])])
            b = jnp.concatenate([gw[2 * width :][s], gwo[s], row_of(bv[s])])
            out.append(split(a, b))
        return out

    def mlp_pieces():
        out = []
        for r in range(4):
            at = {3: 0, 1: 1, 2: 0, 0: 1}[r]
            ga, gd, gb = (gwt_a, gwd_a, gb_a) if r in (3, 1) else (gwt_b, gwd_b, gb_b)
            pair = []
            for k in range(2):
                s = slice(k * h, (k + 1) * h)
                pair.append(jnp.concatenate([ga[at, s], gd[at, s], row_of(gb[at, 0, s])]))
            out.append(split(*pair))
        return out

    small = jnp.stack(
        [sums0[0], sums0[2], sums2[0], sums0[1], sums0[3], sums2[1], sums0[4], sums2[2], sums2[3]]
    ).astype(BF)
    small = jnp.pad(small, ((0, 7), (0, 0)))

    def reduce_piece(p, extra):
        c1 = over_tensor(jnp.stack([p[1][0], p[3][0]]), 1)
        c2 = over_tensor(jnp.stack([p[1][1], p[3][1]]), 1)
        keep = [p[0][0] + c1[0], p[2][0] + c1[1]]
        send = [p[0][1] + c2[0], p[2][1] + c2[1]]
        got = over_dp(jnp.stack(send), 1)
        keep = [keep[0] + got[0], keep[1] + got[1]]
        total = keep[0] + over_tensor(keep[1], 2)
        rows = 0
        if extra is not None:
            extra = extra + over_tensor(extra, 1)
            extra = extra + over_dp(extra, 1)
            extra = extra + over_tensor(extra, 2)
            rows = extra.shape[0]
            total = jnp.concatenate([total, extra])
        bit = 2
        while bit < dp:
            total = total + over_dp(total, bit)
            bit *= 2
        if extra is not None:
            total, extra = total[:-rows], total[-rows:]
        return split(total, over_dp(total, 1)), extra

    (ma, mb), _ = reduce_piece(mlp_pieces(), None)
    (a1, b1), _ = reduce_piece(attn_pieces(gw1, gwo1, sums1[0], sums1[2]), None)
    (a0, b0), small = reduce_piece(attn_pieces(gw0, gwo0, sums0[5], sums0[7]), small)
    small = small.astype(F32)

    gqkv = jnp.stack(
        [jnp.stack([a[:e].T, a[e : 2 * e].T, b[:e].T]) for a, b in ((a0, b0), (a1, b1))]
    ).astype(F32)
    gout = jnp.stack([b0[e : 2 * e], b1[e : 2 * e]]).astype(F32)
    gqv = jnp.stack(
        [jnp.stack([a[2 * e, :e], b[2 * e, :e]]) for a, b in ((a0, b0), (a1, b1))]
    ).astype(F32)
    gwin = jnp.concatenate([ma[:h], mb[:h]]).T.astype(F32)
    gwd = jnp.concatenate([ma[h : 2 * h], mb[h : 2 * h]]).astype(F32)
    gbin = jnp.concatenate([ma[2 * h, :h], mb[2 * h, :h]]).astype(F32)
    return (
        output,
        input_grad,
        small[0:3],
        small[3:6],
        gqkv,
        gqv,
        gout,
        small[6:8],
        gwin,
        gbin,
        gwd,
        small[8],
    )


def solution(mesh):
    placed = (
        P("dp", "tensor", None, None),
        P("dp", "tensor", None, None),
        P(),
        P(),
        P(None, None, None, "tensor"),
        P(None, None, "tensor"),
        P(None, "tensor", None),
        P(),
        P(None, "tensor"),
        P("tensor"),
        P("tensor", None),
        P(),
    )
    return jax.shard_map(
        shards,
        mesh=mesh,
        in_specs=placed,
        out_specs=(
            P("dp", "tensor", None, None),
            P("dp", "tensor", None, None),
            P(),
            P(),
            P(None, None, None, "tensor"),
            P(None, None, "tensor"),
            P(None, "tensor", None),
            P(),
            P(None, "tensor"),
            P("tensor"),
            P("tensor", None),
            P(),
        ),
        check_vma=False,
    )
```

time: 968 us -> 719 us (0.74)
  matrix products: 307 us -> 0 us
  Pallas kernels: 0 us -> 244 us
  other arithmetic: 181 us -> 79.5 us
  local copies, waits for them, and re-layouts: 166 us -> 96.5 us
  waiting for transfers between devices: 263 us -> 253 us
    dot_general x60 -> x0, matrix products: 307 us -> none  [dot(): return jnp.einsum(spec, a, b, preferred_element_type=F32)]
    pallas_call x0 -> x6, Pallas kernels: none -> 244 us  [the longest x1 48.9 us: spatial_back(): pl.pallas_call(functools.partial(spatial_back_body, places), grid=(f,), i...]
    convert_element_type x20 -> x8, other arithmetic: 77.2 us -> 0.74 us  [pair(): rows = [[v[2 * h].astype(F32) for v in got[r]] for r in rs]]
    ppermute x34, waiting for transfers between devices: 119 us -> 69.7 us  [over_tensor(): return lax.ppermute(v, 'tensor', [(i, i ^ bit) for i in range(4)])]
    convert_element_type x9 -> x2, local copies, waits for them, and re-layouts: 39.8 us -> 0.02 us  [row_of(): return jnp.pad(v.astype(BF)[None], ((0, 7), (0, width - v.shape[0])))]
    ppermute x16, waiting for transfers between devices: 144 us -> 183 us  [over_dp(): return lax.ppermute(v, 'dp', [(i, i ^ bit) for i in range(dp)])]
    reduce_sum x14 -> x0, other arithmetic: 36 us -> none  [the longest x2 15.6 us: attention(): total = jnp.sum(ex, axis=-1, keepdims=True)]
    slice x52 -> x31, local copies, waits for them, and re-layouts: 41.5 us -> 24.4 us  [the longest x4 11.2 us: attn_pieces(): b = jnp.concatenate([gw[2 * width:][s], gwo[s], row_of(bv[s])])]
  transfers between devices with their start and end apart: 50 -> 50, of which waited for: 14 -> 13; matrix products, arithmetic and copies ran while one was open for 51% -> 21% of each run, Pallas kernels for 0% -> 22%
where the time goes in v2:
time: 719 us; the launch traced here: 714 us
  waiting for transfers between devices  253 us (35%)
  Pallas kernels  244 us (34%)
  local copies, waits for them, and re-layouts  96.5 us (13%)
  other arithmetic  79.5 us (11%)
  starting transfers between devices  39.2 us (5%)
    ppermute x16, waiting for transfers between devices, over_dp(): return lax.ppermute(v, 'dp', [(i, i ^ bit) for i in range(dp)])  183 us
    ppermute x34, waiting for transfers between devices, over_tensor(): return lax.ppermute(v, 'tensor', [(i, i ^ bit) for i in range(4)])  69.7 us
    pallas_call x1, Pallas kernels, spatial_back(): pl.pallas_call(functools.partial(spatial_back_body, places), grid=(f,), i...  48.9 us
    pallas_call x1, Pallas kernels, temporal_back(): pl.pallas_call(temporal_back_body, grid=(b,), in_specs=[whole(g.shape), w...  46.9 us
    pallas_call x1, Pallas kernels, mlp_second(): pl.pallas_call(mlp_second_body, grid=(rows // tile, ns), in_specs=[blk] *...  43.8 us
    pallas_call x1, Pallas kernels, mlp_first(): pl.pallas_call(mlp_first_body, grid=(rows // tile, ns), in_specs=[blk, bl...  42.8 us
    pallas_call x1, Pallas kernels, temporal(): pl.pallas_call(temporal_body, grid=(b,), in_specs=[blk, whole(w.shape), w...  32.9 us
    unnamed x181, local copies, waits for them, and re-layouts  30 us
  transfers between devices with their start and end apart: 50, of which 13 were waited for; matrix products, arithmetic and copies ran while one was open for 21% of the time, Pallas kernels for 22%

profile of v2, /device:TPU:0, one launch (start us, length us, event | category | flops | bytes accessed | tf_op | source)
XLA Modules:
  0.0 714.4 jit_solution(17639519664297112649)
XLA Ops:
  0.7 3.6 constant_dynamic-slice_fusion.6
  4.3 3.0 collective-permute-start
  10.6 2.8 broadcast_select_fusion.30
  15.1 2.0 collective-permute-start.9
  19.3 2.2 constant_dynamic-slice_fusion.3
  38.6 9.2 %collective-permute-done.2 = bf16[392,768]{1,0:T(8,128)(2,1)} collective-permute-done((bf16[392,768]{1,0:T(8,128)(2,1)}, bf16[392,768]{1,0:T(8,128)(2,1)}, u32[]{:S(2)}, u32[]{:S(2)}) %collective-permute-start.2) | collective-permute-done | bytes 602144 | tf_op jit(solution)/shard_map/ppermute | solution.py:415
  47.8 2.1 collective-permute-start.15
  49.9 10.8 %collective-permute-done.9 = bf16[392,768]{1,0:T(8,128)(2,1)} collective-permute-done((bf16[392,768]{1,0:T(8,128)(2,1)}, bf16[392,768]{1,0:T(8,128)(2,1)}, u32[]{:S(2)}, u32[]{:S(2)}) %collective-permute-start.9) | collective-permute-done | bytes 602144 | tf_op jit(solution)/shard_map/ppermute | solution.py:415
  60.7 2.0 collective-permute-start.3
  65.8 22.0 %collective-permute-done.10 = bf16[392,768]{1,0:T(8,128)(2,1)S(1)} collective-permute-done((bf16[392,768]{1,0:T(8,128)(2,1)}, bf16[392,768]{1,0:T(8,128)(2,1)S(1)}, u32[]{:S(2)}, u32[]{:S(2)}) %collective-permute-start.10) | collective-permute-done | bytes 602144 | tf_op jit(solution)/shard_map/ppermute | solution.py:418
  89.2 2.1 broadcast_select_fusion.25
  91.3 2.0 broadcast_select_fusion.28
  97.6 15.9 %collective-permute-done.16 = bf16[776,768]{1,0:T(8,128)(2,1)} collective-permute-done((bf16[776,768]{1,0:T(8,128)(2,1)S(1)}, bf16[776,768]{1,0:T(8,128)(2,1)}, u32[]{:S(2)}, u32[]{:S(2)}) %collective-permute-start.16) | collective-permute-done | bytes 1191968 | tf_op jit(solution)/shard_map/ppermute | solution.py:415
  130.4 28.5 %spatial.1 = (f32[8,208,768]{2,1,0:T(8,128)}, bf16[8,208,768]{2,1,0:T(8,128)(2,1)}, bf16[8,208,768]{2,1,0:T(8,128)(2,1)}, bf16[8,208,768]{2,1,0:T(8,128)(2,1)}, ...) custom-call(bf16[8,208,768]{2,1,0:T(8,128)(2,1)} %fusion.4.x, ...), custom_call_target="tpu_custom_call" | custom-call | tf_op jit(solution)/shard_map/spatial/pallas_call | solution.py:136
  158.9 1.9 constant_dynamic-slice_fusion.5
  180.0 32.9 %temporal.1 = (bf16[13,128,768]{2,1,0:T(8,128)(2,1)}, bf16[13,128,768]{2,1,0:T(8,128)(2,1)}, bf16[13,128,768]{2,1,0:T(8,128)(2,1)}, bf16[13,128,768]{2,1,0:T(8,128)(2,1)}, f32[13,3,512]{2,1,0:T(4,128)}) custom-call(bf16[13,128,768]{2,1,0:T(8,128)(2,1)} %copy_bitcast_fusion.3.n1.n, bf16[2304,768]{1,0:T(8,128)(2,1)} %get-tuple-element.294.w, ...), custom_call_target="tpu_custom_call" | custom-call | tf_op jit(solution)/shard_map/temporal/pallas_call | solution.py:161
  212.9 1.9 copy_bitcast_fusion.2
  225.6 42.8 %mlp_first.1 = (f32[1664,768]{1,0:T(8,128)}, bf16[1664,768]{1,0:T(8,128)(2,1)}, f32[1664,768]{1,0:T(8,128)}, f32[1664,768]{1,0:T(8,128)}, bf16[2,768,768]{2,1,0:...) custom-call(f32[1664,768]{1,0:T(8,128)} %bitcast.387, bf16[1664,768]{1,0:T(8,128)(2,1)} %bitcast.390, ...), custom_call_target="tpu_custom_call" | custom-call | tf_op jit(solution)/shard_map/mlp_first/pallas_call | solution.py:327
  268.4 43.8 %mlp_second.1 = (f32[1664,768]{1,0:T(8,128)}, f32[1664,768]{1,0:T(8,128)}, bf16[1664,768]{1,0:T(8,128)(2,1)}, bf16[2,768,768]{2,1,0:T(8,128)(2,1)}, bf16[2,768,7...) custom-call(f32[1664,768]{1,0:T(8,128)} %get-tuple-element.49.s2, ...), custom_call_target="tpu_custom_call" | custom-call | tf_op jit(solution)/shard_map/mlp_second/pallas_call | solution.py:384
  312.2 2.0 constant_dynamic-slice_fusion.1
  321.8 3.6 slice_bitcast_fusion.76
  327.0 46.9 %temporal_back.1 = (bf16[13,128,768]{2,1,0:T(8,128)(2,1)}, bf16[2304,768]{1,0:T(8,128)(2,1)}, bf16[768,768]{1,0:T(8,128)(2,1)}, f32[8,768]{1,0:T(8,128)}) custom-call(bf16[13,128,768]{2,1,0:T(8,128)(2,1)} %copy_bitcast_fusion.1.g, bf16[13,128,768]{2,1,0:T(8,128)(2,1)} %copy_bitcast_fusion.3.n1.n, bf16[13,128,768]{2,1,0:T(8,128)(2,1)} %get-tuple-element.55.q, ...), custom_call_target="tpu_custom_call" | custom-call | tf_op jit(solution)/shard_map/temporal_back/pallas_call | solution.py:201
  374.7 2.0 fusion.50
  376.8 3.5 fusion.37
  385.7 2.3 slice_add_fusion.1
  392.7 48.9 %spatial_back.1 = (f32[8,208,768]{2,1,0:T(8,128)}, bf16[2304,768]{1,0:T(8,128)(2,1)}, bf16[768,768]{1,0:T(8,128)(2,1)}, f32[8,768]{1,0:T(8,128)}) custom-call(bf16[8,208,768]{2,1,0:T(8,128)(2,1)} %fusion.4.x, f32[8,208,768]{2,1,0:T(8,128)} %get-tuple-element.46.s1, bf16[8,208,768]{2,1,0:T(8,128)(2,1)} %pad_maximum_fusion.3.dn1, f32[8,208,768]{2,1,0:T(8,128)} %bitcast.391, ...), custom_call_target="tpu_custom_call" | custom-call | tf_op jit(solution)/shard_map/spatial_back/pallas_call | solution.py:262
  442.5 2.2 fusion.51
  444.6 3.4 fusion.38
  452.6 2.4 fusion.15
  466.8 4.9 collective-permute-done.39
  471.8 2.2 fusion.18
  475.7 29.5 %collective-permute-done.45 = bf16[2,776,768]{2,1,0:T(8,128)(2,1)S(1)} collective-permute-done((bf16[2,776,768]{2,1,0:T(8,128)(2,1)}, bf16[2,776,768]{2,1,0:T(8,128)(2,1)S(1)}, u32[]{:S(2)}, u32[]{:S(2)}) %collective-permute-start.45) | collective-permute-done | bytes 2383904 | tf_op jit(solution)/shard_map/ppermute | solution.py:418
  506.0 1.9 fusion.10
  510.3 20.7 %collective-permute-done.28 = bf16[2,392,768]{2,1,0:T(8,128)(2,1)} collective-permute-done((bf16[2,392,768]{2,1,0:T(8,128)(2,1)}, bf16[2,392,768]{2,1,0:T(8,128)(2,1)}, u32[]{:S(2)}, u32[]{:S(2)}) %collective-permute-start.28) | collective-permute-done | bytes 1204256 | tf_op jit(solution)/shard_map/ppermute | solution.py:418
  531.0 1.9 collective-permute-start.41
  536.0 2.1 fusion.6
  539.0 4.1 copy.60
  543.1 28.8 %collective-permute-done.32 = bf16[16,768]{1,0:T(8,128)(2,1)S(1)} collective-permute-done((bf16[16,768]{1,0:T(8,128)(2,1)S(1)}, bf16[16,768]{1,0:T(8,128)(2,1)S(1)}, u32[]{:S(2)}, u32[]{:S(2)}) %collective-permute-start.32) | collective-permute-done | bytes 24608 | tf_op jit(solution)/shard_map/ppermute | solution.py:415
  576.3 2.2 fusion.13
  579.6 2.1 fusion.8
  582.1 4.1 copy.61
  586.3 12.3 %collective-permute-done.33 = bf16[408,768]{1,0:T(8,128)(2,1)S(1)} collective-permute-done((bf16[408,768]{1,0:T(8,128)(2,1)S(1)}, bf16[408,768]{1,0:T(8,128)(2,1)S(1)}, u32[]{:S(2)}, u32[]{:S(2)}) %collective-permute-start.33) | collective-permute-done | bytes 626720 | tf_op jit(solution)/shard_map/ppermute | solution.py:418
  600.4 27.4 %collective-permute-done.47 = bf16[776,768]{1,0:T(8,128)(2,1)S(1)} collective-permute-done((bf16[776,768]{1,0:T(8,128)(2,1)S(1)}, bf16[776,768]{1,0:T(8,128)(2,1)S(1)}, u32[]{:S(2)}, u32[]{:S(2)}) %collective-permute-start.47) | collective-permute-done | bytes 1191968 | tf_op jit(solution)/shard_map/ppermute | solution.py:418
  632.8 9.8 %collective-permute-done.35 = bf16[392,768]{1,0:T(8,128)(2,1)S(1)} collective-permute-done((bf16[392,768]{1,0:T(8,128)(2,1)S(1)}, bf16[392,768]{1,0:T(8,128)(2,1)S(1)}, u32[]{:S(2)}, u32[]{:S(2)}) %collective-permute-start.35) | collective-permute-done | bytes 602144 | tf_op jit(solution)/shard_map/ppermute | solution.py:418
  642.7 38.1 %collective-permute-done.48 = bf16[776,768]{1,0:T(8,128)(2,1)S(1)} collective-permute-done((bf16[776,768]{1,0:T(8,128)(2,1)S(1)}, bf16[776,768]{1,0:T(8,128)(2,1)S(1)}, u32[]{:S(2)}, u32[]{:S(2)}) %collective-permute-start.48) | collective-permute-done | bytes 1191968 | tf_op jit(solution)/shard_map/ppermute | solution.py:418
  683.8 2.0 maximum_convert_fusion
  685.9 23.5 %collective-permute-done.49 = bf16[776,768]{1,0:T(8,128)(2,1)S(1)} collective-permute-done((bf16[776,768]{1,0:T(8,128)(2,1)S(1)}, bf16[776,768]{1,0:T(8,128)(2,1)S(1)}, u32[]{:S(2)}, u32[]{:S(2)}) %collective-permute-start.49) | collective-permute-done | bytes 1191968 | tf_op jit(solution)/shard_map/ppermute | solution.py:418
  710.1 2.0 copy.62
  (477 shorter events, 143.8 us)
Async XLA Ops:
  4.3 89.0 %collective-permute-start = (bf16[4,196,768]{2,0,1:T(4,128)(2,1)}, bf16[4,196,768]{2,0,1:T(4,128)(2,1)}, u32[]{:S(2)}, u32[]{:S(2)}) collective-permute-start(bf16[4,196,768]{2,0,1:T(4,128)(2,1)} %get-tuple-element.171), channel_id=1, source_target_pairs={{0,2},{1,3},{2,0},{3,1},{4,6},{5,7},{6,4},{7,5},{8,10},{9,11},{10,... | collective-permute-start | bytes 3612680 | tf_op jit(solution)/shard_map/ppermute | solution.py:415
  13.4 34.4 %collective-permute-start.2 = (bf16[392,768]{1,0:T(8,128)(2,1)}, bf16[392,768]{1,0:T(8,128)(2,1)}, u32[]{:S(2)}, u32[]{:S(2)}) collective-permute-start(bf16[392,768]{1,0:T(8,128)(2,1)} %get-tuple-element.279), channel_id=1, source_target_pairs={{0,2},{1,3},{2,0},{3,1},{4,6},{5,7},{6,4},{7,5},{8,10},{9,11},{10,... | collective-permute-start | bytes 1806344 | tf_op jit(solution)/shard_map/ppermute | solution.py:415
  15.1 19.5 %collective-permute-start.8 = (bf16[392,768]{1,0:T(8,128)(2,1)}, bf16[392,768]{1,0:T(8,128)(2,1)}, u32[]{:S(2)}, u32[]{:S(2)}) collective-permute-start(bf16[392,768]{1,0:T(8,128)(2,1)} %get-tuple-element.278), channel_id=1, source_target_pairs={{0,1},{1,0},{2,3},{3,2},{4,5},{5,4},{6,7},{7,6},{8,9},{9,8},{10,11... | collective-permute-start | bytes 1806344 | tf_op jit(solution)/shard_map/ppermute | solution.py:415
  15.1 45.6 %collective-permute-start.9 = (bf16[392,768]{1,0:T(8,128)(2,1)}, bf16[392,768]{1,0:T(8,128)(2,1)}, u32[]{:S(2)}, u32[]{:S(2)}) collective-permute-start(bf16[392,768]{1,0:T(8,128)(2,1)} %get-tuple-element.277), channel_id=1, source_target_pairs={{0,2},{1,3},{2,0},{3,1},{4,6},{5,7},{6,4},{7,5},{8,10},{9,11},{10,... | collective-permute-start | bytes 1806344 | tf_op jit(solution)/shard_map/ppermute | solution.py:415
  17.1 16.3 %collective-permute-start.1 = (bf16[392,768]{1,0:T(8,128)(2,1)}, bf16[392,768]{1,0:T(8,128)(2,1)}, u32[]{:S(2)}, u32[]{:S(2)}) collective-permute-start(bf16[392,768]{1,0:T(8,128)(2,1)} %get-tuple-element.280), channel_id=1, source_target_pairs={{0,1},{1,0},{2,3},{3,2},{4,5},{5,4},{6,7},{7,6},{8,9},{9,8},{10,11... | collective-permute-start | bytes 1806344 | tf_op jit(solution)/shard_map/ppermute | solution.py:415
  34.6 28.1 %collective-permute-start.20 = (bf16[776,768]{1,0:T(8,128)(2,1)S(1)}, bf16[776,768]{1,0:T(8,128)(2,1)S(1)}, u32[]{:S(2)}, u32[]{:S(2)}) collective-permute-start(bf16[776,768]{1,0:T(8,128)(2,1)S(1)} %get-tuple-element.244), channel_id=1, source_target_pairs={{0,1},{1,0},{2,3},{3,2},{4,5},{5,4},{6,7},{7,6},{8,9},{9,8},{10,11... | collective-permute-start | bytes 3575816 | tf_op jit(solution)/shard_map/ppermute | solution.py:415
  38.3 86.6 %collective-permute-start.5 = (bf16[392,768]{1,0:T(8,128)(2,1)}, bf16[392,768]{1,0:T(8,128)(2,1)}, u32[]{:S(2)}, u32[]{:S(2)}) collective-permute-start(bf16[392,768]{1,0:T(8,128)(2,1)} %get-tuple-element.302), channel_id=1, source_target_pairs={{0,1},{1,0},{2,3},{3,2},{4,5},{5,4},{6,7},{7,6},{8,9},{9,8},{10,11... | collective-permute-start | bytes 1806344 | tf_op jit(solution)/shard_map/ppermute | solution.py:415
  47.8 65.7 %collective-permute-start.15 = (bf16[4,196,768]{2,0,1:T(4,128)(2,1)S(1)}, bf16[4,196,768]{2,0,1:T(4,128)(2,1)S(1)}, u32[]{:S(2)}, u32[]{:S(2)}) collective-permute-start(bf16[4,196,768]{2,0,1:T(4,128)(2,1)S(1)} %copy-done.43), channel_id=1, source_target_pairs={{0,2},{1,3},{2,0},{3,1},{4,6},{5,7},{6,4},{7,5},{8,10},{9,11},{10,... | collective-permute-start | bytes 3612680 | tf_op jit(solution)/shard_map/ppermute | solution.py:415
  60.7 30.6 %collective-permute-start.3 = (bf16[392,768]{1,0:T(8,128)(2,1)}, bf16[392,768]{1,0:T(8,128)(2,1)S(1)}, u32[]{:S(2)}, u32[]{:S(2)}) collective-permute-start(bf16[392,768]{1,0:T(8,128)(2,1)} %collective-permute-done.2), channel_id=1, source_target_pairs={{0,4},{4,0},{8,12},{12,8},{16,20},{20,16},{24,28},{28,24},{1,5},{5... | collective-permute-start | bytes 1806344 | tf_op jit(solution)/shard_map/ppermute | solution.py:418
  62.8 25.0 %collective-permute-start.10 = (bf16[392,768]{1,0:T(8,128)(2,1)}, bf16[392,768]{1,0:T(8,128)(2,1)S(1)}, u32[]{:S(2)}, u32[]{:S(2)}) collective-permute-start(bf16[392,768]{1,0:T(8,128)(2,1)} %collective-permute-done.9), channel_id=1, source_target_pairs={{0,4},{4,0},{8,12},{12,8},{16,20},{20,16},{24,28},{28,24},{1,5},{5... | collective-permute-start | bytes 1806344 | tf_op jit(solution)/shard_map/ppermute | solution.py:418
  87.8 25.8 %collective-permute-start.16 = (bf16[776,768]{1,0:T(8,128)(2,1)S(1)}, bf16[776,768]{1,0:T(8,128)(2,1)}, u32[]{:S(2)}, u32[]{:S(2)}) collective-permute-start(bf16[776,768]{1,0:T(8,128)(2,1)S(1)} %get-tuple-element.242), channel_id=1, source_target_pairs={{0,2},{1,3},{2,0},{3,1},{4,6},{5,7},{6,4},{7,5},{8,10},{9,11},{10,... | collective-permute-start | bytes 3575816 | tf_op jit(solution)/shard_map/ppermute | solution.py:415
  91.3 24.8 %collective-permute-start.11 = (bf16[392,768]{1,0:T(8,128)(2,1)S(1)}, bf16[392,768]{1,0:T(8,128)(2,1)S(1)}, u32[]{:S(2)}, u32[]{:S(2)}) collective-permute-start(bf16[392,768]{1,0:T(8,128)(2,1)S(1)} %get-tuple-element.239), channel_id=1, source_target_pairs={{0,1},{1,0},{2,3},{3,2},{4,5},{5,4},{6,7},{7,6},{8,9},{9,8},{10,11... | collective-permute-start | bytes 1806344 | tf_op jit(solution)/shard_map/ppermute | solution.py:415
  93.3 23.0 %collective-permute-start.4 = (bf16[392,768]{1,0:T(8,128)(2,1)S(1)}, bf16[392,768]{1,0:T(8,128)(2,1)S(1)}, u32[]{:S(2)}, u32[]{:S(2)}) collective-permute-start(bf16[392,768]{1,0:T(8,128)(2,1)S(1)} %get-tuple-element.241), channel_id=1, source_target_pairs={{0,1},{1,0},{2,3},{3,2},{4,5},{5,4},{6,7},{7,6},{8,9},{9,8},{10,11... | collective-permute-start | bytes 1806344 | tf_op jit(solution)/shard_map/ppermute | solution.py:415
  113.5 49.2 %collective-permute-start.12 = (bf16[392,768]{1,0:T(8,128)(2,1)}, bf16[392,768]{1,0:T(8,128)(2,1)}, u32[]{:S(2)}, u32[]{:S(2)}) collective-permute-start(bf16[392,768]{1,0:T(8,128)(2,1)} %get-tuple-element.301), channel_id=1, source_target_pairs={{0,1},{1,0},{2,3},{3,2},{4,5},{5,4},{6,7},{7,6},{8,9},{9,8},{10,11... | collective-permute-start | bytes 1806344 | tf_op jit(solution)/shard_map/ppermute | solution.py:415
  113.5 55.8 %collective-permute-start.17 = (bf16[776,768]{1,0:T(8,128)(2,1)}, bf16[776,768]{1,0:T(8,128)(2,1)}, u32[]{:S(2)}, u32[]{:S(2)}) collective-permute-start(bf16[776,768]{1,0:T(8,128)(2,1)} %collective-permute-done.16), channel_id=1, source_target_pairs={{0,4},{4,0},{8,12},{12,8},{16,20},{20,16},{24,28},{28,24},{1,5},{5... | collective-permute-start | bytes 3575816 | tf_op jit(solution)/shard_map/ppermute | solution.py:418
  116.1 11.0 %collective-permute-start.6 = (bf16[392,768]{1,0:T(8,128)(2,1)}, bf16[392,768]{1,0:T(8,128)(2,1)}, u32[]{:S(2)}, u32[]{:S(2)}) collective-permute-start(bf16[392,768]{1,0:T(8,128)(2,1)} %get-tuple-element.240), channel_id=1, source_target_pairs={{0,1},{1,0},{2,3},{3,2},{4,5},{5,4},{6,7},{7,6},{8,9},{9,8},{10,11... | collective-permute-start | bytes 1806344 | tf_op jit(solution)/shard_map/ppermute | solution.py:415
  116.4 50.0 %collective-permute-start.13 = (bf16[392,768]{1,0:T(8,128)(2,1)}, bf16[392,768]{1,0:T(8,128)(2,1)}, u32[]{:S(2)}, u32[]{:S(2)}) collective-permute-start(bf16[392,768]{1,0:T(8,128)(2,1)} %get-tuple-element.238), channel_id=1, source_target_pairs={{0,1},{1,0},{2,3},{3,2},{4,5},{5,4},{6,7},{7,6},{8,9},{9,8},{10,11... | collective-permute-start | bytes 1806344 | tf_op jit(solution)/shard_map/ppermute | solution.py:415
  160.8 17.5 %collective-permute-start.7 = (bf16[8,104,768]{2,1,0:T(8,128)(2,1)S(1)}, bf16[8,104,768]{2,1,0:T(8,128)(2,1)S(1)}, u32[]{:S(2)}, u32[]{:S(2)}) collective-permute-start(bf16[8,104,768]{2,1,0:T(8,128)(2,1)S(1)} %get-tuple-element.167), channel_id=1, source_target_pairs={{0,1},{1,0},{2,3},{3,2},{4,5},{5,4},{6,7},{7,6},{8,9},{9,8},{10,11... | collective-permute-start | bytes 3833864 | tf_op jit(solution)/shard_map/ppermute | solution.py:415
  171.1 44.2 %collective-permute-start.19 = (bf16[776,768]{1,0:T(8,128)(2,1)S(1)}, bf16[776,768]{1,0:T(8,128)(2,1)S(1)}, u32[]{:S(2)}, u32[]{:S(2)}) collective-permute-start(bf16[776,768]{1,0:T(8,128)(2,1)S(1)} %get-tuple-element.181), channel_id=1, source_target_pairs={{0,1},{1,0},{2,3},{3,2},{4,5},{5,4},{6,7},{7,6},{8,9},{9,8},{10,11... | collective-permute-start | bytes 3575816 | tf_op jit(solution)/shard_map/ppermute | solution.py:415
  171.5 43.8 %collective-permute-start.18 = (bf16[776,768]{1,0:T(8,128)(2,1)S(1)}, bf16[776,768]{1,0:T(8,128)(2,1)}, u32[]{:S(2)}, u32[]{:S(2)}) collective-permute-start(bf16[776,768]{1,0:T(8,128)(2,1)S(1)} %get-tuple-element.180), channel_id=1, source_target_pairs={{0,1},{1,0},{2,3},{3,2},{4,5},{5,4},{6,7},{7,6},{8,9},{9,8},{10,11... | collective-permute-start | bytes 3575816 | tf_op jit(solution)/shard_map/ppermute | solution.py:415
  214.9 7.8 %collective-permute-start.14 = (bf16[8,104,768]{2,1,0:T(8,128)(2,1)S(1)}, bf16[8,104,768]{2,1,0:T(8,128)(2,1)S(1)}, u32[]{:S(2)}, u32[]{:S(2)}) collective-permute-start(bf16[8,104,768]{2,1,0:T(8,128)(2,1)S(1)} %slice_bitcast_fusion.2), channel_id=1, source_target_pairs={{0,1},{1,0},{2,3},{3,2},{4,5},{5,4},{6,7},{7,6},{8,9},{9,8},{10,11... | collective-permute-start | bytes 3833864 | tf_op jit(solution)/shard_map/ppermute | solution.py:415
  314.3 11.1 %collective-permute-start.23 = (bf16[8,104,768]{2,1,0:T(8,128)(2,1)S(1)}, bf16[8,104,768]{2,1,0:T(8,128)(2,1)S(1)}, u32[]{:S(2)}, u32[]{:S(2)}) collective-permute-start(bf16[8,104,768]{2,1,0:T(8,128)(2,1)S(1)} %get-tuple-element.165), channel_id=1, source_target_pairs={{0,1},{1,0},{2,3},{3,2},{4,5},{5,4},{6,7},{7,6},{8,9},{9,8},{10,11... | collective-permute-start | bytes 3833864 | tf_op jit(solution)/shard_map/ppermute | solution.py:415
  318.3 66.0 %collective-permute-start.44 = (bf16[2,776,768]{2,1,0:T(8,128)(2,1)}, bf16[2,776,768]{2,1,0:T(8,128)(2,1)S(1)}, u32[]{:S(2)}, u32[]{:S(2)}) collective-permute-start(bf16[2,776,768]{2,1,0:T(8,128)(2,1)} %pad_maximum_fusion.5), channel_id=1, source_target_pairs={{0,1},{1,0},{2,3},{3,2},{4,5},{5,4},{6,7},{7,6},{8,9},{9,8},{10,11... | collective-permute-start | bytes 7151624 | tf_op jit(solution)/shard_map/ppermute | solution.py:415
  320.2 145.4 %collective-permute-start.43 = (bf16[2,776,768]{2,1,0:T(8,128)(2,1)}, bf16[2,776,768]{2,1,0:T(8,128)(2,1)}, u32[]{:S(2)}, u32[]{:S(2)}) collective-permute-start(bf16[2,776,768]{2,1,0:T(8,128)(2,1)} %pad_maximum_fusion.4), channel_id=1, source_target_pairs={{0,1},{1,0},{2,3},{3,2},{4,5},{5,4},{6,7},{7,6},{8,9},{9,8},{10,11... | collective-permute-start | bytes 7151624 | tf_op jit(solution)/shard_map/ppermute | solution.py:415
  380.9 7.1 collective-permute-start.37
  382.5 8.4 %collective-permute-start.24 = (bf16[8,104,768]{2,1,0:T(8,128)(2,1)S(1)}, bf16[8,104,768]{2,1,0:T(8,128)(2,1)S(1)}, u32[]{:S(2)}, u32[]{:S(2)}) collective-permute-start(bf16[8,104,768]{2,1,0:T(8,128)(2,1)S(1)} %slice_bitcast_fusion), channel_id=1, source_target_pairs={{0,1},{1,0},{2,3},{3,2},{4,5},{5,4},{6,7},{7,6},{8,9},{9,8},{10,11... | collective-permute-start | bytes 3833864 | tf_op jit(solution)/shard_map/ppermute | solution.py:415
  384.0 68.3 %collective-permute-start.36 = (bf16[2,392,768]{2,1,0:T(8,128)(2,1)}, bf16[2,392,768]{2,1,0:T(8,128)(2,1)}, u32[]{:S(2)}, u32[]{:S(2)}) collective-permute-start(bf16[2,392,768]{2,1,0:T(8,128)(2,1)} %pad_maximum_fusion.17), channel_id=1, source_target_pairs={{0,1},{1,0},{2,3},{3,2},{4,5},{5,4},{6,7},{7,6},{8,9},{9,8},{10,11... | collective-permute-start | bytes 3612680 | tf_op jit(solution)/shard_map/ppermute | solution.py:415
  389.6 63.0 %collective-permute-start.38 = (bf16[2,392,768]{2,1,0:T(8,128)(2,1)}, bf16[2,392,768]{2,1,0:T(8,128)(2,1)}, u32[]{:S(2)}, u32[]{:S(2)}) collective-permute-start(bf16[2,392,768]{2,1,0:T(8,128)(2,1)} %pad_maximum_fusion.19), channel_id=1, source_target_pairs={{0,4},{4,0},{8,12},{12,8},{16,20},{20,16},{24,28},{28,24},{1,5},{5... | collective-permute-start | bytes 3612680 | tf_op jit(solution)/shard_map/ppermute | solution.py:418
  448.7 7.8 %collective-permute-start.27 = (bf16[2,392,768]{2,1,0:T(8,128)(2,1)S(1)}, bf16[2,392,768]{2,1,0:T(8,128)(2,1)S(1)}, u32[]{:S(2)}, u32[]{:S(2)}) collective-permute-start(bf16[2,392,768]{2,1,0:T(8,128)(2,1)S(1)} %pad_maximum_fusion.15), channel_id=1, source_target_pairs={{0,1},{1,0},{2,3},{3,2},{4,5},{5,4},{6,7},{7,6},{8,9},{9,8},{10,11... | collective-permute-start | bytes 3612680 | tf_op jit(solution)/shard_map/ppermute | solution.py:415
  450.4 54.8 %collective-permute-start.45 = (bf16[2,776,768]{2,1,0:T(8,128)(2,1)}, bf16[2,776,768]{2,1,0:T(8,128)(2,1)S(1)}, u32[]{:S(2)}, u32[]{:S(2)}) collective-permute-start(bf16[2,776,768]{2,1,0:T(8,128)(2,1)} %pad_maximum_fusion.6), channel_id=1, source_target_pairs={{0,4},{4,0},{8,12},{12,8},{16,20},{20,16},{24,28},{28,24},{1,5},{5... | collective-permute-start | bytes 7151624 | tf_op jit(solution)/shard_map/ppermute | solution.py:418
  452.4 57.3 %collective-permute-start.26 = (bf16[2,392,768]{2,1,0:T(8,128)(2,1)}, bf16[2,392,768]{2,1,0:T(8,128)(2,1)}, u32[]{:S(2)}, u32[]{:S(2)}) collective-permute-start(bf16[2,392,768]{2,1,0:T(8,128)(2,1)} %pad_maximum_fusion.14), channel_id=1, source_target_pairs={{0,1},{1,0},{2,3},{3,2},{4,5},{5,4},{6,7},{7,6},{8,9},{9,8},{10,11... | collective-permute-start | bytes 3612680 | tf_op jit(solution)/shard_map/ppermute | solution.py:415
  455.0 16.7 %collective-permute-start.39 = (bf16[392,768]{1,0:T(8,128)(2,1)}, bf16[392,768]{1,0:T(8,128)(2,1)}, u32[]{:S(2)}, u32[]{:S(2)}) collective-permute-start(bf16[392,768]{1,0:T(8,128)(2,1)} %fusion.15), channel_id=1, source_target_pairs={{0,2},{1,3},{2,0},{3,1},{4,6},{5,7},{6,4},{7,5},{8,10},{9,11},{10,... | collective-permute-start | bytes 1806344 | tf_op jit(solution)/shard_map/ppermute | solution.py:415
  458.1 72.9 %collective-permute-start.28 = (bf16[2,392,768]{2,1,0:T(8,128)(2,1)}, bf16[2,392,768]{2,1,0:T(8,128)(2,1)}, u32[]{:S(2)}, u32[]{:S(2)}) collective-permute-start(bf16[2,392,768]{2,1,0:T(8,128)(2,1)} %pad_maximum_fusion.16), channel_id=1, source_target_pairs={{0,4},{4,0},{8,12},{12,8},{16,20},{20,16},{24,28},{28,24},{1,5},{5... | collective-permute-start | bytes 3612680 | tf_op jit(solution)/shard_map/ppermute | solution.py:418
  465.5 68.9 %collective-permute-start.22 = (bf16[4,196,768]{2,0,1:T(4,128)(2,1)}, bf16[4,196,768]{2,0,1:T(4,128)(2,1)S(1)}, u32[]{:S(2)}, u32[]{:S(2)}) collective-permute-start(bf16[4,196,768]{2,0,1:T(4,128)(2,1)} %copy.54), channel_id=1, source_target_pairs={{0,2},{1,3},{2,0},{3,1},{4,6},{5,7},{6,4},{7,5},{8,10},{9,11},{10,... | collective-permute-start | bytes 3612680 | tf_op jit(solution)/shard_map/ppermute | solution.py:415
  474.0 34.0 %collective-permute-start.40 = (bf16[392,768]{1,0:T(8,128)(2,1)S(1)}, bf16[392,768]{1,0:T(8,128)(2,1)S(1)}, u32[]{:S(2)}, u32[]{:S(2)}) collective-permute-start(bf16[392,768]{1,0:T(8,128)(2,1)S(1)} %fusion.18), channel_id=1, source_target_pairs={{0,8},{4,12},{8,0},{12,4},{16,24},{20,28},{24,16},{28,20},{1,9},{5... | collective-permute-start | bytes 1806344 | tf_op jit(solution)/shard_map/ppermute | solution.py:418
  505.2 74.5 %collective-permute-start.25 = (bf16[4,196,768]{2,0,1:T(4,128)(2,1)S(1)}, bf16[4,196,768]{2,0,1:T(4,128)(2,1)S(1)}, u32[]{:S(2)}, u32[]{:S(2)}) collective-permute-start(bf16[4,196,768]{2,0,1:T(4,128)(2,1)S(1)} %copy-done.42), channel_id=1, source_target_pairs={{0,2},{1,3},{2,0},{3,1},{4,6},{5,7},{6,4},{7,5},{8,10},{9,11},{10,... | collective-permute-start | bytes 3612680 | tf_op jit(solution)/shard_map/ppermute | solution.py:415
  508.0 30.1 %collective-permute-start.31 = (bf16[16,768]{1,0:T(8,128)(2,1)S(1)}, bf16[16,768]{1,0:T(8,128)(2,1)S(1)}, u32[]{:S(2)}, u32[]{:S(2)}) collective-permute-start(bf16[16,768]{1,0:T(8,128)(2,1)S(1)} %pad_add_fusion), channel_id=1, source_target_pairs={{0,4},{4,0},{8,12},{12,8},{16,20},{20,16},{24,28},{28,24},{1,5},{5... | collective-permute-start | bytes 73736 | tf_op jit(solution)/shard_map/ppermute | solution.py:418
  509.7 66.6 %collective-permute-start.46 = (bf16[776,768]{1,0:T(8,128)(2,1)S(1)}, bf16[776,768]{1,0:T(8,128)(2,1)S(1)}, u32[]{:S(2)}, u32[]{:S(2)}) collective-permute-start(bf16[776,768]{1,0:T(8,128)(2,1)S(1)} %fusion.10), channel_id=1, source_target_pairs={{0,2},{1,3},{2,0},{3,1},{4,6},{5,7},{6,4},{7,5},{8,10},{9,11},{10,... | collective-permute-start | bytes 3575816 | tf_op jit(solution)/shard_map/ppermute | solution.py:415
  531.0 40.9 %collective-permute-start.41 = (bf16[392,768]{1,0:T(8,128)(2,1)S(1)}, bf16[392,768]{1,0:T(8,128)(2,1)S(1)}, u32[]{:S(2)}, u32[]{:S(2)}) collective-permute-start(bf16[392,768]{1,0:T(8,128)(2,1)S(1)} %add.315), channel_id=1, source_target_pairs={{0,16},{4,20},{8,24},{12,28},{16,0},{20,4},{24,8},{28,12},{1,17},{... | collective-permute-start | bytes 1806344 | tf_op jit(solution)/shard_map/ppermute | solution.py:418
  534.4 38.5 %collective-permute-start.29 = (bf16[392,768]{1,0:T(8,128)(2,1)S(1)}, bf16[392,768]{1,0:T(8,128)(2,1)S(1)}, u32[]{:S(2)}, u32[]{:S(2)}) collective-permute-start(bf16[392,768]{1,0:T(8,128)(2,1)S(1)} %fusion.20), channel_id=1, source_target_pairs={{0,2},{1,3},{2,0},{3,1},{4,6},{5,7},{6,4},{7,5},{8,10},{9,11},{10,... | collective-permute-start | bytes 1806344 | tf_op jit(solution)/shard_map/ppermute | solution.py:415
  538.1 33.8 %collective-permute-start.32 = (bf16[16,768]{1,0:T(8,128)(2,1)S(1)}, bf16[16,768]{1,0:T(8,128)(2,1)S(1)}, u32[]{:S(2)}, u32[]{:S(2)}) collective-permute-start(bf16[16,768]{1,0:T(8,128)(2,1)S(1)} %add.304), channel_id=1, source_target_pairs={{0,2},{1,3},{2,0},{3,1},{4,6},{5,7},{6,4},{7,5},{8,10},{9,11},{10,... | collective-permute-start | bytes 73736 | tf_op jit(solution)/shard_map/ppermute | solution.py:415
  572.1 14.1 %collective-permute-start.42 = (bf16[392,768]{1,0:T(8,128)(2,1)S(1)}, bf16[392,768]{1,0:T(8,128)(2,1)S(1)}, u32[]{:S(2)}, u32[]{:S(2)}) collective-permute-start(bf16[392,768]{1,0:T(8,128)(2,1)S(1)} %add.316), channel_id=1, source_target_pairs={{0,4},{4,0},{8,12},{12,8},{16,20},{20,16},{24,28},{28,24},{1,5},{5... | collective-permute-start | bytes 1806344 | tf_op jit(solution)/shard_map/ppermute | solution.py:418
  574.7 23.8 %collective-permute-start.33 = (bf16[408,768]{1,0:T(8,128)(2,1)S(1)}, bf16[408,768]{1,0:T(8,128)(2,1)S(1)}, u32[]{:S(2)}, u32[]{:S(2)}) collective-permute-start(bf16[408,768]{1,0:T(8,128)(2,1)S(1)} %pad_maximum_fusion.28), channel_id=1, source_target_pairs={{0,8},{4,12},{8,0},{12,4},{16,24},{20,28},{24,16},{28,20},{1,9},{5... | collective-permute-start | bytes 1880072 | tf_op jit(solution)/shard_map/ppermute | solution.py:418
  578.5 49.4 %collective-permute-start.47 = (bf16[776,768]{1,0:T(8,128)(2,1)S(1)}, bf16[776,768]{1,0:T(8,128)(2,1)S(1)}, u32[]{:S(2)}, u32[]{:S(2)}) collective-permute-start(bf16[776,768]{1,0:T(8,128)(2,1)S(1)} %fusion.13), channel_id=1, source_target_pairs={{0,8},{4,12},{8,0},{12,4},{16,24},{20,28},{24,16},{28,20},{1,9},{5... | collective-permute-start | bytes 3575816 | tf_op jit(solution)/shard_map/ppermute | solution.py:418
  598.7 31.3 %collective-permute-start.34 = (bf16[408,768]{1,0:T(8,128)(2,1)S(1)}, bf16[408,768]{1,0:T(8,128)(2,1)S(1)}, u32[]{:S(2)}, u32[]{:S(2)}) collective-permute-start(bf16[408,768]{1,0:T(8,128)(2,1)S(1)} %fusion.36), channel_id=1, source_target_pairs={{0,16},{4,20},{8,24},{12,28},{16,0},{20,4},{24,8},{28,12},{1,17},{... | collective-permute-start | bytes 1880072 | tf_op jit(solution)/shard_map/ppermute | solution.py:418
  628.2 52.7 %collective-permute-start.48 = (bf16[776,768]{1,0:T(8,128)(2,1)S(1)}, bf16[776,768]{1,0:T(8,128)(2,1)S(1)}, u32[]{:S(2)}, u32[]{:S(2)}) collective-permute-start(bf16[776,768]{1,0:T(8,128)(2,1)S(1)} %add.324), channel_id=1, source_target_pairs={{0,16},{4,20},{8,24},{12,28},{16,0},{20,4},{24,8},{28,12},{1,17},{... | collective-permute-start | bytes 3575816 | tf_op jit(solution)/shard_map/ppermute | solution.py:418
  630.2 12.4 %collective-permute-start.35 = (bf16[392,768]{1,0:T(8,128)(2,1)S(1)}, bf16[392,768]{1,0:T(8,128)(2,1)S(1)}, u32[]{:S(2)}, u32[]{:S(2)}) collective-permute-start(bf16[392,768]{1,0:T(8,128)(2,1)S(1)} %slice.1394), channel_id=1, source_target_pairs={{0,4},{4,0},{8,12},{12,8},{16,20},{20,16},{24,28},{28,24},{1,5},{5... | collective-permute-start | bytes 1806344 | tf_op jit(solution)/shard_map/ppermute | solution.py:418
  681.2 28.2 %collective-permute-start.49 = (bf16[776,768]{1,0:T(8,128)(2,1)S(1)}, bf16[776,768]{1,0:T(8,128)(2,1)S(1)}, u32[]{:S(2)}, u32[]{:S(2)}) collective-permute-start(bf16[776,768]{1,0:T(8,128)(2,1)S(1)} %add.325), channel_id=1, source_target_pairs={{0,4},{4,0},{8,12},{12,8},{16,20},{20,16},{24,28},{28,24},{1,5},{5... | collective-permute-start | bytes 3575816 | tf_op jit(solution)/shard_map/ppermute | solution.py:418
  (81 other events, 597.1 us)

commit v3 on v2

v3 whole, which is shorter than its diff:
```python
import functools

import jax
import jax.numpy as jnp
from jax import lax
from jax.experimental import pallas as pl
from jax.experimental.pallas import tpu as pltpu
from jax.sharding import PartitionSpec as P

BF = jnp.bfloat16
F32 = jnp.float32
HEAD_DIM = 64
norm_epsilon = 1e-06
LIMIT = 60 << 20


def nn(a, b):
    return lax.dot_general(a, b, (((1,), (0,)), ((), ())), preferred_element_type=F32)


def nt(a, b):
    return lax.dot_general(a, b, (((1,), (1,)), ((), ())), preferred_element_type=F32)


def tn(a, b):
    return lax.dot_general(a, b, (((0,), (0,)), ((), ())), preferred_element_type=F32)


def hat_of(values):
    mean = jnp.mean(values, axis=-1, keepdims=True)
    centered = values - mean
    inv = lax.rsqrt(jnp.mean(centered * centered, axis=-1, keepdims=True) + norm_epsilon)
    return centered * inv, inv


def hat_back(hat, inv, gain, grad):
    e = grad * gain
    return inv * (
        e - jnp.mean(e, axis=-1, keepdims=True) - hat * jnp.mean(e * hat, axis=-1, keepdims=True)
    )


GROUP = 256
PER = GROUP // HEAD_DIM


def head_of_lane(rows):
    return lax.broadcasted_iota(jnp.int32, (rows, GROUP), 1) // HEAD_DIM


def stacked(v):
    lane = head_of_lane(v.shape[0])
    return jnp.concatenate([jnp.where(lane == h, v, jnp.zeros_like(v)) for h in range(PER)])


def unstacked(v):
    rows = v.shape[0] // PER
    lane = head_of_lane(rows)
    out = v[:rows]
    for h in range(1, PER):
        out = jnp.where(lane == h, v[h * rows : (h + 1) * rows], out)
    return out


def only_places(places):
    def mask(s):
        cut = places // 8 * 8
        row = lax.broadcasted_iota(jnp.int32, (s.shape[0] - cut, s.shape[1]), 0)
        return jnp.concatenate([s[:cut], jnp.where(row < places - cut, s[cut:], -1e30)])

    return mask


def same_place(bias):
    return lambda s: s + bias


def place_bias(rows):
    a = lax.broadcasted_iota(jnp.int32, (rows, PER * rows), 0) & 7
    b = lax.broadcasted_iota(jnp.int32, (rows, PER * rows), 1) & 7
    return jnp.where(a == b, 0.0, -1e30).astype(F32)


def attend(q_ref, k_ref, v_ref, o_ref, lse_ref, mask):
    for g in range(o_ref.shape[1] // GROUP):
        at = slice(GROUP * g, GROUP * g + GROUP)
        s = mask(nt(k_ref[:, at], stacked(q_ref[:, at])))
        top = jnp.max(s, axis=0, keepdims=True)
        ex = jnp.exp(s - top)
        total = jnp.sum(ex, axis=0, keepdims=True)
        p = (ex * (1.0 / total)).astype(BF)
        o_ref[:, at] = unstacked(tn(p, v_ref[:, at])).astype(BF)
        lse_ref[g : g + 1] = top + jnp.log(total)


def attend_back(q_ref, k_ref, v_ref, do_ref, lse_ref, dq_ref, dk_ref, dv_ref, mask):
    for g in range(do_ref.shape[1] // GROUP):
        at = slice(GROUP * g, GROUP * g + GROUP)
        qs, dos = stacked(q_ref[:, at]), stacked(do_ref[:, at])
        k = k_ref[:, at]
        p = jnp.exp(mask(nt(k, qs)) - lse_ref[g : g + 1])
        dp = nt(v_ref[:, at], dos)
        ds = (p * (dp - jnp.sum(p * dp, axis=0, keepdims=True))).astype(BF)
        dv_ref[:, at] = nn(p.astype(BF), dos).astype(BF)
        dk_ref[:, at] = nn(ds, qs).astype(BF)
        dq_ref[:, at] = (unstacked(tn(ds, k)) * HEAD_DIM**-0.5).astype(BF)


def whole(shape):
    return pl.BlockSpec(shape, lambda *_: (0,) * len(shape), pipeline_mode=pl.Buffered(1))


def params(n=1):
    return pltpu.CompilerParams(
        dimension_semantics=("arbitrary",) * n, vmem_limit_bytes=LIMIT
    )


def cost(us):
    return pl.CostEstimate(flops=int(us * 1.1e9), bytes_accessed=int(us * 1e5), transcendentals=0)


def spatial_body(places, x, w, wo, vec, *refs):
    stream, n1, q, k, v, o, lse = refs[-7:]
    xv = x[0].astype(F32)
    d = xv.shape[1]
    n0 = (hat_of(xv)[0] * vec[0:1] + vec[1:2]).astype(BF)
    q[0] = ((nt(n0, w[0:d]) + vec[2:3]) * HEAD_DIM**-0.5).astype(BF)
    k[0] = nt(n0, w[d : 2 * d]).astype(BF)
    v[0] = (nt(n0, w[2 * d : 3 * d]) + vec[3:4]).astype(BF)
    attend(q.at[0], k.at[0], v.at[0], o.at[0], lse.at[0], only_places(places))
    s1 = xv + (nn(o[0], wo[...]) + vec[4:5])
    stream[0] = s1
    n1[0] = (hat_of(s1)[0] * vec[5:6] + vec[6:7]).astype(BF)


def spatial(x, w, wo, vec, places, frames, start, before=()):
    f, r, d = x.shape
    blk = pl.BlockSpec((1, r, d), lambda i: (i, 0, 0))
    out = pl.BlockSpec((1, r, d), lambda i: (i + start, 0, 0))
    big = jax.ShapeDtypeStruct((frames, r, d), BF)
    return pl.pallas_call(
        functools.partial(spatial_body, places),
        grid=(f,),
        in_specs=[blk, whole(w.shape), whole(wo.shape), whole(vec.shape)]
        + [pl.BlockSpec(memory_space=pl.ANY)] * len(before),
        out_specs=[out] * 6
        + [pl.BlockSpec((1, d // GROUP, PER * r), lambda i: (i + start, 0, 0))],
        out_shape=[jax.ShapeDtypeStruct((frames, r, d), F32)]
        + [big] * 5
        + [jax.ShapeDtypeStruct((frames, d // GROUP, PER * r), F32)],
        input_output_aliases={4 + i: i for i in range(len(before))},
        compiler_params=params(),
        name="spatial",
        cost_estimate=cost(3.6 * f),
    )(x, w, wo, vec, *before)


def temporal_body(n1, w, vec, q, k, v, o, lse):
    n = n1[0]
    d = n.shape[1]
    q[0] = ((nt(n, w[0:d]) + vec[0:1]) * HEAD_DIM**-0.5).astype(BF)
    k[0] = nt(n, w[d : 2 * d]).astype(BF)
    v[0] = (nt(n, w[2 * d : 3 * d]) + vec[1:2]).astype(BF)
    attend(q.at[0], k.at[0], v.at[0], o.at[0], lse.at[0], same_place(place_bias(n.shape[0])))


def temporal(n1, w, vec):
    b, r, d = n1.shape
    blk = pl.BlockSpec((1, r, d), lambda i: (i, 0, 0))
    return pl.pallas_call(
        temporal_body,
        grid=(b,),
        in_specs=[blk, whole(w.shape), whole(vec.shape)],
        out_specs=[blk] * 4 + [pl.BlockSpec((1, d // GROUP, PER * r), lambda i: (i, 0, 0))],
        out_shape=[jax.ShapeDtypeStruct((b, r, d), BF)] * 4
        + [jax.ShapeDtypeStruct((b, d // GROUP, PER * r), F32)],
        compiler_params=params(),
        name="temporal",
        cost_estimate=cost(2.4 * b),
    )(n1, w, vec)


def temporal_back_body(g, q, k, v, lse, w, wo, dn, dqkv, do):
    i = pl.program_id(0)
    d = g.shape[-1]
    r = q.shape[1]
    do[...] = nt(g[0], wo[...]).astype(BF)
    attend_back(
        q.at[0], k.at[0], v.at[0], do, lse.at[0],
        dqkv.at[0, i], dqkv.at[1, i], dqkv.at[2, i], same_place(place_bias(r)),
    )

    @pl.when(i == pl.num_programs(0) - 1)
    def _():
        rows = dqkv.shape[1] * r
        acc = nn(dqkv[0].reshape(rows, d), w[0:d])
        acc += nn(dqkv[1].reshape(rows, d), w[d : 2 * d])
        acc += nn(dqkv[2].reshape(rows, d), w[2 * d : 3 * d])
        dn[...] = acc.astype(BF).reshape(dn.shape)


def temporal_back(g, q, k, v, lse, w, wo):
    b, r, d = g.shape
    blk = pl.BlockSpec((1, r, d), lambda i: (i, 0, 0))
    return pl.pallas_call(
        temporal_back_body,
        grid=(b,),
        in_specs=[blk] * 4
        + [pl.BlockSpec((1, d // GROUP, PER * r), lambda i: (i, 0, 0)),
           whole(w.shape), whole(wo.shape)],
        out_specs=[whole(g.shape), whole((3, b, r, d))],
        out_shape=[jax.ShapeDtypeStruct(g.shape, BF), jax.ShapeDtypeStruct((3, b, r, d), BF)],
        scratch_shapes=[pltpu.VMEM((r, d), BF)],
        compiler_params=params(),
        name="temporal_back",
        cost_estimate=cost(36),
    )(g, q, k, v, lse, w, wo)


def weight_grads_body(dqkv, o, n, g, send, keep, sums):
    c = pl.program_id(0)
    d = n.shape[1]
    e = d // 4

    def put(m):
        m = m.astype(BF)
        for r in range(4):
            to = send if r % 2 else keep
            to[r // 2, 0] = m[r * e : (r + 1) * e]

    @pl.when(c < 3)
    def _():
        v = dqkv[0]
        put(tn(v, n[...]))
        sums[0] = jnp.sum(v.astype(F32), axis=0, keepdims=True)

    @pl.when(c == 3)
    def _():
        put(tn(o[...], g[...]))
        sums[0] = jnp.zeros_like(sums[0])


def weight_grads(dqkv, o, n, g):
    d = n.shape[-1]
    rows = n.size // d
    dqkv = dqkv.reshape(3, rows, d)
    o, n, g = (v.reshape(rows, d) for v in (o, n, g))
    out = pl.BlockSpec((2, 1, d // 4, d), lambda c: (0, c, 0, 0))
    return pl.pallas_call(
        weight_grads_body,
        grid=(4,),
        in_specs=[pl.BlockSpec((1, rows, d), lambda c: (jnp.minimum(c, 2), 0, 0))]
        + [whole((rows, d))] * 3,
        out_specs=[out, out, pl.BlockSpec((1, 1, d), lambda c: (c, 0, 0))],
        out_shape=[jax.ShapeDtypeStruct((2, 4, d // 4, d), BF)] * 2
        + [jax.ShapeDtypeStruct((4, 1, d), F32)],
        compiler_params=params(),
        name="weight_grads",
        cost_estimate=cost(14),
    )(dqkv, o, n, g)


def spatial_back_body(places, x, s1, dn1, g2, q, k, v, lse, w, wo, vec, *refs):
    g0, sums, dqkv, n0, gb, do = refs[-6:]
    i = pl.program_id(0)
    r, d = x.shape[1:]

    @pl.when(i == 0)
    def _():
        sums[...] = jnp.zeros_like(sums)

    def add(at, val):
        sums[at : at + 1] += jnp.sum(val, axis=0, keepdims=True)

    hat, inv = hat_of(s1[0])
    dn = dn1[0].astype(F32)
    add(2, dn * hat)
    add(3, dn)
    g1 = g2[0] + hat_back(hat, inv, vec[2:3], dn)
    add(4, g1)
    gb[0] = g1.astype(BF)
    do[...] = nt(gb[0], wo[...]).astype(BF)
    attend_back(
        q.at[0], k.at[0], v.at[0], do, lse.at[0],
        dqkv.at[0, 0], dqkv.at[1, 0], dqkv.at[2, 0], only_places(places),
    )
    hat, inv = hat_of(x[0].astype(F32))
    n0[0] = (hat * vec[0:1] + vec[1:2]).astype(BF)
    dn = nn(dqkv[0, 0], w[0:d]) + nn(dqkv[1, 0], w[d : 2 * d]) + nn(dqkv[2, 0], w[2 * d : 3 * d])
    add(0, dn * hat)
    add(1, dn)
    g0[0] = (g1 + hat_back(hat, inv, vec[0:1], dn)).astype(g0.dtype)


def spatial_back(x, s1, dn1, g2, q, k, v, lse, w, wo, vec, places, start, kind, before=()):
    f, r, d = x.shape
    frames = s1.shape[0]
    own = pl.BlockSpec((1, r, d), lambda i: (i, 0, 0))
    blk = pl.BlockSpec((1, r, d), lambda i: (i + start, 0, 0))
    big = jax.ShapeDtypeStruct((frames, r, d), BF)
    return pl.pallas_call(
        functools.partial(spatial_back_body, places),
        grid=(f,),
        in_specs=[own] + [blk] * 6
        + [pl.BlockSpec((1, d // GROUP, PER * r), lambda i: (i + start, 0, 0)),
           whole(w.shape), whole(wo.shape), whole(vec.shape)]
        + [pl.BlockSpec(memory_space=pl.ANY)] * len(before),
        out_specs=[own, whole((8, d)), pl.BlockSpec((3, 1, r, d), lambda i: (0, i + start, 0, 0)),
                   blk, blk],
        out_shape=[jax.ShapeDtypeStruct(x.shape, kind), jax.ShapeDtypeStruct((8, d), F32),
                   jax.ShapeDtypeStruct((3, frames, r, d), BF), big, big],
        input_output_aliases={11 + i: 2 + i for i in range(len(before))},
        scratch_shapes=[pltpu.VMEM((r, d), BF)],
        compiler_params=params(),
        name="spatial_back",
        cost_estimate=cost(5 * f),
    )(x, s1, dn1, g2, q, k, v, lse, w, wo, vec, *before)


def gelu_parts(u):
    cdf = 0.5 + 0.5 * lax.erf(u * 0.7071067811865476)
    return u * cdf, cdf + u * (jnp.exp(-0.5 * u * u) * 0.3989422804014327)


def mlp_step(n2, gb, wt, wd, b, s, branch, dn, gwt, gwd, gbi):
    u = nt(n2, wt[s]) + b[s]
    h, slope = gelu_parts(u)
    h = h.astype(BF)
    branch[...] += nn(h, wd[s])
    dr = (nt(gb, wd[s]) * slope).astype(BF)
    dn[...] += nn(dr, wt[s])
    gwt[s] += tn(dr, n2)
    gwd[s] += tn(h, gb)
    gbi[s] += jnp.sum(dr.astype(F32), axis=0, keepdims=True)


def mlp_ends(i, s, gwt, gwd, gbi, gwt_o, gwd_o):
    @pl.when(i == pl.num_programs(0) - 1)
    def _():
        gwt_o[s] = gwt[s].astype(BF)
        gwd_o[s] = gwd[s].astype(BF)


def mlp_first_body(s1, o1, gb, wo, vec, wt, wd, b, s2, n2, branch, dn, gwt_o, gwd_o, gbi, gwt, gwd):
    i, s = pl.program_id(0), pl.program_id(1)

    @pl.when((i == 0) & (s == 0))
    def _():
        gwt[...] = jnp.zeros_like(gwt)
        gwd[...] = jnp.zeros_like(gwd)
        gbi[...] = jnp.zeros_like(gbi)

    @pl.when(s == 0)
    def _():
        v = s1[...] + (nn(o1[...], wo[...]) + vec[0:1])
        s2[...] = v
        n2[...] = (hat_of(v)[0] * vec[1:2] + vec[2:3]).astype(BF)
        branch[...] = jnp.zeros_like(branch)
        dn[...] = jnp.zeros_like(dn)

    mlp_step(n2[...], gb[...], wt, wd, b, s, branch, dn, gwt, gwd, gbi)
    mlp_ends(i, s, gwt, gwd, gbi, gwt_o, gwd_o)


def mlp_first(s1, o1, gb, wo, vec, wt, wd, b, tile):
    rows, d = s1.shape
    ns, h, _ = wt.shape
    blk = pl.BlockSpec((tile, d), lambda i, s: (i, 0))
    sh = lambda t: jax.ShapeDtypeStruct((rows, d), t)
    return pl.pallas_call(
        mlp_first_body,
        grid=(rows // tile, ns),
        in_specs=[blk, blk, blk, whole(wo.shape), whole(vec.shape), whole(wt.shape),
                  whole(wd.shape), whole(b.shape)],
        out_specs=[blk] * 4 + [whole(wt.shape), whole(wd.shape), whole(b.shape)],
        out_shape=[sh(F32), sh(BF), sh(F32), sh(F32), jax.ShapeDtypeStruct(wt.shape, BF),
                   jax.ShapeDtypeStruct(wd.shape, BF), jax.ShapeDtypeStruct(b.shape, F32)],
        scratch_shapes=[pltpu.VMEM(wt.shape, F32), pltpu.VMEM(wd.shape, F32)],
        compiler_params=params(2),
        name="mlp_first",
        cost_estimate=cost(42),
    )(s1, o1, gb, wo, vec, wt, wd, b)


def mlp_second_body(s2, n2, gb, br0, dn0, vec, wt, wd, b,
                    near, far, g2, g2b, gwt_o, gwd_o, gbi, sums, branch, dn, gwt, gwd):
    i, s = pl.program_id(0), pl.program_id(1)

    @pl.when((i == 0) & (s == 0))
    def _():
        gwt[...] = jnp.zeros_like(gwt)
        gwd[...] = jnp.zeros_like(gwd)
        gbi[...] = jnp.zeros_like(gbi)
        sums[...] = jnp.zeros_like(sums)

    @pl.when(s == 0)
    def _():
        branch[...] = br0[...]
        dn[...] = dn0[...]

    mlp_step(n2[...], gb[...], wt, wd, b, s, branch, dn, gwt, gwd, gbi)
    mlp_ends(i, s, gwt, gwd, gbi, gwt_o, gwd_o)

    @pl.when(s == pl.num_programs(1) - 1)
    def _():
        def add(at, val):
            sums[at : at + 1] += jnp.sum(val, axis=0, keepdims=True)

        v = s2[...]
        out = v + (branch[...] + vec[0:1])

        @pl.when(i < pl.num_programs(0) // 2)
        def _():
            near[...] = out

        @pl.when(i >= pl.num_programs(0) // 2)
        def _():
            far[...] = out.astype(BF)

        hat, inv = hat_of(v)
        dv = dn[...]
        add(0, dv * hat)
        add(1, dv)
        g3 = gb[...].astype(F32)
        add(3, g3)
        g = g3 + hat_back(hat, inv, vec[1:2], dv)
        add(2, g)
        g2[...] = g
        g2b[...] = g.astype(BF)


def mlp_second(s2, n2, gb, br0, dn0, vec, wt, wd, b, tile):
    rows, d = s2.shape
    ns, h, _ = wt.shape
    half = rows // tile // 2
    blk = pl.BlockSpec((tile, d), lambda i, s: (i, 0))
    sh = lambda t, n=rows: jax.ShapeDtypeStruct((n, d), t)
    return pl.pallas_call(
        mlp_second_body,
        grid=(rows // tile, ns),
        in_specs=[blk] * 5 + [whole(vec.shape), whole(wt.shape), whole(wd.shape), whole(b.shape)],
        out_specs=[pl.BlockSpec((tile, d), lambda i, s: (jnp.minimum(i, half - 1), 0)),
                   pl.BlockSpec((tile, d), lambda i, s: (jnp.maximum(i - half, 0), 0)),
                   blk, blk, whole(wt.shape), whole(wd.shape), whole(b.shape), whole((8, d))],
        out_shape=[sh(F32, rows // 2), sh(BF, rows // 2), sh(F32), sh(BF),
                   jax.ShapeDtypeStruct(wt.shape, BF), jax.ShapeDtypeStruct(wd.shape, BF),
                   jax.ShapeDtypeStruct(b.shape, F32), jax.ShapeDtypeStruct((8, d), F32)],
        scratch_shapes=[pltpu.VMEM((tile, d), F32), pltpu.VMEM((tile, d), F32),
                        pltpu.VMEM(wt.shape, F32), pltpu.VMEM(wd.shape, F32)],
        compiler_params=params(2),
        name="mlp_second",
        cost_estimate=cost(42),
    )(s2, n2, gb, br0, dn0, vec, wt, wd, b)


def finish_body(dp, gs, gk, t1, rel, rep, f0, f1, rel_o, rep_o, *scratch):
    (rc, kk, ry, rx, tt, zr, ta, tb, aa, ab, xs, rel_r, rep_r, rel_s, rep_s, send, recv) = scratch
    me_d, me_t = lax.axis_index("dp"), lax.axis_index("tensor")
    x = lax.rem(me_d, 2)
    bits = []
    bit = 2
    while bit < dp:
        bits.append(bit)
        bit *= 2

    def flip(v, b):
        return v + b - 2 * b * lax.rem(v // b, 2)

    def core():
        return (me_d, flip(me_t, 1))

    def over_y():
        return (me_d, flip(me_t, 2))

    def over_d(b):
        return (flip(me_d, b), me_t)

    partners = [core(), over_y(), over_d(1)] + [over_d(b) for b in bits]
    barrier = pltpu.get_barrier_semaphore()
    for p in partners:
        pl.semaphore_signal(barrier, inc=1, device_id=p, device_id_type=pl.DeviceIdType.MESH)
    pl.semaphore_wait(barrier, len(partners))

    count = [0]

    def copy(src, dst, to):
        k = count[0]
        count[0] += 1
        c = pltpu.make_async_remote_copy(
            src_ref=src, dst_ref=dst, send_sem=send.at[k], recv_sem=recv.at[k],
            device_id=to, device_id_type=pl.DeviceIdType.MESH,
        )
        c.start()
        return c

    def plus(a, b):
        return (a.astype(F32) + b.astype(F32)).astype(BF)

    n = tt.shape[1]

    def rest(k, out):
        size, held = n, tt.at[k]
        done = []
        for z, b in enumerate(bits[:2]):
            half = size // 2
            bitv = lax.rem(me_d // b, 2)
            mine = pl.multiple_of(bitv * half, 16)
            other = pl.multiple_of((1 - bitv) * half, 16)
            dst = zr.at[k, z, pl.ds(0, half)]
            c = copy(held.at[pl.ds(other, half)], dst, over_d(b))
            yield
            c.wait()
            nxt = (ta if z == 0 else tb).at[k]
            nxt[...] = plus(held[pl.ds(mine, half)], dst[...])
            done.append(((aa if z == 0 else ab).at[k], mine, half, b))
            size, held = half, nxt
        for z, b in enumerate(bits[2:]):
            dst = zr.at[k, 2 + z, pl.ds(0, size)]
            c = copy(held, dst, over_d(b))
            yield
            c.wait()
            held[...] = plus(held[...], dst[...])
        for z, (up, mine, half, b) in enumerate(reversed(done)):
            up[pl.ds(mine, half)] = held[...]
            c = copy(up.at[pl.ds(mine, half)], up.at[pl.ds(mine, half)], over_d(b))
            yield
            c.wait()
            held = up
        c = copy(held, xs.at[k], over_d(1))
        yield
        c.wait()
        out(held, xs.at[k])

    def attn0(j):
        c = [copy(gs.at[:, j + 2 * u], rc.at[j, u], core()) for u in range(2)]
        yield
        for v in c:
            v.wait()
        for u in range(2):
            at = x + u - 2 * x * u
            for r in range(2):
                kk[j, u, r] = plus(gk[r, j + 2 * at], rc[j, at, r])
        if j == 0:
            c = [copy(kk.at[j, u, 1], ry.at[j, u], over_y()) for u in (1, 0)]
            yield
            c[0].wait()
            kk[j, 1, 0] = plus(kk[j, 1, 0], ry[j, 1])
            d = copy(kk.at[j, 1, 0], rx.at[j, 0], over_d(1))
            c[1].wait()
            kk[j, 0, 0] = plus(kk[j, 0, 0], ry[j, 0])
            yield
            d.wait()
            tt[j] = plus(kk[j, 0, 0], rx[j, 0])
        else:
            c = [copy(kk.at[j, 1, r], rx.at[j, r], over_d(1)) for r in (1, 0)]
            yield
            c[0].wait()
            kk[j, 0, 1] = plus(kk[j, 0, 1], rx[j, 1])
            d = copy(kk.at[j, 0, 1], ry.at[j, 0], over_y())
            c[1].wait()
            kk[j, 0, 0] = plus(kk[j, 0, 0], rx[j, 0])
            yield
            d.wait()
            tt[j] = plus(kk[j, 0, 0], ry[j, 0])

        def out(mine, got):
            f0[j + 2 * x] = mine[...]
            f0[j + 2 * (1 - x)] = got[...]

        yield from rest(j, out)

    def attn1(j):
        k = 2 + j
        tt[k] = t1[j]

        def out(mine, got):
            f1[j + 2 * x] = mine[...]
            f1[j + 2 * (1 - x)] = got[...]

        yield from rest(k, out)

    def small():
        rel_s[...] = rel[...]
        rep_s[...] = rep[...]
        for z, (to, b) in enumerate([(core(), 1), (over_y(), 2)]):
            c = [copy(rel_s, rel_r.at[z], to), copy(rep_s, rep_r.at[z], to)]
            yield
            for v in c:
                v.wait()
            rep_s[...] += rep_r[z]
            for r in range(4):
                rel_s[r] = rel_s[r] + rel_r[z, r ^ b]
        for z, b in enumerate([1] + bits):
            c = [
                copy(rel_s.at[0], rel_r.at[2 + z, 0], over_d(b)),
                copy(rep_s, rep_r.at[2 + z], over_d(b)),
            ]
            yield
            for v in c:
                v.wait()
            rep_s[...] += rep_r[2 + z]
            rel_s[0] = rel_s[0] + rel_r[2 + z, 0]
        rel_o[...] = rel_s[0]
        rep_o[...] = rep_s[...]

    chains = [attn0(0), attn0(1), attn1(0), attn1(1), small()]
    while chains:
        left = []
        for chain in chains:
            try:
                next(chain)
                left.append(chain)
            except StopIteration:
                pass
        chains = left


def finish(gs, gk, t1, rel, rep, dp):
    _, _, n, d = gs.shape
    nb = max(dp.bit_length() - 2, 0)
    vm = pl.BlockSpec(memory_space=pltpu.VMEM)
    return pl.pallas_call(
        functools.partial(finish_body, dp),
        in_specs=[vm] * 5,
        out_specs=[vm] * 4,
        out_shape=[jax.ShapeDtypeStruct((4, n, d), BF)] * 2
        + [jax.ShapeDtypeStruct(rel.shape[1:], F32), jax.ShapeDtypeStruct(rep.shape, F32)],
        scratch_shapes=[
            pltpu.VMEM((2, 2, 2, n, d), BF),
            pltpu.VMEM((2, 2, 2, n, d), BF),
            pltpu.VMEM((2, 2, n, d), BF),
            pltpu.VMEM((2, 2, n, d), BF),
            pltpu.VMEM((4, n, d), BF),
            pltpu.VMEM((4, max(nb, 1), n // 2, d), BF),
            pltpu.VMEM((4, n // 2, d), BF),
            pltpu.VMEM((4, n // 4, d), BF),
            pltpu.VMEM((4, n, d), BF),
            pltpu.VMEM((4, n // 2, d), BF),
            pltpu.VMEM((4, n, d), BF),
            pltpu.VMEM((3 + nb,) + rel.shape, F32),
            pltpu.VMEM((3 + nb,) + rep.shape, F32),
            pltpu.VMEM(rel.shape, F32),
            pltpu.VMEM(rep.shape, F32),
            pltpu.SemaphoreType.DMA((96,)),
            pltpu.SemaphoreType.DMA((96,)),
        ],
        compiler_params=pltpu.CompilerParams(
            collective_id=0, has_side_effects=True, vmem_limit_bytes=LIMIT
        ),
        name="finish",
        cost_estimate=cost(60),
    )(gs, gk, t1, rel, rep)


ROWS = 208
HALF = ROWS // 2
TILE = 416


def shards(clips, cot, gain, shift, qkv, qvb, wout, bout, win, b_in, wdown, bdown):
    tensor = lax.axis_index("tensor")
    y, core = tensor // 2, tensor % 2
    x = lax.axis_index("dp") % 2
    dp = lax.axis_size("dp")
    width = clips.shape[-1]
    places = clips.shape[2]
    e = qkv.shape[-1]
    h = win.shape[1] // 2

    def over_tensor(v, bit):
        return lax.ppermute(v, "tensor", [(i, i ^ bit) for i in range(4)])

    def over_dp(v, bit):
        return lax.ppermute(v, "dp", [(i, i ^ bit) for i in range(dp)])

    def after(v, *others):
        return lax.optimization_barrier((v,) + others)[0]

    def pad(v):
        return jnp.pad(v, ((0, 0), (0, ROWS - places), (0, 0)))

    def split(a, b):
        return jnp.where(x == 0, a, b), jnp.where(x == 0, b, a)

    def swap_clip(v):
        return over_tensor(lax.dynamic_index_in_dim(v, 1 - y, 0, False), 2)

    def mine_of(v):
        return lax.dynamic_index_in_dim(v, y, 0, False)

    def back(mine, got):
        mine, got = mine[:, :places], got[:, :places]
        return jnp.stack([jnp.where(y == 0, mine, got), jnp.where(y == 0, got, mine)])

    wt = [qkv[i].transpose(0, 2, 1).reshape(3 * e, width) for i in range(2)]
    pa = [v[: 2 * e] for v in wt]
    pb = [jnp.concatenate([v[2 * e :], wout[i]]) for i, v in enumerate(wt)]
    send = [jnp.where(x == 0, pa[i], pb[i]) for i in range(2)]
    y0 = over_tensor(send[0], 2)
    y1 = over_tensor(after(send[1], send[0]), 2)
    x_got = swap_clip(after(clips, send[0], send[1]))
    ab = [jnp.concatenate([pa[i], pb[i]]) for i in range(2)]
    c0 = over_tensor(ab[0], 1)
    bias = jnp.concatenate([qvb.reshape(1, -1), b_in.reshape(1, -1)])
    bias_y = over_tensor(bias, 2)
    bias_all = jnp.stack([bias, over_tensor(bias, 1), bias_y, over_tensor(bias_y, 1)])
    x0 = over_dp(y0, 1)
    cy0 = over_tensor(y0, 1)
    cx0 = over_tensor(x0, 1)
    win_t = win.T
    at = x * h
    send_m = [
        lax.dynamic_slice_in_dim(after(v, y0), at, h, 0) for v in (win_t, wdown)
    ]
    m_y = [over_tensor(v, 2) for v in send_m]
    cot_got = swap_clip(after(cot, x0, *send_m))
    x1 = over_dp(y1, 1)
    c1 = over_tensor(after(ab[1], c0), 1)
    cy1 = over_tensor(y1, 1)
    cx1 = over_tensor(x1, 1)
    m_x = [over_dp(v, 1) for v in m_y]
    m_c = [over_tensor(after(v, c0), 1) for v in (win_t, wdown)]
    m_cy = [over_tensor(v, 1) for v in m_y]
    m_cx = [over_tensor(v, 1) for v in m_x]

    def attn_weights(i, own, c, yy, xx, cy, cx):
        a2, b2 = split(yy, xx)
        a3, b3 = split(cy, cx)
        shards_a = [own[: 2 * e], c[: 2 * e], a2, a3]
        shards_b = [own[2 * e :], c[2 * e :], b2, b3]
        w = jnp.concatenate(
            [v[:e] for v in shards_a] + [v[e:] for v in shards_a] + [v[:e] for v in shards_b]
        )
        wo = jnp.concatenate([v[e:] for v in shards_b])
        b = bias_all[:, 0].reshape(4, 2, 2, e)
        return w, wo, b[:, i, 0].reshape(-1), b[:, i, 1].reshape(-1)

    def mlp_weights(k):
        two = jnp.concatenate(split(m_y[k], m_x[k]))
        three = jnp.concatenate(split(m_cy[k], m_cx[k]))
        own = (win_t, wdown)[k]
        return jnp.stack([three, m_c[k]]), jnp.stack([two, own])

    def to_places(v):
        own = lax.dynamic_slice_in_dim(v, HALF * core, HALF, 1)
        send = lax.dynamic_slice_in_dim(v, HALF * (1 - core), HALF, 1)
        both = jnp.concatenate([own, over_tensor(send, 1)])
        f = both.shape[0]
        both = both.reshape(f, HALF // 8, 8, width).transpose(1, 0, 2, 3)
        return both.reshape(HALF // 8, f * 8, width)

    def to_frames(v, flip=False):
        f = v.shape[1] // 8
        v = v.reshape(HALF // 8, f, 8, width).transpose(1, 0, 2, 3).reshape(f, HALF, width)
        own = v[: f // 2]
        got = over_tensor(v[f // 2 :], 1)
        if flip:
            got = jnp.concatenate([got[..., i * e : (i + 1) * e] for i in (1, 0, 3, 2)], axis=-1)
        return jnp.concatenate(
            [jnp.where(core == 0, own, got), jnp.where(core == 0, got, own)], axis=1
        )

    def rows8(*vs):
        return jnp.pad(jnp.stack(vs), ((0, 8 - len(vs)), (0, 0)))

    frames = 2 * clips.shape[1]
    flat = (frames * ROWS, width)
    w0, wo0, bq0, bv0 = attn_weights(0, ab[0], c0, y0, x0, cy0, cx0)
    w1, wo1, bq1, bv1 = attn_weights(1, ab[1], c1, y1, x1, cy1, cx1)
    vec = rows8(gain[0], shift[0], bq0, bv0, bout[0], gain[1], shift[1])
    xs = [pad(mine_of(clips)), pad(x_got)]
    half = frames // 2
    fwd = spatial(xs[0], w0, wo0, vec, places, frames, 0)
    s1, n1, q0, k0, v0, o0, lse0 = spatial(xs[1], w0, wo0, vec, places, frames, half, fwd)
    n1p = to_places(n1)
    q1, k1, v1, o1p, lse1 = temporal(n1p, w1, rows8(bq1, bv1))
    o1 = to_frames(o1p, True)
    wts, wds = mlp_weights(0), mlp_weights(1)
    bm = bias_all[:, 1:2]
    ma = (wts[0], wds[0], jnp.stack([bm[3], bm[1]]))
    mb = (wts[1], wds[1], jnp.stack([bm[2], bm[0]]))
    gb3 = jnp.concatenate([pad(mine_of(cot)), pad(cot_got)]).reshape(flat)

    vec = rows8(bout[1], gain[2], shift[2])
    s2, n2, branch, dn2, gwt_a, gwd_a, gb_a = mlp_first(
        s1.reshape(flat), o1.reshape(flat), gb3, wo1, vec, *ma, TILE
    )
    near, far, g2, g2b, gwt_b, gwd_b, gb_b, sums2 = mlp_second(
        s2, n2, gb3, branch, dn2, rows8(bdown, gain[2]), *mb, TILE
    )
    shape3 = (frames, ROWS, width)
    shape2 = (half, ROWS, width)

    def pick(v, axis):
        n = v.shape[axis] // 2
        return (
            lax.dynamic_slice_in_dim(v, x * n, n, axis),
            lax.dynamic_slice_in_dim(v, (1 - x) * n, n, axis),
        )

    keep_t = gwt_b + over_tensor(gwt_a, 1)
    keep_d = gwd_b + over_tensor(gwd_a, 1)
    g2p = to_places(g2b.reshape(shape3))
    g2p, keep_t, keep_d = lax.optimization_barrier((g2p, keep_t, keep_d))
    got_t = over_tensor(keep_t[0], 2)
    mine_d, send_d = pick(keep_d, 1)
    got_d = over_dp(send_d, 1)
    far_got = over_tensor(after(far.reshape(shape2)[:, :places], keep_t), 2)

    dn1p, dqkv1 = temporal_back(g2p, q1, k1, v1, lse1, w1, wo1)
    mine_t, send_t = pick(keep_t[1] + got_t, 0)
    mine_d = mine_d + got_d
    dn1 = to_frames(dn1p)
    gs1, gk1, sums1 = weight_grads(dqkv1, o1p, n1p, g2p)
    dn1, mine_t, send_t, mine_d = lax.optimization_barrier((dn1, mine_t, send_t, mine_d))
    got_t = over_dp(send_t, 1)
    got_d = over_tensor(mine_d[0], 2)
    keep1 = gk1 + over_tensor(gs1, 1)
    dn1, keep1 = lax.optimization_barrier((dn1, keep1))
    mine1, send1 = pick(keep1, 1)
    got1 = over_dp(send1, 1)
    output = back(near.reshape(shape2), far_got.astype(F32))
    g2 = g2.reshape(shape3)
    vec = rows8(gain[0], shift[0], gain[1])
    kept = (s1, dn1, g2, q0, k0, v0, lse0, w0, wo0, vec, places)
    g0_far, sums_f, *rest = spatial_back(xs[1], *kept, half, BF)
    in_got = over_tensor(g0_far[:, :places], 2)
    mlp_sum = jnp.concatenate([mine_t + got_t, mine_d[1] + got_d])
    mine1 = mine1 + got1
    rest[0], mlp_sum, mine1 = lax.optimization_barrier((rest[0], mlp_sum, mine1))
    if dp > 2:
        groups = [[i for i in range(dp) if i % 2 == p] for p in range(2)]
        mlp_sum = lax.psum(mlp_sum, "dp", axis_index_groups=groups)
    got1 = over_tensor(mine1[1], 2)
    g0, sums_n, dqkv0, n0, gb0 = spatial_back(xs[0], *kept, 0, F32, rest)
    t1 = mine1[0] + got1
    sums0 = sums_f + sums_n
    gs0, gk0, sums_b = weight_grads(dqkv0, o0, n0, gb0)
    input_grad = back(g0, in_got.astype(F32))

    rep = jnp.stack(
        [sums0[0], sums0[2], sums2[0], sums0[1], sums0[3], sums2[1], sums0[4], sums2[2], sums2[3]]
    )
    rep = jnp.pad(rep, ((0, 7), (0, 0)))
    qv = jnp.stack([sums_b[0, 0], sums_b[2, 0], sums1[0, 0], sums1[2, 0]])
    qv = qv.reshape(4, 4, e).transpose(1, 0, 2).reshape(4, 1, 4 * e)
    hid = jnp.stack([gb_b[1], gb_a[1], gb_b[0], gb_a[0]])
    rel = jnp.concatenate([qv, hid, jnp.zeros((4, 6, width), F32)], axis=1)
    f0, f1, rel, rep = finish(gs0, gk0, t1, rel, rep, dp)
    mlp = split(mlp_sum, over_dp(mlp_sum, 1))

    gqkv = jnp.stack([f0[:3], f1[:3]]).astype(F32).transpose(0, 1, 3, 2)
    gout = jnp.stack([f0[3], f1[3]]).astype(F32)
    gqv = rel[0].reshape(2, 2, e)
    gwin = jnp.concatenate([v[:h] for v in mlp]).T.astype(F32)
    gwd = jnp.concatenate([v[h:] for v in mlp]).astype(F32)
    return (
        output,
        input_grad,
        rep[0:3],
        rep[3:6],
        gqkv,
        gqv,
        gout,
        rep[6:8],
        gwin,
        rel[1],
        gwd,
        rep[8],
    )


def solution(mesh):
    placed = (
        P("dp", "tensor", None, None),
        P("dp", "tensor", None, None),
        P(),
        P(),
        P(None, None, None, "tensor"),
        P(None, None, "tensor"),
        P(None, "tensor", None),
        P(),
        P(None, "tensor"),
        P("tensor"),
        P("tensor", None),
        P(),
    )
    return jax.shard_map(
        shards,
        mesh=mesh,
        in_specs=placed,
        out_specs=(
            P("dp", "tensor", None, None),
            P("dp", "tensor", None, None),
            P(),
            P(),
            P(None, None, None, "tensor"),
            P(None, None, "tensor"),
            P(None, "tensor", None),
            P(),
            P(None, "tensor"),
            P("tensor"),
            P("tensor", None),
            P(),
        ),
        check_vma=False,
    )
```

time: 719 us -> 627 us (0.87)
  waiting for transfers between devices: 253 us -> 90.9 us
  Pallas kernels: 244 us -> 343 us
  local copies, waits for them, and re-layouts: 96.5 us -> 76.4 us
  between operations: 2.51 us -> 15.7 us
  starting transfers between devices: 39.2 us -> 27.8 us
  other arithmetic: 79.5 us -> 68.7 us
    ppermute x16 -> x8, waiting for transfers between devices: 183 us -> 34 us  [over_dp(): return lax.ppermute(v, 'dp', [(i, i ^ bit) for i in range(dp)])]
    pallas_call x1 -> x4, Pallas kernels: 46.9 us -> 146 us  [the longest x1 79.9 us: finish(): pl.pallas_call(functools.partial(finish_body, dp), in_specs=[vm] * 5, out...]
    slice x46 -> x30, local copies, waits for them, and re-layouts: 35.7 us -> 16.8 us  [the longest x6 3.09 us: attn_weights(): wo = jnp.concatenate([v[e:] for v in shards_b])]
    ppermute x34 -> x33, waiting for transfers between devices: 69.7 us -> 57 us  [over_tensor(): return lax.ppermute(v, 'tensor', [(i, i ^ bit) for i in range(4)])]
    another operation x30 -> x11, other arithmetic: 20.3 us -> 10.5 us  [the longest x8 9.31 us: mlp_weights(): return (jnp.stack([three, m_c[k]]), jnp.stack([two, own]))]
    ppermute x16 -> x8, starting transfers between devices: 18.8 us -> 9.05 us  [over_dp(): return lax.ppermute(v, 'dp', [(i, i ^ bit) for i in range(dp)])]
    pallas_call x1 -> x2, Pallas kernels: 48.9 us -> 44 us  [spatial_back(): pl.pallas_call(functools.partial(spatial_back_body, places), grid=(f,), i...]
    unnamed x181 -> x133, local copies, waits for them, and re-layouts: 30 us -> 25.2 us
  transfers between devices with their start and end apart: 50 -> 42, of which waited for: 13 -> 12; matrix products, arithmetic and copies ran while one was open for 21% -> 19% of each run, Pallas kernels for 22% -> 48%
where the time goes in v3:
time: 627 us; the launch traced here: 623 us
  Pallas kernels  343 us (55%)
  waiting for transfers between devices  90.9 us (14%)
  local copies, waits for them, and re-layouts  76.4 us (12%)
  other arithmetic  68.7 us (11%)
  starting transfers between devices  27.8 us (4%)
  between operations  15.7 us (3%)
    pallas_call x1, Pallas kernels, finish(): pl.pallas_call(functools.partial(finish_body, dp), in_specs=[vm] * 5, out...  79.9 us
    ppermute x33, waiting for transfers between devices, over_tensor(): return lax.ppermute(v, 'tensor', [(i, i ^ bit) for i in range(4)])  57 us
    pallas_call x1, Pallas kernels, mlp_second(): pl.pallas_call(mlp_second_body, grid=(rows // tile, ns), in_specs=[blk] *...  45.2 us
    pallas_call x2, Pallas kernels, spatial_back(): pl.pallas_call(functools.partial(spatial_back_body, places), grid=(f,), i...  44 us
    pallas_call x1, Pallas kernels, mlp_first(): pl.pallas_call(mlp_first_body, grid=(rows // tile, ns), in_specs=[blk, bl...  42.7 us
    pallas_call x1, Pallas kernels, temporal_back(): pl.pallas_call(temporal_back_body, grid=(b,), in_specs=[blk] * 4 + [pl.Bl...  36.7 us
    ppermute x8, waiting for transfers between devices, over_dp(): return lax.ppermute(v, 'dp', [(i, i ^ bit) for i in range(dp)])  34 us
    pallas_call x1, Pallas kernels, temporal(): pl.pallas_call(temporal_body, grid=(b,), in_specs=[blk, whole(w.shape), w...  32.9 us
  transfers between devices with their start and end apart: 42, of which 12 were waited for; matrix products, arithmetic and copies ran while one was open for 19% of the time, Pallas kernels for 48%

profile of v3, /device:TPU:0, one launch (start us, length us, event | category | flops | bytes accessed | tf_op | source)
XLA Modules:
  0.0 622.7 jit_solution(422119669796730307)
XLA Ops:
  8.9 3.0 collective-permute-start.7
  16.9 1.9 collective-permute-start.11
  22.1 2.7 constant_dynamic-slice_fusion.8
  27.5 1.7 fusion.10
  36.3 1.9 collective-permute-start.3
  42.1 1.9 collective-permute-done.11
  46.6 6.2 collective-permute-done.3
  52.8 1.9 collective-permute-start.22
  57.5 7.3 %collective-permute-done.12 = bf16[384,768]{1,0:T(8,128)(2,1)S(1)} collective-permute-done((bf16[384,768]{1,0:T(8,128)(2,1)}, bf16[384,768]{1,0:T(8,128)(2,1)S(1)}, u32[]{:S(2)}, u32[]{:S(2)}) %collective-permute-start.12) | collective-permute-done | bytes 589856 | tf_op jit(solution)/shard_map/ppermute | solution.py:675
  66.4 2.2 broadcast_select_fusion.15
  72.8 9.6 %collective-permute-done.17 = bf16[384,768]{1,0:T(8,128)(2,1)} collective-permute-done((bf16[384,768]{1,0:T(8,128)(2,1)S(1)}, bf16[384,768]{1,0:T(8,128)(2,1)}, u32[]{:S(2)}, u32[]{:S(2)}) %collective-permute-start.17) | collective-permute-done | bytes 589856 | tf_op jit(solution)/shard_map/ppermute | solution.py:672
  82.4 12.3 %collective-permute-done.22 = bf16[384,768]{1,0:T(8,128)(2,1)} collective-permute-done((bf16[384,768]{1,0:T(8,128)(2,1)S(1)}, bf16[384,768]{1,0:T(8,128)(2,1)}, u32[]{:S(2)}, u32[]{:S(2)}) %collective-permute-start.22) | collective-permute-done | bytes 589856 | tf_op jit(solution)/shard_map/ppermute | solution.py:672
  101.4 15.9 %spatial.2 = (f32[8,208,768]{2,1,0:T(8,128)}, bf16[8,208,768]{2,1,0:T(8,128)(2,1)}, bf16[8,208,768]{2,1,0:T(8,128)(2,1)}, bf16[8,208,768]{2,1,0:T(8,128)(2,1)}, ...) custom-call(bf16[4,208,768]{2,1,0:T(8,128)(2,1)} %pad.37.x, ...), custom_call_target="tpu_custom_call" | custom-call | flops 15840000000 | bytes 1440000 | tf_op jit(solution)/shard_map/spatial/pallas_call | solution.py:142
  117.3 16.0 %spatial.3 = (f32[8,208,768]{2,1,0:T(8,128)}, bf16[8,208,768]{2,1,0:T(8,128)(2,1)}, bf16[8,208,768]{2,1,0:T(8,128)(2,1)}, bf16[8,208,768]{2,1,0:T(8,128)(2,1)}, ...) custom-call(bf16[4,208,768]{2,1,0:T(8,128)(2,1)} %pad.35.x, ...), custom_call_target="tpu_custom_call", output_to_operand_aliasing={{0}: (4, {}), {1}: (5, {}), {2}: (6, {}), {3}: (7, {}), {4}... | custom-call | flops 15840000000 | bytes 1440000 | tf_op jit(solution)/shard_map/spatial/pallas_call | solution.py:142
  136.8 1.6 pad_maximum_fusion.6.wt
  150.0 2.9 fusion.16
  153.0 32.9 %temporal.1 = (bf16[13,128,768]{2,1,0:T(8,128)(2,1)}, bf16[13,128,768]{2,1,0:T(8,128)(2,1)}, bf16[13,128,768]{2,1,0:T(8,128)(2,1)}, bf16[13,128,768]{2,1,0:T(8,128)(2,1)}, f32[13,3,512]{2,1,0:T(4,128)}) custom-call(bf16[13,128,768]{2,1,0:T(8,128)(2,1)} %get-tuple-element.221.n1, bf16[2304,768]{1,0:T(8,128)(2,1)} %copy-done.42, f32[8,768]{1,0:T(8,128)} %select_maximum_fusion.2.vec), custom_call_target="tpu_custom_call" | custom-call | flops 34319998976 | bytes 3120000 | tf_op jit(solution)/shard_map/temporal/pallas_call | solution.py:171
  185.9 1.9 copy_bitcast_fusion.2
  191.5 2.9 pad_maximum_fusion.4.wt
  194.4 2.9 pad_maximum_fusion.5.wd
  198.7 1.7 fusion.2
  201.7 1.7 pad_maximum_fusion.2
  203.4 42.7 %mlp_first.1 = (f32[1664,768]{1,0:T(8,128)}, bf16[1664,768]{1,0:T(8,128)(2,1)}, f32[1664,768]{1,0:T(8,128)}, f32[1664,768]{1,0:T(8,128)}, bf16[2,768,768]{2,1,0:...) custom-call(f32[1664,768]{1,0:T(8,128)} %bitcast.182, bf16[1664,768]{1,0:T(8,128)(2,1)} %bitcast.167, ...), custom_call_target="tpu_custom_call" | custom-call | flops 46200000512 | bytes 4200000 | tf_op jit(solution)/shard_map/mlp_first/pallas_call | solution.py:371
  246.7 45.2 %mlp_second.1 = (f32[832,768]{1,0:T(8,128)}, bf16[832,768]{1,0:T(8,128)(2,1)}, f32[1664,768]{1,0:T(8,128)}, bf16[1664,768]{1,0:T(8,128)(2,1)}, bf16[2,768,768]{2...) custom-call(f32[1664,768]{1,0:T(8,128)} %get-tuple-element.107.s2, ...), custom_call_target="tpu_custom_call" | custom-call | flops 46200000512 | bytes 4200000 | tf_op jit(solution)/shard_map/mlp_second/pallas_call | solution.py:439
  291.9 3.0 constant_dynamic-slice_fusion.5
  298.7 1.7 copy_bitcast_fusion.1.g
  301.3 2.4 add.102
  303.7 3.1 add.101
  311.7 36.7 %temporal_back.1 = (bf16[13,128,768]{2,1,0:T(8,128)(2,1)}, bf16[3,13,128,768]{3,2,1,0:T(8,128)(2,1)}) custom-call(bf16[13,128,768]{2,1,0:T(8,128)(2,1)} %copy_bitcast_fusion.1.g, bf16[13,128,768]{2,1,0:T(8,128)(2,1)} %get-tuple-element.121.q, bf16[13,128,768]{2,1,0:T(8,128)(2,1)} %get-tuple-element.122.k, bf16[13,128,768]{2,1,0:T(8,128)(2,1)} %get-tuple-element.123.v, ...), custom_call_target="tpu_custom_call" | custom-call | flops 39600001024 | bytes 3600000 | tf_op jit(solution)/shard_map/temporal_back/pallas_call | solution.py:206
  348.4 1.9 copy_bitcast_fusion
  351.4 14.9 %weight_grads.2 = (bf16[2,4,192,768]{3,2,1,0:T(8,128)(2,1)}, bf16[2,4,192,768]{3,2,1,0:T(8,128)(2,1)}, f32[4,1,768]{2,1,0:T(1,128)}) custom-call(bf16[3,1664,768]{2,1,0:T(8,128)(2,1)} %bitcast.179, bf16[1664,768]{1,0:T(8,128)(2,1)} %bitcast.163, bf16[1664,768]{1,0:T(8,128)(2,1)} %bitcast.169, bf16[1664,768]{1,0:T(8,128)(2,1)} %bitcast.166), custom_call_target="tpu_custom_call" | custom-call | flops 15399999488 | bytes 1400000 | tf_op jit(solution)/shard_map/weight_grads/pallas_call | solution.py:250
  368.7 1.7 bitcast_add_fusion
  373.7 1.6 pad_maximum_fusion.3.dn1
  377.1 20.2 %collective-permute-done.30 = bf16[4,196,768]{2,0,1:T(4,128)(2,1)S(1)} collective-permute-done((bf16[4,196,768]{2,0,1:T(4,128)(2,1)}, bf16[4,196,768]{2,0,1:T(4,128)(2,1)S(1)}, u32[]{:S(2)}, u32[]{:S(2)}) %collective-permute-start.30) | collective-permute-done | bytes 1204256 | tf_op jit(solution)/shard_map/ppermute | solution.py:672
  398.1 4.1 copy.88
  402.4 6.7 %collective-permute-done.36 = bf16[384,768]{1,0:T(8,128)(2,1)S(1)} collective-permute-done((bf16[384,768]{1,0:T(8,128)(2,1)S(1)}, bf16[384,768]{1,0:T(8,128)(2,1)S(1)}, u32[]{:S(2)}, u32[]{:S(2)}) %collective-permute-start.36) | collective-permute-done | bytes 589856 | tf_op jit(solution)/shard_map/ppermute | solution.py:672
  410.2 2.9 add.106
  414.0 21.8 %spatial_back.2 = (bf16[4,208,768]{2,1,0:T(8,128)(2,1)}, f32[8,768]{1,0:T(8,128)}, bf16[3,8,208,768]{3,2,1,0:T(8,128)(2,1)}, bf16[8,208,768]{2,1,0:T(8,128)(2,1)}, bf16[8,208,768]{2,1,0:T(8,128)(2,1)}) custom-call(bf16[4,208,768]{2,1,0:T(8,128)(2,1)} %pad.35.x, f32[8,208,768]{2,1,0:T(8,128)} %get-tuple-element.97.s1, ...), custom_call_target="tpu_custom_call" | custom-call | flops 22000001024 | bytes 2000000 | tf_op jit(solution)/shard_map/spatial_back/pallas_call | solution.py:302
  441.9 22.2 %spatial_back.3 = (f32[4,208,768]{2,1,0:T(8,128)}, f32[8,768]{1,0:T(8,128)}, bf16[3,8,208,768]{3,2,1,0:T(8,128)(2,1)}, bf16[8,208,768]{2,1,0:T(8,128)(2,1)}, bf16[8,208,768]{2,1,0:T(8,128)(2,1)}) custom-call(bf16[4,208,768]{2,1,0:T(8,128)(2,1)} %pad.37.x, ...), custom_call_target="tpu_custom_call", output_to_operand_aliasing={{2}: (11, {}), {3}: (12, {}), {4}: (13, {})} | custom-call | flops 22000001024 | bytes 2000000 | tf_op jit(solution)/shard_map/spatial_back/pallas_call | solution.py:302
  464.1 14.8 %weight_grads.3 = (bf16[2,4,192,768]{3,2,1,0:T(8,128)(2,1)}, bf16[2,4,192,768]{3,2,1,0:T(8,128)(2,1)}, f32[4,1,768]{2,1,0:T(1,128)}) custom-call(bf16[3,1664,768]{2,1,0:T(8,128)(2,1)} %bitcast.178, bf16[1664,768]{1,0:T(8,128)(2,1)} %bitcast.185, bf16[1664,768]{1,0:T(8,128)(2,1)} %bitcast.183, bf16[1664,768]{1,0:T(8,128)(2,1)} %bitcast.184), custom_call_target="tpu_custom_call" | custom-call | flops 15399999488 | bytes 1400000 | tf_op jit(solution)/shard_map/weight_grads/pallas_call | solution.py:250
  482.9 2.4 fusion.5
  485.7 4.1 copy.89
  489.7 4.9 collective-permute-done.39
  495.6 79.9 %finish.1 = (bf16[4,192,768]{2,1,0:T(8,128)(2,1)}, bf16[4,192,768]{2,1,0:T(8,128)(2,1)}, f32[8,768]{1,0:T(8,128)}, f32[16,768]{1,0:T(8,128)}) custom-call(bf16[2,4,192,768]{3,2,1,0:T(8,128)(2,1)} %get-tuple-element.151.gs, bf16[2,4,192,768]{3,2,1,0:T(8,128)(2,1)} %get-tuple-element.152.gk, bf16[2,192,768]{2,1,0:T(8,128)(2,1)} %bitcast_add_fusion.1.t1, ...), custom_call_target="tpu_custom_call" | custom-call | flops 65999998976 | bytes 6000000 | tf_op jit(solution)/shard_map/finish/pallas_call | solution.py:623
  584.5 2.0 convert_bitcast_fusion
  587.1 19.6 %collective-permute-done.40 = bf16[768,768]{1,0:T(8,128)(2,1)S(1)} collective-permute-done((bf16[768,768]{1,0:T(8,128)(2,1)}, bf16[768,768]{1,0:T(8,128)(2,1)S(1)}, u32[]{:S(2)}, u32[]{:S(2)}) %collective-permute-start.40) | collective-permute-done | bytes 1179680 | tf_op jit(solution)/shard_map/ppermute | solution.py:675
  609.5 3.2 copy.90
  612.7 2.6 maximum_convert_fusion
  (324 shorter events, 107.3 us)
Async XLA Ops:
  7.2 573.9 %all-reduce.12.cloned.1.call-start = ((), (), s32[]{:S(2)}) async-start(), calls=%async_computation | async-start | bytes 2359296 | tf_op jit(solution)/shard_map/psum | solution.py:834
  8.9 25.9 %collective-permute-start.7 = (f32[2,768]{1,0:T(2,128)S(1)}, f32[2,768]{1,0:T(2,128)S(1)}, u32[]{:S(2)}, u32[]{:S(2)}) collective-permute-start(f32[2,768]{1,0:T(2,128)S(1)} %get-tuple-element.292), channel_id=1, source_target_pairs={{0,2},{1,3},{2,0},{3,1},{4,6},{5,7},{6,4},{7,5},{8,10},{9,11},{10,... | collective-permute-start | bytes 18440 | tf_op jit(solution)/shard_map/ppermute | solution.py:672
  11.9 24.0 %collective-permute-start.6 = (f32[2,768]{1,0:T(2,128)S(1)}, f32[2,768]{1,0:T(2,128)S(1)}, u32[]{:S(2)}, u32[]{:S(2)}) collective-permute-start(f32[2,768]{1,0:T(2,128)S(1)} %get-tuple-element.292), channel_id=1, source_target_pairs={{0,1},{1,0},{2,3},{3,2},{4,5},{5,4},{6,7},{7,6},{8,9},{9,8},{10,11... | collective-permute-start | bytes 18440 | tf_op jit(solution)/shard_map/ppermute | solution.py:672
  14.9 21.4 %collective-permute-start.2 = (bf16[384,768]{1,0:T(8,128)(2,1)}, bf16[384,768]{1,0:T(8,128)(2,1)}, u32[]{:S(2)}, u32[]{:S(2)}) collective-permute-start(bf16[384,768]{1,0:T(8,128)(2,1)} %maximum_select_fusion), channel_id=1, source_target_pairs={{0,2},{1,3},{2,0},{3,1},{4,6},{5,7},{6,4},{7,5},{8,10},{9,11},{10,... | collective-permute-start | bytes 1769480 | tf_op jit(solution)/shard_map/ppermute | solution.py:672
  16.9 27.1 %collective-permute-start.11 = (bf16[384,768]{1,0:T(8,128)(2,1)}, bf16[384,768]{1,0:T(8,128)(2,1)}, u32[]{:S(2)}, u32[]{:S(2)}) collective-permute-start(bf16[384,768]{1,0:T(8,128)(2,1)} %maximum_select_fusion.1), channel_id=1, source_target_pairs={{0,2},{1,3},{2,0},{3,1},{4,6},{5,7},{6,4},{7,5},{8,10},{9,11},{10,... | collective-permute-start | bytes 1769480 | tf_op jit(solution)/shard_map/ppermute | solution.py:672
  19.9 35.1 %collective-permute-start.1 = (bf16[768,768]{1,0:T(8,128)(2,1)}, bf16[768,768]{1,0:T(8,128)(2,1)}, u32[]{:S(2)}, u32[]{:S(2)}) collective-permute-start(bf16[768,768]{1,0:T(8,128)(2,1)} %pad_maximum_fusion.9), channel_id=1, source_target_pairs={{0,1},{1,0},{2,3},{3,2},{4,5},{5,4},{6,7},{7,6},{8,9},{9,8},{10,11... | collective-permute-start | bytes 3538952 | tf_op jit(solution)/shard_map/ppermute | solution.py:672
  34.7 1.4 collective-permute-start.8
  35.9 33.9 %collective-permute-start = (bf16[4,196,768]{2,0,1:T(4,128)(2,1)}, bf16[4,196,768]{2,0,1:T(4,128)(2,1)}, u32[]{:S(2)}, u32[]{:S(2)}) collective-permute-start(bf16[4,196,768]{2,0,1:T(4,128)(2,1)} %dynamic-slice_bitcast_fusion.1), channel_id=1, source_target_pairs={{0,2},{1,3},{2,0},{3,1},{4,6},{5,7},{6,4},{7,5},{8,10},{9,11},{10,... | collective-permute-start | bytes 3612680 | tf_op jit(solution)/shard_map/ppermute | solution.py:672
  36.3 16.5 %collective-permute-start.3 = (bf16[384,768]{1,0:T(8,128)(2,1)}, bf16[384,768]{1,0:T(8,128)(2,1)}, u32[]{:S(2)}, u32[]{:S(2)}) collective-permute-start(bf16[384,768]{1,0:T(8,128)(2,1)} %collective-permute-done.2), channel_id=1, source_target_pairs={{0,4},{4,0},{8,12},{12,8},{16,20},{20,16},{24,28},{28,24},{1,5},{5... | collective-permute-start | bytes 1769480 | tf_op jit(solution)/shard_map/ppermute | solution.py:675
  38.6 16.1 %copy-start.7 = (bf16[2,4,196,768]{3,1,2,0:T(4,128)(2,1)S(1)}, bf16[2,4,196,768]{3,1,2,0:T(4,128)(2,1)}, u32[]{:S(2)}) copy-start(bf16[2,4,196,768]{3,1,2,0:T(4,128)(2,1)} %param.13) | copy-start | bytes 7225348
  40.5 41.9 %collective-permute-start.17 = (bf16[384,768]{1,0:T(8,128)(2,1)S(1)}, bf16[384,768]{1,0:T(8,128)(2,1)}, u32[]{:S(2)}, u32[]{:S(2)}) collective-permute-start(bf16[384,768]{1,0:T(8,128)(2,1)S(1)} %constant_dynamic-slice_fusion.7), channel_id=1, source_target_pairs={{0,2},{1,3},{2,0},{3,1},{4,6},{5,7},{6,4},{7,5},{8,10},{9,11},{10,... | collective-permute-start | bytes 1769480 | tf_op jit(solution)/shard_map/ppermute | solution.py:672
  44.0 20.8 %collective-permute-start.12 = (bf16[384,768]{1,0:T(8,128)(2,1)}, bf16[384,768]{1,0:T(8,128)(2,1)S(1)}, u32[]{:S(2)}, u32[]{:S(2)}) collective-permute-start(bf16[384,768]{1,0:T(8,128)(2,1)} %collective-permute-done.11), channel_id=1, source_target_pairs={{0,4},{4,0},{8,12},{12,8},{16,20},{20,16},{24,28},{28,24},{1,5},{5... | collective-permute-start | bytes 1769480 | tf_op jit(solution)/shard_map/ppermute | solution.py:675
  52.8 41.9 %collective-permute-start.22 = (bf16[384,768]{1,0:T(8,128)(2,1)S(1)}, bf16[384,768]{1,0:T(8,128)(2,1)}, u32[]{:S(2)}, u32[]{:S(2)}) collective-permute-start(bf16[384,768]{1,0:T(8,128)(2,1)S(1)} %constant_dynamic-slice_fusion.6), channel_id=1, source_target_pairs={{0,2},{1,3},{2,0},{3,1},{4,6},{5,7},{6,4},{7,5},{8,10},{9,11},{10,... | collective-permute-start | bytes 1769480 | tf_op jit(solution)/shard_map/ppermute | solution.py:672
  55.1 17.3 %collective-permute-start.4 = (bf16[384,768]{1,0:T(8,128)(2,1)}, bf16[384,768]{1,0:T(8,128)(2,1)S(1)}, u32[]{:S(2)}, u32[]{:S(2)}) collective-permute-start(bf16[384,768]{1,0:T(8,128)(2,1)} %collective-permute-done.2), channel_id=1, source_target_pairs={{0,1},{1,0},{2,3},{3,2},{4,5},{5,4},{6,7},{7,6},{8,9},{9,8},{10,11... | collective-permute-start | bytes 1769480 | tf_op jit(solution)/shard_map/ppermute | solution.py:672
  64.8 31.4 %collective-permute-start.5 = (bf16[384,768]{1,0:T(8,128)(2,1)}, bf16[384,768]{1,0:T(8,128)(2,1)S(1)}, u32[]{:S(2)}, u32[]{:S(2)}) collective-permute-start(bf16[384,768]{1,0:T(8,128)(2,1)} %collective-permute-done.3), channel_id=1, source_target_pairs={{0,1},{1,0},{2,3},{3,2},{4,5},{5,4},{6,7},{7,6},{8,9},{9,8},{10,11... | collective-permute-start | bytes 1769480 | tf_op jit(solution)/shard_map/ppermute | solution.py:672
  69.8 71.4 %collective-permute-start.13 = (bf16[384,768]{1,0:T(8,128)(2,1)}, bf16[384,768]{1,0:T(8,128)(2,1)}, u32[]{:S(2)}, u32[]{:S(2)}) collective-permute-start(bf16[384,768]{1,0:T(8,128)(2,1)} %collective-permute-done.11), channel_id=1, source_target_pairs={{0,1},{1,0},{2,3},{3,2},{4,5},{5,4},{6,7},{7,6},{8,9},{9,8},{10,11... | collective-permute-start | bytes 1769480 | tf_op jit(solution)/shard_map/ppermute | solution.py:672
  71.2 25.6 %copy-start.6 = (bf16[3,192,768]{2,1,0:T(8,128)(2,1)S(1)}, bf16[3,192,768]{2,1,0:T(8,128)(2,1)}, u32[]{:S(2)}) copy-start(bf16[3,192,768]{2,1,0:T(8,128)(2,1)} %copy-done.5) | copy-start | bytes 2654212
  72.3 71.0 %collective-permute-start.10 = (bf16[768,768]{1,0:T(8,128)(2,1)}, bf16[768,768]{1,0:T(8,128)(2,1)}, u32[]{:S(2)}, u32[]{:S(2)}) collective-permute-start(bf16[768,768]{1,0:T(8,128)(2,1)} %pad_maximum_fusion.11), channel_id=1, source_target_pairs={{0,1},{1,0},{2,3},{3,2},{4,5},{5,4},{6,7},{7,6},{8,9},{9,8},{10,11... | collective-permute-start | bytes 3538952 | tf_op jit(solution)/shard_map/ppermute | solution.py:672
  82.4 109.1 %collective-permute-start.21 = (bf16[768,768]{1,0:T(8,128)(2,1)S(1)}, bf16[768,768]{1,0:T(8,128)(2,1)}, u32[]{:S(2)}, u32[]{:S(2)}) collective-permute-start(bf16[768,768]{1,0:T(8,128)(2,1)S(1)} %bitcast.156), channel_id=1, source_target_pairs={{0,1},{1,0},{2,3},{3,2},{4,5},{5,4},{6,7},{7,6},{8,9},{9,8},{10,11... | collective-permute-start | bytes 3538952 | tf_op jit(solution)/shard_map/ppermute | solution.py:672
  94.7 38.6 %collective-permute-start.19 = (bf16[384,768]{1,0:T(8,128)(2,1)}, bf16[384,768]{1,0:T(8,128)(2,1)}, u32[]{:S(2)}, u32[]{:S(2)}) collective-permute-start(bf16[384,768]{1,0:T(8,128)(2,1)} %collective-permute-done.17), channel_id=1, source_target_pairs={{0,4},{4,0},{8,12},{12,8},{16,20},{20,16},{24,28},{28,24},{1,5},{5... | collective-permute-start | bytes 1769480 | tf_op jit(solution)/shard_map/ppermute | solution.py:675
  96.2 38.7 %collective-permute-start.24 = (bf16[384,768]{1,0:T(8,128)(2,1)}, bf16[384,768]{1,0:T(8,128)(2,1)}, u32[]{:S(2)}, u32[]{:S(2)}) collective-permute-start(bf16[384,768]{1,0:T(8,128)(2,1)} %collective-permute-done.22), channel_id=1, source_target_pairs={{0,4},{4,0},{8,12},{12,8},{16,20},{20,16},{24,28},{28,24},{1,5},{5... | collective-permute-start | bytes 1769480 | tf_op jit(solution)/shard_map/ppermute | solution.py:675
  133.3 61.1 %collective-permute-start.26 = (bf16[768,768]{1,0:T(8,128)(2,1)}, bf16[768,768]{1,0:T(8,128)(2,1)}, u32[]{:S(2)}, u32[]{:S(2)}) collective-permute-start(bf16[768,768]{1,0:T(8,128)(2,1)} %param.22), channel_id=1, source_target_pairs={{0,1},{1,0},{2,3},{3,2},{4,5},{5,4},{6,7},{7,6},{8,9},{9,8},{10,11... | collective-permute-start | bytes 3538952 | tf_op jit(solution)/shard_map/ppermute | solution.py:672
  134.9 6.5 %collective-permute-start.14 = (bf16[384,768]{1,0:T(8,128)(2,1)S(1)}, bf16[384,768]{1,0:T(8,128)(2,1)S(1)}, u32[]{:S(2)}, u32[]{:S(2)}) collective-permute-start(bf16[384,768]{1,0:T(8,128)(2,1)S(1)} %copy-done.34), channel_id=1, source_target_pairs={{0,1},{1,0},{2,3},{3,2},{4,5},{5,4},{6,7},{7,6},{8,9},{9,8},{10,11... | collective-permute-start | bytes 1769480 | tf_op jit(solution)/shard_map/ppermute | solution.py:672
  141.2 6.4 %collective-permute-start.18 = (bf16[384,768]{1,0:T(8,128)(2,1)}, bf16[384,768]{1,0:T(8,128)(2,1)S(1)}, u32[]{:S(2)}, u32[]{:S(2)}) collective-permute-start(bf16[384,768]{1,0:T(8,128)(2,1)} %collective-permute-done.17), channel_id=1, source_target_pairs={{0,1},{1,0},{2,3},{3,2},{4,5},{5,4},{6,7},{7,6},{8,9},{9,8},{10,11... | collective-permute-start | bytes 1769480 | tf_op jit(solution)/shard_map/ppermute | solution.py:672
  141.4 8.2 %collective-permute-start.9 = (bf16[8,104,768]{2,1,0:T(8,128)(2,1)S(1)}, bf16[8,104,768]{2,1,0:T(8,128)(2,1)S(1)}, u32[]{:S(2)}, u32[]{:S(2)}) collective-permute-start(bf16[8,104,768]{2,1,0:T(8,128)(2,1)S(1)} %get-tuple-element.225), channel_id=1, source_target_pairs={{0,1},{1,0},{2,3},{3,2},{4,5},{5,4},{6,7},{7,6},{8,9},{9,8},{10,11... | collective-permute-start | bytes 3833864 | tf_op jit(solution)/shard_map/ppermute | solution.py:672
  143.3 4.6 collective-permute-start.20
  147.6 49.7 %collective-permute-start.16 = (bf16[4,196,768]{2,0,1:T(4,128)(2,1)}, bf16[4,196,768]{2,0,1:T(4,128)(2,1)}, u32[]{:S(2)}, u32[]{:S(2)}) collective-permute-start(bf16[4,196,768]{2,0,1:T(4,128)(2,1)} %copy.76), channel_id=1, source_target_pairs={{0,2},{1,3},{2,0},{3,1},{4,6},{5,7},{6,4},{7,5},{8,10},{9,11},{10,... | collective-permute-start | bytes 3612680 | tf_op jit(solution)/shard_map/ppermute | solution.py:672
  147.9 40.0 %collective-permute-start.23 = (bf16[384,768]{1,0:T(8,128)(2,1)}, bf16[384,768]{1,0:T(8,128)(2,1)}, u32[]{:S(2)}, u32[]{:S(2)}) collective-permute-start(bf16[384,768]{1,0:T(8,128)(2,1)} %collective-permute-done.22), channel_id=1, source_target_pairs={{0,1},{1,0},{2,3},{3,2},{4,5},{5,4},{6,7},{7,6},{8,9},{9,8},{10,11... | collective-permute-start | bytes 1769480 | tf_op jit(solution)/shard_map/ppermute | solution.py:672
  149.6 39.3 %collective-permute-start.25 = (bf16[384,768]{1,0:T(8,128)(2,1)}, bf16[384,768]{1,0:T(8,128)(2,1)}, u32[]{:S(2)}, u32[]{:S(2)}) collective-permute-start(bf16[384,768]{1,0:T(8,128)(2,1)} %collective-permute-done.24), channel_id=1, source_target_pairs={{0,1},{1,0},{2,3},{3,2},{4,5},{5,4},{6,7},{7,6},{8,9},{9,8},{10,11... | collective-permute-start | bytes 1769480 | tf_op jit(solution)/shard_map/ppermute | solution.py:672
  187.9 12.5 %collective-permute-start.15 = (bf16[8,104,768]{2,1,0:T(8,128)(2,1)S(1)}, bf16[8,104,768]{2,1,0:T(8,128)(2,1)S(1)}, u32[]{:S(2)}, u32[]{:S(2)}) collective-permute-start(bf16[8,104,768]{2,1,0:T(8,128)(2,1)S(1)} %slice_bitcast_fusion.2), channel_id=1, source_target_pairs={{0,1},{1,0},{2,3},{3,2},{4,5},{5,4},{6,7},{7,6},{8,9},{9,8},{10,11... | collective-permute-start | bytes 3833864 | tf_op jit(solution)/shard_map/ppermute | solution.py:672
  246.1 54.3 %collective-permute-start.29 = (bf16[2,768,768]{2,1,0:T(8,128)(2,1)}, bf16[2,768,768]{2,1,0:T(8,128)(2,1)}, u32[]{:S(2)}, u32[]{:S(2)}) collective-permute-start(bf16[2,768,768]{2,1,0:T(8,128)(2,1)} %get-tuple-element.117), channel_id=1, source_target_pairs={{0,1},{1,0},{2,3},{3,2},{4,5},{5,4},{6,7},{7,6},{8,9},{9,8},{10,11... | collective-permute-start | bytes 7077896 | tf_op jit(solution)/shard_map/ppermute | solution.py:672
  246.3 57.4 %collective-permute-start.28 = (bf16[2,768,768]{2,1,0:T(8,128)(2,1)}, bf16[2,768,768]{2,1,0:T(8,128)(2,1)}, u32[]{:S(2)}, u32[]{:S(2)}) collective-permute-start(bf16[2,768,768]{2,1,0:T(8,128)(2,1)} %get-tuple-element.115), channel_id=1, source_target_pairs={{0,1},{1,0},{2,3},{3,2},{4,5},{5,4},{6,7},{7,6},{8,9},{9,8},{10,11... | collective-permute-start | bytes 7077896 | tf_op jit(solution)/shard_map/ppermute | solution.py:672
  294.9 3.8 collective-permute-start.27
  308.0 62.6 %collective-permute-start.33 = (bf16[2,384,768]{2,1,0:T(8,128)(2,1)}, bf16[2,384,768]{2,1,0:T(8,128)(2,1)}, u32[]{:S(2)}, u32[]{:S(2)}) collective-permute-start(bf16[2,384,768]{2,1,0:T(8,128)(2,1)} %constant_dynamic-slice_fusion.1), channel_id=1, source_target_pairs={{0,4},{4,0},{8,12},{12,8},{16,20},{20,16},{24,28},{28,24},{1,5},{5... | collective-permute-start | bytes 3538952 | tf_op jit(solution)/shard_map/ppermute | solution.py:675
  310.6 58.1 %collective-permute-start.32 = (bf16[768,768]{1,0:T(8,128)(2,1)}, bf16[768,768]{1,0:T(8,128)(2,1)}, u32[]{:S(2)}, u32[]{:S(2)}) collective-permute-start(bf16[768,768]{1,0:T(8,128)(2,1)} %slice_bitcast_fusion.4), channel_id=1, source_target_pairs={{0,2},{1,3},{2,0},{3,1},{4,6},{5,7},{6,4},{7,5},{8,10},{9,11},{10,... | collective-permute-start | bytes 3538952 | tf_op jit(solution)/shard_map/ppermute | solution.py:672
  351.4 20.8 %collective-permute-start.31 = (bf16[8,104,768]{2,1,0:T(8,128)(2,1)}, bf16[8,104,768]{2,1,0:T(8,128)(2,1)}, u32[]{:S(2)}, u32[]{:S(2)}) collective-permute-start(bf16[8,104,768]{2,1,0:T(8,128)(2,1)} %slice_bitcast_fusion), channel_id=1, source_target_pairs={{0,1},{1,0},{2,3},{3,2},{4,5},{5,4},{6,7},{7,6},{8,9},{9,8},{10,11... | collective-permute-start | bytes 3833864 | tf_op jit(solution)/shard_map/ppermute | solution.py:672
  366.4 43.9 %collective-permute-start.34 = (bf16[2,4,192,768]{3,2,1,0:T(8,128)(2,1)}, bf16[2,4,192,768]{3,2,1,0:T(8,128)(2,1)}, u32[]{:S(2)}, u32[]{:S(2)}) collective-permute-start(bf16[2,4,192,768]{3,2,1,0:T(8,128)(2,1)} %get-tuple-element.130), channel_id=1, source_target_pairs={{0,1},{1,0},{2,3},{3,2},{4,5},{5,4},{6,7},{7,6},{8,9},{9,8},{10,11... | collective-permute-start | bytes 7077896 | tf_op jit(solution)/shard_map/ppermute | solution.py:672
  367.8 29.6 %collective-permute-start.30 = (bf16[4,196,768]{2,0,1:T(4,128)(2,1)}, bf16[4,196,768]{2,0,1:T(4,128)(2,1)S(1)}, u32[]{:S(2)}, u32[]{:S(2)}) collective-permute-start(bf16[4,196,768]{2,0,1:T(4,128)(2,1)} %copy.94), channel_id=1, source_target_pairs={{0,2},{1,3},{2,0},{3,1},{4,6},{5,7},{6,4},{7,5},{8,10},{9,11},{10,... | collective-permute-start | bytes 3612680 | tf_op jit(solution)/shard_map/ppermute | solution.py:672
  373.7 23.7 %copy-start.21 = (f32[832,768]{1,0:T(8,128)S(1)}, f32[832,768]{1,0:T(8,128)}, u32[]{:S(2)}) copy-start(f32[832,768]{1,0:T(8,128)} %get-tuple-element.111) | copy-start | bytes 7667716
  375.3 26.9 %collective-permute-start.35 = (bf16[384,768]{1,0:T(8,128)(2,1)S(1)}, bf16[384,768]{1,0:T(8,128)(2,1)S(1)}, u32[]{:S(2)}, u32[]{:S(2)}) collective-permute-start(bf16[384,768]{1,0:T(8,128)(2,1)S(1)} %get-tuple-element.139), channel_id=1, source_target_pairs={{0,4},{4,0},{8,12},{12,8},{16,20},{20,16},{24,28},{28,24},{1,5},{5... | collective-permute-start | bytes 1769480 | tf_op jit(solution)/shard_map/ppermute | solution.py:675
  376.0 33.1 %collective-permute-start.36 = (bf16[384,768]{1,0:T(8,128)(2,1)S(1)}, bf16[384,768]{1,0:T(8,128)(2,1)S(1)}, u32[]{:S(2)}, u32[]{:S(2)}) collective-permute-start(bf16[384,768]{1,0:T(8,128)(2,1)S(1)} %slice_bitcast_fusion.10), channel_id=1, source_target_pairs={{0,2},{1,3},{2,0},{3,1},{4,6},{5,7},{6,4},{7,5},{8,10},{9,11},{10,... | collective-permute-start | bytes 1769480 | tf_op jit(solution)/shard_map/ppermute | solution.py:672
  413.3 27.2 %collective-permute-start.37 = (bf16[2,2,192,768]{3,2,1,0:T(8,128)(2,1)S(1)}, bf16[2,2,192,768]{3,2,1,0:T(8,128)(2,1)}, u32[]{:S(2)}, u32[]{:S(2)}) collective-permute-start(bf16[2,2,192,768]{3,2,1,0:T(8,128)(2,1)S(1)} %constant_dynamic-slice_fusion), channel_id=1, source_target_pairs={{0,4},{4,0},{8,12},{12,8},{16,20},{20,16},{24,28},{28,24},{1,5},{5... | collective-permute-start | bytes 3538952 | tf_op jit(solution)/shard_map/ppermute | solution.py:675
  438.7 44.2 %collective-permute-start.38 = (bf16[4,196,768]{2,0,1:T(4,128)(2,1)}, bf16[4,196,768]{2,0,1:T(4,128)(2,1)}, u32[]{:S(2)}, u32[]{:S(2)}) collective-permute-start(bf16[4,196,768]{2,0,1:T(4,128)(2,1)} %copy.82), channel_id=1, source_target_pairs={{0,2},{1,3},{2,0},{3,1},{4,6},{5,7},{6,4},{7,5},{8,10},{9,11},{10,... | collective-permute-start | bytes 3612680 | tf_op jit(solution)/shard_map/ppermute | solution.py:672
  464.1 14.9 %copy-start.45 = (f32[8,768]{1,0:T(8,128)S(1)}, f32[8,768]{1,0:T(8,128)}, u32[]{:S(2)}) copy-start(f32[8,768]{1,0:T(8,128)} %get-tuple-element.158) | copy-start | bytes 73732
  464.1 14.8 %copy-start.46 = (f32[8,768]{1,0:T(8,128)S(1)}, f32[8,768]{1,0:T(8,128)}, u32[]{:S(2)}) copy-start(f32[8,768]{1,0:T(8,128)} %get-tuple-element.159) | copy-start | bytes 73732
  481.2 13.5 %collective-permute-start.39 = (bf16[2,192,768]{2,1,0:T(8,128)(2,1)S(1)}, bf16[2,192,768]{2,1,0:T(8,128)(2,1)S(1)}, u32[]{:S(2)}, u32[]{:S(2)}) collective-permute-start(bf16[2,192,768]{2,1,0:T(8,128)(2,1)S(1)} %slice_bitcast_fusion.9), channel_id=1, source_target_pairs={{0,2},{1,3},{2,0},{3,1},{4,6},{5,7},{6,4},{7,5},{8,10},{9,11},{10,... | collective-permute-start | bytes 1769480 | tf_op jit(solution)/shard_map/ppermute | solution.py:672
  581.1 25.7 %collective-permute-start.40 = (bf16[768,768]{1,0:T(8,128)(2,1)}, bf16[768,768]{1,0:T(8,128)(2,1)S(1)}, u32[]{:S(2)}, u32[]{:S(2)}) collective-permute-start(bf16[768,768]{1,0:T(8,128)(2,1)} %all-reduce.12.cloned.1.call-done), channel_id=1, source_target_pairs={{0,4},{4,0},{8,12},{12,8},{16,20},{20,16},{24,28},{28,24},{1,5},{5... | collective-permute-start | bytes 3538952 | tf_op jit(solution)/shard_map/ppermute | solution.py:675
  584.5 22.3 %copy-start.27 = (bf16[768,768]{1,0:T(8,128)(2,1)S(1)}, bf16[768,768]{1,0:T(8,128)(2,1)}, u32[]{:S(2)}) copy-start(bf16[768,768]{1,0:T(8,128)(2,1)} %all-reduce.12.cloned.1.call-done) | copy-start | bytes 3538948
  (49 other events, 192.6 us)
Sparse Core Ops, SparseCore 0:
  442.0 55.9 all-reduce.11

commit v4 on v3

v4 whole, which is shorter than its diff:
```python
import functools

import jax
import jax.numpy as jnp
from jax import lax
from jax.experimental import pallas as pl
from jax.experimental.pallas import tpu as pltpu
from jax.sharding import PartitionSpec as P

BF = jnp.bfloat16
F32 = jnp.float32
HEAD_DIM = 64
norm_epsilon = 1e-06
LIMIT = 60 << 20
ROWS = 208
HALF = ROWS // 2


def nn(a, b):
    return lax.dot_general(a, b, (((1,), (0,)), ((), ())), preferred_element_type=F32)


def nt(a, b):
    return lax.dot_general(a, b, (((1,), (1,)), ((), ())), preferred_element_type=F32)


def tn(a, b):
    return lax.dot_general(a, b, (((0,), (0,)), ((), ())), preferred_element_type=F32)


def hat_of(values):
    mean = jnp.mean(values, axis=-1, keepdims=True)
    centered = values - mean
    inv = lax.rsqrt(jnp.mean(centered * centered, axis=-1, keepdims=True) + norm_epsilon)
    return centered * inv, inv


def hat_back(hat, inv, gain, grad):
    e = grad * gain
    return inv * (
        e - jnp.mean(e, axis=-1, keepdims=True) - hat * jnp.mean(e * hat, axis=-1, keepdims=True)
    )


GROUP = 256
PER = GROUP // HEAD_DIM


def head_of_lane(rows):
    return lax.broadcasted_iota(jnp.int32, (rows, GROUP), 1) // HEAD_DIM


def stacked(v):
    lane = head_of_lane(v.shape[0])
    return jnp.concatenate([jnp.where(lane == h, v, jnp.zeros_like(v)) for h in range(PER)])


def unstacked(v):
    rows = v.shape[0] // PER
    lane = head_of_lane(rows)
    out = v[:rows]
    for h in range(1, PER):
        out = jnp.where(lane == h, v[h * rows : (h + 1) * rows], out)
    return out


def only_places(places):
    def mask(s):
        cut = places // 8 * 8
        row = lax.broadcasted_iota(jnp.int32, (s.shape[0] - cut, s.shape[1]), 0)
        return jnp.concatenate([s[:cut], jnp.where(row < places - cut, s[cut:], -1e30)])

    return mask


def same_place(bias):
    return lambda s: s + bias


def place_bias(rows):
    a = lax.broadcasted_iota(jnp.int32, (rows, PER * rows), 0) & 7
    b = lax.broadcasted_iota(jnp.int32, (rows, PER * rows), 1) & 7
    return jnp.where(a == b, 0.0, -1e30).astype(F32)


def attend(q, k, v, o, lse, mask):
    spans = [slice(a, a + GROUP) for a in range(0, q.shape[1], GROUP)]
    s = [mask(nt(k[:, at], stacked(q[:, at]))) for at in spans]
    top = [jnp.max(m, axis=0, keepdims=True) for m in s]
    ex = [jnp.exp(m - t) for m, t in zip(s, top)]
    total = [jnp.sum(m, axis=0, keepdims=True) for m in ex]
    p = [(m * (1.0 / t)).astype(BF) for m, t in zip(ex, total)]
    r = [tn(m, v[:, at]) for m, at in zip(p, spans)]
    for g, at in enumerate(spans):
        o(at, unstacked(r[g]))
        lse[g : g + 1] = top[g] + jnp.log(total[g])


def attend_back(q, k, v, do, lse, dq, dk, dv, mask):
    spans = [slice(a, a + GROUP) for a in range(0, q.shape[1], GROUP)]
    qs = [stacked(q[:, at]) for at in spans]
    dos = [stacked(do[:, at]) for at in spans]
    s = [mask(nt(k[:, at], m)) for at, m in zip(spans, qs)]
    dp = [nt(v[:, at], m) for at, m in zip(spans, dos)]
    p = [jnp.exp(m - lse[g : g + 1]) for g, m in enumerate(s)]
    row = [jnp.sum(a * b, axis=0, keepdims=True) for a, b in zip(p, dp)]
    ds = [(a * (b - t)).astype(BF) for a, b, t in zip(p, dp, row)]
    for g, at in enumerate(spans):
        dv[:, at] = nn(p[g].astype(BF), dos[g]).astype(BF)
        dk[:, at] = nn(ds[g], qs[g]).astype(BF)
    r = [tn(m, k[:, at]) for m, at in zip(ds, spans)]
    for g, at in enumerate(spans):
        dq[:, at] = (unstacked(r[g]) * HEAD_DIM**-0.5).astype(BF)


def whole(shape, index=None):
    index = (0,) * len(shape) if index is None else index
    return pl.BlockSpec(shape, lambda *_: index, pipeline_mode=pl.Buffered(1))


def cost(us):
    return pl.CostEstimate(flops=int(us * 1.1e9), bytes_accessed=int(us * 1e5), transcendentals=0)


def struct(shape, kind):
    return jax.ShapeDtypeStruct(shape, kind)


ANY = pl.BlockSpec(memory_space=pl.ANY)
MESH = pl.DeviceIdType.MESH


def call(body, name, us, ids, grid, in_specs, out_specs, out_shape, args, scratch=(), aliases=None):
    return pl.pallas_call(
        body,
        grid_spec=pltpu.PrefetchScalarGridSpec(
            num_scalar_prefetch=1,
            grid=grid,
            in_specs=in_specs,
            out_specs=out_specs,
            scratch_shapes=list(scratch),
        ),
        out_shape=out_shape,
        input_output_aliases=aliases or {},
        compiler_params=pltpu.CompilerParams(
            dimension_semantics=("arbitrary",) * len(grid), vmem_limit_bytes=LIMIT
        ),
        name=name,
        cost_estimate=cost(us),
    )(ids, *args)


def core_index():
    return lax.rem(lax.axis_index("tensor"), 2)


def joined(own, got):
    first = core_index() == 0
    a, b = own.astype(F32), got.astype(F32)
    return jnp.concatenate([jnp.where(first, a, b), jnp.where(first, b, a)], axis=-2)


def parted(v, own, send):
    first = core_index() == 0
    n = v.shape[1] // 2
    a, b = v[:, :n], v[:, n:]
    own[...] = jnp.where(first, a, b).astype(BF)
    send[...] = jnp.where(first, b, a).astype(BF)


def in_blocks(own, got, out):
    f, blocks, _, d = own.shape
    for b in range(blocks):
        both = [v[:, b].astype(F32).reshape(f * 8, d) for v in (own, got)]
        out[b] = jnp.concatenate(both).astype(BF)


def start_body(qkv, wout, bias, clips, w, far, b, own, send, recv, local):
    me_d, me_t = lax.axis_index("dp"), lax.axis_index("tensor")
    x, y = lax.rem(me_d, 2), me_t // 2
    core = (me_d, me_t + 1 - 2 * lax.rem(me_t, 2))
    over_y = (me_d, me_t + 2 - 4 * y)
    over_x = (me_d + 1 - 2 * x, me_t)
    z = lax.rem(me_d // 2, 2)
    over_z = (me_d + 2 - 4 * z, me_t)
    loads = []
    for i in range(2):
        loads.append(pltpu.make_async_copy(qkv.at[i], own.at[i, 0:3], local.at[3 * i]))
        loads.append(pltpu.make_async_copy(wout.at[i], own.at[i, 3], local.at[3 * i + 1]))
    for c in loads:
        c.start()
    barrier = pltpu.get_barrier_semaphore()
    for to in (core, over_y, over_x, over_z):
        pl.semaphore_signal(barrier, inc=1, device_id=to, device_id_type=MESH)
    pl.semaphore_wait(barrier, 4)
    count = [0]

    def copy(src, dst, to):
        k = count[0]
        count[0] += 1
        c = pltpu.make_async_remote_copy(
            src_ref=src, dst_ref=dst, send_sem=send.at[k], recv_sem=recv.at[k],
            device_id=to, device_id_type=MESH,
        )
        c.start()
        return c

    one, two = 2 * x + z, 2 * x + 1 - z
    mine, other = pl.ds(2 * x, 2), pl.ds(2 - 2 * x, 2)
    done, ys, zs, xs = [], [], [], []
    for i in range(2):
        loads[2 * i].wait()
        loads[2 * i + 1].wait()
        ys.append(copy(own.at[i, one], w.at[i, one, 2], over_y))
    done.append(copy(clips.at[1 - y], far, over_y))
    for i in range(2):
        done.append(copy(own.at[i], w.at[i, :, 1], core))
        c = pltpu.make_async_copy(own.at[i], w.at[i, :, 0], local.at[3 * i + 2])
        c.start()
        done.append(c)
    b[0] = bias[...]
    done.append(copy(b.at[0], b.at[1], core))
    by = copy(b.at[0], b.at[2], over_y)
    for i in range(2):
        ys[i].wait()
        zs.append(copy(w.at[i, one, 2], w.at[i, one, 2], over_z))
        done.append(copy(w.at[i, one, 2], w.at[i, one, 3], core))
    for i in range(2):
        zs[i].wait()
        xs.append(copy(w.at[i, mine, 2], w.at[i, mine, 2], over_x))
        done.append(copy(w.at[i, two, 2], w.at[i, two, 3], core))
    for i in range(2):
        xs[i].wait()
        done.append(copy(w.at[i, other, 2], w.at[i, other, 3], core))
    by.wait()
    done.append(copy(b.at[2], b.at[3], core))
    for c in done:
        c.wait()


def start(qkv, wout, bias, clips):
    _, _, e, d = qkv.shape
    return pl.pallas_call(
        start_body,
        in_specs=[ANY, ANY, pl.BlockSpec(memory_space=pltpu.VMEM), ANY],
        out_specs=[ANY, ANY, pl.BlockSpec(memory_space=pltpu.VMEM)],
        out_shape=[struct((2, 4, 4, e, d), BF), struct(clips.shape[1:], BF),
                   struct((4,) + bias.shape, F32)],
        scratch_shapes=[pltpu.VMEM((2, 4, e, d), BF), pltpu.SemaphoreType.DMA((20,)),
                        pltpu.SemaphoreType.DMA((20,)), pltpu.SemaphoreType.DMA((6,))],
        compiler_params=pltpu.CompilerParams(
            collective_id=1, has_side_effects=True, vmem_limit_bytes=LIMIT
        ),
        name="start",
        cost_estimate=cost(50),
    )(qkv, wout, bias, clips)


def weight(w, c):
    v = w[0, c]
    return v.reshape(v.shape[0] * v.shape[1], v.shape[2])


def spatial_body(ids, x, w, gain, shift, qv, bout, *refs):
    stream, n_own, n_send, q, k, v, o, lse, rows = refs[-9:]
    f, r, d = rows.shape
    places = x.shape[-2]

    @pl.when(pl.program_id(0) == 0)
    def _():
        rows[...] = jnp.zeros_like(rows)

    rows[:, :places] = x[...].reshape(f, places, d).astype(F32)
    xv = rows[...].reshape(f * r, d)
    n0 = (hat_of(xv)[0] * gain[0:1] + shift[0:1]).astype(BF)

    def three(m):
        return m.astype(BF).reshape(f, r, d)

    q[...] = three((nt(n0, weight(w, 0)) + qv[0:1]) * HEAD_DIM**-0.5)
    k[...] = three(nt(n0, weight(w, 1)))
    v[...] = three(nt(n0, weight(w, 2)) + qv[1:2])
    for j in range(f):

        def put(at, m, j=j):
            o[j, :, at] = m.astype(BF)

        attend(q.at[j], k.at[j], v.at[j], put, lse.at[j], only_places(places))
    s1 = xv + (nn(o[...].reshape(f * r, d), weight(w, 3)) + bout[0:1])
    stream[...] = s1.reshape(f, r, d)
    n1 = hat_of(s1)[0] * gain[1:2] + shift[1:2]
    parted(n1.reshape(f, r, d), n_own, n_send)


def tokens_spec(near, places, d):
    if near:
        return pl.BlockSpec((1, 2, places, d), lambda i, t: (t[0], i, 0, 0))
    return pl.BlockSpec((2, places, d), lambda i, t: (i, 0, 0))


def spatial(ids, x, w, gain, shift, qv, bout, near, before=()):
    n, places, d = x.shape[-3:]
    steps, frames = n // 2, 2 * n
    begin = 0 if near else steps
    blk = pl.BlockSpec((2, ROWS, d), lambda i, t: (i + begin, 0, 0))
    part = pl.BlockSpec((2, HALF, d), lambda i, t: (i + begin, 0, 0))
    return call(
        spatial_body, "spatial", 12, ids, (steps,),
        [tokens_spec(near, places, d), whole((1,) + w.shape[1:]), whole(gain.shape),
         whole(shift.shape), whole(qv.shape), whole(bout.shape)] + [ANY] * len(before),
        [blk, part, part] + [blk] * 4
        + [pl.BlockSpec((2, d // GROUP, PER * ROWS), lambda i, t: (i + begin, 0, 0))],
        [struct((frames, ROWS, d), F32)] + [struct((frames, HALF, d), BF)] * 2
        + [struct((frames, ROWS, d), BF)] * 4
        + [struct((frames, d // GROUP, PER * ROWS), F32)],
        (x, w, gain, shift, qv, bout) + tuple(before),
        [pltpu.VMEM((2, ROWS, d), F32)],
        {7 + i: i for i in range(len(before))},
    )


def temporal_body(ids, own, got, w, qv, n, q, k, v, o, o_own, o_send, lse):
    i = pl.program_id(0)
    b, r, d = n.shape
    f = own.shape[0]

    @pl.when(i == 0)
    def _():
        in_blocks(own, got, n)
        step = b * r // 4
        ws = [weight(w, c) for c in range(3)]
        for c in range(4):
            at = slice(c * step, (c + 1) * step)
            t = n[...].reshape(b * r, d)[at]
            q[at] = ((nt(t, ws[0]) + qv[2:3]) * HEAD_DIM**-0.5).astype(BF)
            k[at] = nt(t, ws[1]).astype(BF)
            v[at] = (nt(t, ws[2]) + qv[3:4]).astype(BF)

    at = pl.ds(pl.multiple_of(i * r, r), r)

    def put(lanes, m):
        o[0, :, lanes] = m.astype(BF)
        m = m.reshape(2 * f, 1, 8, GROUP)
        o_own[:, :, :, lanes] = m[:f].astype(BF)
        o_send[:, :, :, lanes] = m[f:].astype(BF)

    attend(q.at[at], k.at[at], v.at[at], put, lse.at[0], same_place(place_bias(r)))


def temporal(ids, own, got, w, qv):
    f, half, d = own.shape
    b, r = half // 8, 16 * f
    own, got = own.reshape(f, b, 8, d), got.reshape(f, b, 8, d)
    part = pl.BlockSpec((f, 1, 8, d), lambda i, t: (0, i, 0, 0))
    res = call(
        temporal_body, "temporal", 22, ids, (b,),
        [whole(own.shape), whole(got.shape), whole((1,) + w.shape[1:], (1, 0, 0, 0, 0)),
         whole(qv.shape)],
        [whole((b, r, d))] + [whole((b * r, d))] * 3
        + [pl.BlockSpec((1, r, d), lambda i, t: (i, 0, 0)), part, part,
           pl.BlockSpec((1, d // GROUP, PER * r), lambda i, t: (i, 0, 0))],
        [struct((b, r, d), BF)] + [struct((b * r, d), BF)] * 3 + [struct((b, r, d), BF)]
        + [struct(own.shape, BF)] * 2 + [struct((b, d // GROUP, PER * r), F32)],
        (own, got, w, qv),
    )
    n, q, k, v, o, o_own, o_send, lse = res
    return n, q, k, v, o, o_own.reshape(f, half, d), o_send.reshape(f, half, d), lse


def temporal_back_body(ids, own, got, q, k, v, lse, w, g, dn_own, dn_send, dqkv, do):
    i = pl.program_id(0)
    b, r, d = g.shape
    f = own.shape[0]

    @pl.when(i == 0)
    def _():
        in_blocks(own, got, g)
        wo = weight(w, 3)
        step = b * r // 4
        for c in range(4):
            at = slice(c * step, (c + 1) * step)
            do[at] = nt(g[...].reshape(b * r, d)[at], wo).astype(BF)

    at = pl.ds(pl.multiple_of(i * r, r), r)
    attend_back(
        q, k, v, do.at[at], lse.at[0],
        dqkv.at[0, at], dqkv.at[1, at], dqkv.at[2, at], same_place(place_bias(r)),
    )

    @pl.when(i == pl.num_programs(0) - 1)
    def _():
        ws = [weight(w, c) for c in range(3)]
        acc = nn(dqkv[0], ws[0]) + nn(dqkv[1], ws[1]) + nn(dqkv[2], ws[2])
        for s in range(b):
            m = acc[s * r : (s + 1) * r].reshape(2 * f, 8, d).astype(BF)
            dn_own[:, s] = m[:f]
            dn_send[:, s] = m[f:]


def temporal_back(ids, own, got, q, k, v, lse, w):
    f, half, d = own.shape
    b, r = half // 8, 16 * f
    own, got = own.reshape(f, b, 8, d), got.reshape(f, b, 8, d)
    res = call(
        temporal_back_body, "temporal_back", 34, ids, (b,),
        [whole(own.shape), whole(got.shape)]
        + [pl.BlockSpec((r, d), lambda i, t: (i, 0))] * 3
        + [pl.BlockSpec((1, d // GROUP, PER * r), lambda i, t: (i, 0, 0)),
           whole((1,) + w.shape[1:], (1, 0, 0, 0, 0))],
        [whole((b, r, d)), whole(own.shape), whole(own.shape), whole((3, b * r, d))],
        [struct((b, r, d), BF), struct(own.shape, BF), struct(own.shape, BF),
         struct((3, b * r, d), BF)],
        (own, got, q, k, v, lse, w),
        [pltpu.VMEM((b * r, d), BF)],
    )
    g, dn_own, dn_send, dqkv = res
    return g, dn_own.reshape(f, half, d), dn_send.reshape(f, half, d), dqkv


def weight_grads_body(ids, dqkv, o_in, n, g_in, send, keep, sums, o, g, sem):
    c = pl.program_id(0)

    def loads():
        return [pltpu.make_async_copy(a, b, sem.at[z])
                for z, (a, b) in enumerate(((o_in, o), (g_in, g)))]

    @pl.when(c == 0)
    def _():
        for v in loads():
            v.start()

    d = n.shape[1]
    e = d // 4

    def put(m):
        m = m.astype(BF)
        for r in range(4):
            to = send if r % 2 else keep
            to[r // 2, 0] = m[r * e : (r + 1) * e]

    @pl.when(c < 3)
    def _():
        v = dqkv[0]
        put(tn(v, n[...]))
        sums[0] = jnp.sum(v.astype(F32), axis=0, keepdims=True)

    @pl.when(c == 3)
    def _():
        for v in loads():
            v.wait()
        put(tn(o[...], g[...]))
        sums[0] = jnp.zeros_like(sums[0])


def weight_grads(ids, dqkv, o, n, g):
    d = n.shape[-1]
    rows = n.size // d
    dqkv = dqkv.reshape(3, rows, d)
    o, n, g = (v.reshape(rows, d) for v in (o, n, g))
    out = pl.BlockSpec((2, 1, d // 4, d), lambda c, t: (0, c, 0, 0))
    return call(
        weight_grads_body, "weight_grads", 13, ids, (4,),
        [pl.BlockSpec((1, rows, d), lambda c, t: (jnp.minimum(c, 2), 0, 0))]
        + [ANY, whole((rows, d)), ANY],
        [out, out, pl.BlockSpec((1, 1, d), lambda c, t: (c, 0, 0))],
        [struct((2, 4, d // 4, d), BF)] * 2 + [struct((4, 1, d), F32)],
        (dqkv, o, n, g),
        [pltpu.VMEM((rows, d), BF), pltpu.VMEM((rows, d), BF), pltpu.SemaphoreType.DMA((2,))],
    )


def spatial_back_body(ids, x, s1, dn_own, dn_got, g2, q, k, v, lse, w, gain, shift, *refs):
    g0, sums, dqkv, n0, gb, rows, do = refs[-7:]
    i = pl.program_id(0)
    f, r, d = rows.shape
    places = x.shape[-2]

    @pl.when(i == 0)
    def _():
        sums[...] = jnp.zeros_like(sums)
        rows[...] = jnp.zeros_like(rows)

    def add(at, val):
        sums[at : at + 1] += jnp.sum(val, axis=0, keepdims=True)

    def three(m):
        return m.reshape(f, r, d)

    hat, inv = hat_of(s1[...].reshape(f * r, d))
    dn = joined(dn_own[...], dn_got[...]).reshape(f * r, d)
    add(2, dn * hat)
    add(3, dn)
    g1 = g2[...].reshape(f * r, d) + hat_back(hat, inv, gain[1:2], dn)
    add(4, g1)
    gv = g1.astype(BF)
    gb[...] = three(gv)
    do[...] = three(nt(gv, weight(w, 3)).astype(BF))
    for j in range(f):
        attend_back(
            q.at[j], k.at[j], v.at[j], do.at[j], lse.at[j],
            dqkv.at[0, j], dqkv.at[1, j], dqkv.at[2, j], only_places(places),
        )
    rows[:, :places] = x[...].reshape(f, places, d).astype(F32)
    hat, inv = hat_of(rows[...].reshape(f * r, d))
    n0[...] = three((hat * gain[0:1] + shift[0:1]).astype(BF))
    dn = nn(dqkv[0].reshape(f * r, d), weight(w, 0))
    dn += nn(dqkv[1].reshape(f * r, d), weight(w, 1))
    dn += nn(dqkv[2].reshape(f * r, d), weight(w, 2))
    add(0, dn * hat)
    add(1, dn)
    out = three(g1 + hat_back(hat, inv, gain[0:1], dn))
    g0[...] = out[:, : g0.shape[1]].astype(g0.dtype)


def spatial_back(ids, x, s1, dn_own, dn_got, g2, q, k, v, lse, w, gain, shift, near, before=()):
    frames, _, d = s1.shape
    places = x.shape[-2]
    steps = frames // 4
    begin = 0 if near else steps
    blk = pl.BlockSpec((2, ROWS, d), lambda i, t: (i + begin, 0, 0))
    part = pl.BlockSpec((2, HALF, d), lambda i, t: (i + begin, 0, 0))
    size = places if near else ROWS
    out = pl.BlockSpec((2, size, d), lambda i, t: (i, 0, 0))
    big = struct((frames, ROWS, d), BF)
    return call(
        spatial_back_body, "spatial_back", 20, ids, (steps,),
        [tokens_spec(near, places, d), blk, part, part] + [blk] * 4
        + [pl.BlockSpec((2, d // GROUP, PER * ROWS), lambda i, t: (i + begin, 0, 0)),
           whole((1,) + w.shape[1:]), whole(gain.shape), whole(shift.shape)] + [ANY] * len(before),
        [out, whole((8, d)),
         pl.BlockSpec((3, 2, ROWS, d), lambda i, t: (0, i + begin, 0, 0)), blk, blk],
        [struct((frames // 2, size, d), F32 if near else BF), struct((8, d), F32),
         struct((3, frames, ROWS, d), BF), big, big],
        (x, s1, dn_own, dn_got, g2, q, k, v, lse, w, gain, shift) + tuple(before),
        [pltpu.VMEM((2, ROWS, d), F32), pltpu.VMEM((2, ROWS, d), BF)],
        {13 + i: 2 + i for i in range(len(before))},
    )


def gelu_parts(u):
    cdf = 0.5 + 0.5 * lax.erf(u * 0.7071067811865476)
    return u * cdf, cdf + u * (jnp.exp(-0.5 * u * u) * 0.3989422804014327)


def mlp_load(parts, wt, wd, sem):
    a, b, ct, cd = parts
    x = lax.rem(lax.axis_index("dp"), 2)
    h = a.shape[0] // 2
    mine = pl.ds(pl.multiple_of(x * h, h), h)
    other = pl.ds(pl.multiple_of((1 - x) * h, h), h)
    copies = []
    for z, (w, c) in enumerate(((wt, ct), (wd, cd))):
        rows = pl.ds(z * h, h)
        copies.append(pltpu.make_async_copy(a.at[rows], w.at[0, mine], sem.at[3 * z]))
        copies.append(pltpu.make_async_copy(b.at[rows], w.at[0, other], sem.at[3 * z + 1]))
        copies.append(pltpu.make_async_copy(c, w.at[1], sem.at[3 * z + 2]))
    return copies


def mlp_tile(n2, gb, wt, wd, b, h_s, dr_s):
    u = nt(n2, wt) + b
    dh = nt(gb, wd)
    h, slope = gelu_parts(u)
    h = h.astype(BF)
    h_s[...] = h
    dr = (dh * slope).astype(BF)
    dr_s[...] = dr
    return nn(h, wd), nn(dr, wt)


def mlp_grads(s, n2, gb, h, dr, gwt, gwd, gbi):
    gwt[s] = tn(dr, n2).astype(BF)
    gwd[s] = tn(h, gb).astype(BF)
    gbi[s] = jnp.sum(dr.astype(F32), axis=0, keepdims=True)


def mlp_first_body(ids, s1, o_own, o_got, near, far, w, b, bout, gain, shift, *refs):
    parts = refs[:4]
    (s2, n2, gb, branch, dn, gwt, gwd, gbi,
     n2s, gbs, hs, drs, brs, dns, wt, wd, sem) = refs[4:]
    s, i = pl.program_id(0), pl.program_id(1)
    tile, d = n2.shape
    steps = n2s.shape[0]

    @pl.when((i == 0) & (s == 0))
    def _():
        for c in mlp_load(parts, wt, wd, sem):
            c.start()

    @pl.when(s == 0)
    def _():
        @pl.when(i < steps // 2)
        def _():
            gb[...] = near[...].reshape(tile, d)

        @pl.when(i >= steps // 2)
        def _():
            gb[...] = far[...].reshape(tile, d)

        f, n, _ = o_own.shape

        def flat(v):
            return v[...].astype(F32).reshape(f * n, d).astype(BF)

        wo = w[0, 3]
        turned = jnp.concatenate([wo[r] for r in (1, 0, 3, 2)])
        own = nn(flat(o_own), wo.reshape(d, d)).reshape(f, n, d)
        got = nn(flat(o_got), turned).reshape(f, n, d)
        v = s1[...] + (joined(own, got).reshape(s1.shape) + bout[1:2])
        s2[...] = v
        n = (hat_of(v)[0] * gain[2:3] + shift[2:3]).astype(BF)
        n2[...] = n
        n2s[i] = n
        gbs[i] = gb[...]

    @pl.when((i == 0) & (s == 0))
    def _():
        for c in mlp_load(parts, wt, wd, sem):
            c.wait()

    br, dv = mlp_tile(
        n2s[i], gbs[i], wt[s], wd[s], b[3 - 2 * s, 1:2], hs.at[i], drs.at[i]
    )

    @pl.when(s == 0)
    def _():
        brs[i] = br
        dns[i] = dv

    @pl.when(s == 1)
    def _():
        branch[...] = brs[i] + br
        dn[...] = dns[i] + dv

    @pl.when(i == steps - 1)
    def _():
        rows = steps * tile
        mlp_grads(s, *(v[...].reshape(rows, d) for v in (n2s, gbs, hs, drs)), gwt, gwd, gbi)


def mlp_scratch(steps, tile, d, h):
    return [pltpu.VMEM((steps, tile, d), BF), pltpu.VMEM((steps, tile, d), BF),
            pltpu.VMEM((steps, tile, h), BF), pltpu.VMEM((steps, tile, h), BF),
            pltpu.VMEM((steps, tile, d), F32), pltpu.VMEM((steps, tile, d), F32),
            pltpu.VMEM((2, h, d), BF), pltpu.VMEM((2, h, d), BF), pltpu.SemaphoreType.DMA((6,))]


def mlp_first(ids, s1, o_own, o_got, cot, far, w, b, bout, gain, shift, parts):
    frames, _, d = s1.shape
    tile = 2 * ROWS
    steps = frames // 2
    half = steps // 2
    rows = frames * ROWS
    h = parts[2].shape[0]

    def early(s, i):
        return jnp.where(s == 0, i, steps - 1)

    blk = pl.BlockSpec((tile, d), lambda s, i, t: (early(s, i), 0))
    part = pl.BlockSpec((2, HALF, d), lambda s, i, t: (early(s, i), 0, 0))
    late = pl.BlockSpec((tile, d), lambda s, i, t: (jnp.where(s == 0, 0, i), 0))
    return call(
        mlp_first_body, "mlp_first", 33, ids, (2, steps),
        [blk, part, part,
         pl.BlockSpec((2, ROWS, d), lambda s, i, t: (jnp.minimum(early(s, i), half - 1), 0, 0)),
         pl.BlockSpec((2, ROWS, d), lambda s, i, t: (jnp.maximum(early(s, i) - half, 0), 0, 0)),
         whole((1, 4) + w.shape[2:], (1, 0, 0, 0, 0)), whole(b.shape), whole(bout.shape),
         whole(gain.shape), whole(shift.shape)] + [ANY] * 4,
        [blk] * 3 + [late] * 2 + [whole((2, h, d)), whole((2, h, d)), whole((2, 1, h))],
        [struct((rows, d), F32), struct((rows, d), BF), struct((rows, d), BF),
         struct((rows, d), F32), struct((rows, d), F32), struct((2, h, d), BF),
         struct((2, h, d), BF), struct((2, 1, h), F32)],
        (s1.reshape(rows, d), o_own, o_got, cot, far, w, b, bout, gain, shift) + tuple(parts),
        mlp_scratch(steps, tile, d, h),
    )


def mlp_second_body(ids, s2, n2, gb, br0, dn0, b, bdown, gain, *refs):
    parts = refs[:4]
    (near, far, g2, g_own, g_send, gwt, gwd, gbi, sums,
     n2s, gbs, hs, drs, brs, dns, wt, wd, sem) = refs[4:]
    s, i = pl.program_id(0), pl.program_id(1)
    tile, d = n2.shape
    steps = n2s.shape[0]

    @pl.when((i == 0) & (s == 0))
    def _():
        sums[...] = jnp.zeros_like(sums)
        for c in mlp_load(parts, wt, wd, sem):
            c.start()

    @pl.when(s == 0)
    def _():
        n2s[i] = n2[...]
        gbs[i] = gb[...]

    @pl.when((i == 0) & (s == 0))
    def _():
        for c in mlp_load(parts, wt, wd, sem):
            c.wait()

    br, dv = mlp_tile(
        n2s[i], gbs[i], wt[s], wd[s], b[2 - 2 * s, 1:2], hs.at[i], drs.at[i]
    )

    @pl.when(s == 0)
    def _():
        brs[i] = br0[...] + br
        dns[i] = dn0[...] + dv

    @pl.when(i == steps - 1)
    def _():
        rows = steps * tile
        mlp_grads(s, *(v[...].reshape(rows, d) for v in (n2s, gbs, hs, drs)), gwt, gwd, gbi)

    @pl.when(s == 1)
    def _():
        def add(at, val):
            sums[at : at + 1] += jnp.sum(val, axis=0, keepdims=True)

        v = s2[...]
        f, places, _ = near.shape
        out = (v + (brs[i] + br + bdown[...])).reshape(f, ROWS, d)

        @pl.when(i < steps // 2)
        def _():
            near[...] = out[:, :places]

        @pl.when(i >= steps // 2)
        def _():
            far[...] = out.astype(BF)

        hat, inv = hat_of(v)
        dt = dns[i] + dv
        add(0, dt * hat)
        add(1, dt)
        g3 = gbs[i].astype(F32)
        add(3, g3)
        g = g3 + hat_back(hat, inv, gain[2:3], dt)
        add(2, g)
        g = g.reshape(f, ROWS, d)
        g2[...] = g
        parted(g, g_own, g_send)


def mlp_second(ids, s2, n2, gb, br0, dn0, b, bdown, gain, parts, shape):
    rows, d = s2.shape
    _, n, places, _ = shape
    frames = rows // ROWS
    steps = frames // 2
    half = steps // 2
    tile = 2 * ROWS
    h = parts[2].shape[0]

    def late(s, i):
        return jnp.where(s == 0, 0, i)

    blk = pl.BlockSpec((tile, d), lambda s, i, t: (jnp.where(s == 0, i, steps - 1), 0))
    end = pl.BlockSpec((tile, d), lambda s, i, t: (late(s, i), 0))
    three = pl.BlockSpec((2, ROWS, d), lambda s, i, t: (late(s, i), 0, 0))
    part = pl.BlockSpec((2, HALF, d), lambda s, i, t: (late(s, i), 0, 0))
    return call(
        mlp_second_body, "mlp_second", 33, ids, (2, steps),
        [end] + [blk] * 4 + [whole(b.shape), whole(bdown.shape), whole(gain.shape)] + [ANY] * 4,
        [pl.BlockSpec((2, places, d), lambda s, i, t: (jnp.minimum(late(s, i), half - 1), 0, 0)),
         pl.BlockSpec((2, ROWS, d), lambda s, i, t: (jnp.maximum(late(s, i) - half, 0), 0, 0)),
         three, part, part, whole((2, h, d)), whole((2, h, d)), whole((2, 1, h)), whole((8, d))],
        [struct((n, places, d), F32), struct((n, ROWS, d), BF), struct((frames, ROWS, d), F32),
         struct((frames, HALF, d), BF), struct((frames, HALF, d), BF), struct((2, h, d), BF),
         struct((2, h, d), BF), struct((2, 1, h), F32), struct((8, d), F32)],
        (s2, n2, gb, br0, dn0, b, bdown, gain) + tuple(parts),
        mlp_scratch(steps, tile, d, h),
    )


def both_clips_body(ids, near, got, out):
    mine = pl.program_id(0) == ids[0]
    f, places, _ = near.shape

    @pl.when(mine)
    def _():
        for j in range(f):
            out[0, :, j] = near[j]

    @pl.when(jnp.logical_not(mine))
    def _():
        for j in range(f):
            out[0, :, j] = got[j, :places].astype(F32)


def both_clips(ids, near, got):
    n, places, d = near.shape
    out = call(
        both_clips_body, "both_clips", 6, ids, (2,),
        [whole(near.shape), whole(got.shape)],
        pl.BlockSpec((1, places, n, d), lambda i, t: (i, 0, 0, 0)),
        struct((2, places, n, d), F32),
        (near, got),
    )
    return out.transpose(0, 2, 1, 3)


def shape_body(ids, f0, f1, m, mo, gqkv, gout, gwin, gwd):
    x = lax.rem(lax.axis_index("dp"), 2)
    for i, f in enumerate((f0, f1)):
        for c in range(3):
            gqkv[i, c] = f[c].astype(F32)
        gout[i] = f[3].astype(F32)
    n = m.shape[0] // 2
    lo = jnp.where(x == 0, m[...], mo[...]).astype(F32)
    hi = jnp.where(x == 0, mo[...], m[...]).astype(F32)
    gwin[:, :n] = lo[:n].T
    gwin[:, n:] = hi[:n].T
    gwd[:n] = lo[n:]
    gwd[n:] = hi[n:]


def to_results(ids, f0, f1, m, mo):
    _, e, d = f0.shape
    h = m.shape[0]
    shapes = [(2, 3, e, d), (2, e, d), (d, h), (h, d)]
    return call(
        shape_body, "to_results", 5, ids, (1,),
        [whole(v.shape) for v in (f0, f1, m, mo)],
        [whole(v) for v in shapes],
        [struct(v, F32) for v in shapes],
        (f0, f1, m, mo),
    )


def finish_body(dp, t0, t1, rel, rep, f0, f1, rel_o, rep_o, *scratch):
    (tt, zr, ta, tb, aa, ab, xs, rel_r, rep_r, rel_s, rep_s, send, recv) = scratch
    me_d, me_t = lax.axis_index("dp"), lax.axis_index("tensor")
    x = lax.rem(me_d, 2)
    bits = []
    bit = 2
    while bit < dp:
        bits.append(bit)
        bit *= 2

    def flip(v, b):
        return v + b - 2 * b * lax.rem(v // b, 2)

    def core():
        return (me_d, flip(me_t, 1))

    def over_y():
        return (me_d, flip(me_t, 2))

    def over_d(b):
        return (flip(me_d, b), me_t)

    partners = [core(), over_y(), over_d(1)] + [over_d(b) for b in bits]
    barrier = pltpu.get_barrier_semaphore()
    for p in partners:
        pl.semaphore_signal(barrier, inc=1, device_id=p, device_id_type=pl.DeviceIdType.MESH)
    pl.semaphore_wait(barrier, len(partners))

    count = [0]

    def copy(src, dst, to):
        k = count[0]
        count[0] += 1
        c = pltpu.make_async_remote_copy(
            src_ref=src, dst_ref=dst, send_sem=send.at[k], recv_sem=recv.at[k],
            device_id=to, device_id_type=pl.DeviceIdType.MESH,
        )
        c.start()
        return c

    def plus(a, b):
        return (a.astype(F32) + b.astype(F32)).astype(BF)

    n = tt.shape[1]

    def rest(k, out):
        size, held = n, tt.at[k]
        done = []
        for z, b in enumerate(bits[:2]):
            half = size // 2
            bitv = lax.rem(me_d // b, 2)
            mine = pl.multiple_of(bitv * half, 16)
            other = pl.multiple_of((1 - bitv) * half, 16)
            dst = zr.at[k, z, pl.ds(0, half)]
            c = copy(held.at[pl.ds(other, half)], dst, over_d(b))
            yield
            c.wait()
            nxt = (ta if z == 0 else tb).at[k]
            nxt[...] = plus(held[pl.ds(mine, half)], dst[...])
            done.append(((aa if z == 0 else ab).at[k], mine, half, b))
            size, held = half, nxt
        for z, b in enumerate(bits[2:]):
            dst = zr.at[k, 2 + z, pl.ds(0, size)]
            c = copy(held, dst, over_d(b))
            yield
            c.wait()
            held[...] = plus(held[...], dst[...])
        for z, (up, mine, half, b) in enumerate(reversed(done)):
            up[pl.ds(mine, half)] = held[...]
            c = copy(up.at[pl.ds(mine, half)], up.at[pl.ds(mine, half)], over_d(b))
            yield
            c.wait()
            held = up
        c = copy(held, xs.at[k, 0], over_d(1))
        yield
        c.wait()
        out(held, xs.at[k, 0])

    def attn0(j):
        tt[j] = t0[j]

        def out(mine, got):
            f0[j + 2 * x] = mine[...]
            f0[j + 2 * (1 - x)] = got[...]

        yield from rest(j, out)

    def attn1():
        c = copy(t1, xs.at[2], over_d(1))
        f1[pl.ds(2 * x, 2)] = t1[...]
        yield
        yield
        yield
        c.wait()
        f1[pl.ds(2 - 2 * x, 2)] = xs[2]

    def small():
        rel_s[...] = rel[...]
        rep_s[...] = rep[...]
        for z, (to, b) in enumerate([(core(), 1), (over_y(), 2)]):
            c = [copy(rel_s, rel_r.at[z], to), copy(rep_s, rep_r.at[z], to)]
            yield
            for v in c:
                v.wait()
            rep_s[...] += rep_r[z]
            for r in range(4):
                rel_s[r] = rel_s[r] + rel_r[z, r ^ b]
        for z, b in enumerate([1] + bits):
            c = [
                copy(rel_s.at[0], rel_r.at[2 + z, 0], over_d(b)),
                copy(rep_s, rep_r.at[2 + z], over_d(b)),
            ]
            yield
            for v in c:
                v.wait()
            rep_s[...] += rep_r[2 + z]
            rel_s[0] = rel_s[0] + rel_r[2 + z, 0]
        rel_o[...] = rel_s[0]
        rep_o[...] = rep_s[...]

    chains = [attn0(0), attn0(1), attn1(), small()]
    while chains:
        left = []
        for chain in chains:
            try:
                next(chain)
                left.append(chain)
            except StopIteration:
                pass
        chains = left


def finish(t0, t1, rel, rep, dp):
    _, n, d = t0.shape
    nb = max(dp.bit_length() - 2, 0)
    vm = pl.BlockSpec(memory_space=pltpu.VMEM)
    return pl.pallas_call(
        functools.partial(finish_body, dp),
        in_specs=[vm] * 4,
        out_specs=[vm] * 4,
        out_shape=[struct((4, n, d), BF)] * 2 + [struct(rel.shape[1:], F32), struct(rep.shape, F32)],
        scratch_shapes=[
            pltpu.VMEM((2, n, d), BF),
            pltpu.VMEM((2, max(nb, 1), n // 2, d), BF),
            pltpu.VMEM((2, n // 2, d), BF),
            pltpu.VMEM((2, n // 4, d), BF),
            pltpu.VMEM((2, n, d), BF),
            pltpu.VMEM((2, n // 2, d), BF),
            pltpu.VMEM((3, 2, n, d), BF),
            pltpu.VMEM((3 + nb,) + rel.shape, F32),
            pltpu.VMEM((3 + nb,) + rep.shape, F32),
            pltpu.VMEM(rel.shape, F32),
            pltpu.VMEM(rep.shape, F32),
            pltpu.SemaphoreType.DMA((96,)),
            pltpu.SemaphoreType.DMA((96,)),
        ],
        compiler_params=pltpu.CompilerParams(
            collective_id=0, has_side_effects=True, vmem_limit_bytes=LIMIT
        ),
        name="finish",
        cost_estimate=cost(40),
    )(t0, t1, rel, rep)


def shards(clips, cot, gain, shift, qkv, qvb, wout, bout, win, b_in, wdown, bdown):
    tensor = lax.axis_index("tensor")
    y = tensor // 2
    x = lax.axis_index("dp") % 2
    dp = lax.axis_size("dp")
    width = clips.shape[-1]
    e = qkv.shape[-1]
    h = win.shape[1] // 2
    ids = y.reshape(1).astype(jnp.int32)

    def over_tensor(v, bit):
        return lax.ppermute(v, "tensor", [(i, i ^ bit) for i in range(4)])

    def over_dp(v, bit):
        return lax.ppermute(v, "dp", [(i, i ^ bit) for i in range(dp)])

    def after(v, *others):
        return lax.optimization_barrier((v,) + others)[0]

    def pick(v, axis):
        n = v.shape[axis] // 2
        return (
            lax.dynamic_slice_in_dim(v, x * n, n, axis),
            lax.dynamic_slice_in_dim(v, (1 - x) * n, n, axis),
        )

    def padded(v):
        return jnp.pad(v, ((0, 0), (0, ROWS - v.shape[1]), (0, 0)))

    bias = jnp.concatenate([qvb.reshape(1, -1), b_in.reshape(1, -1), jnp.zeros((6, width), F32)])
    w, clips_far, b = start(qkv.transpose(0, 1, 3, 2), wout, bias, clips)
    win_t = win.T
    z = lax.axis_index("dp") // 2 % 2
    n = h // 2
    at = x * h + z * n
    sent = [jnp.concatenate([lax.dynamic_slice_in_dim(v, at, n, 0) for v in (win_t, wdown)])]
    sent.append(padded(lax.dynamic_index_in_dim(cot, 1 - y, 0, False)))
    w, *sent = lax.optimization_barrier((w, *sent))
    m_q = over_tensor(sent[0], 2)
    cot_far = over_tensor(sent[1], 2)
    m_c = [over_tensor(after(v, w), 1) for v in (win_t, wdown)]
    qv = b[:, 0].reshape(4, 4, e).transpose(1, 0, 2).reshape(4, width)

    some = spatial(ids, clips, w, gain, shift, qv, bout, True)
    clips_far, m_q = lax.optimization_barrier((clips_far, m_q))
    m_z = over_dp(m_q, 2)
    s1, n_own, n_send, q0, k0, v0, o0, lse0 = spatial(
        ids, clips_far, w, gain, shift, qv, bout, False, some
    )
    n_own, m_z = lax.optimization_barrier((n_own, m_z))
    m_a, m_b = jnp.where(z == 0, m_q, m_z), jnp.where(z == 0, m_z, m_q)
    m_y = jnp.concatenate([m_a[:n], m_b[:n], m_a[n:], m_b[n:]])
    m_x = over_dp(m_y, 1)
    m_cy = over_tensor(m_y, 1)
    n1p, q1, k1, v1, o1p, o_own, o_send, lse1 = temporal(
        ids, n_own, over_tensor(n_send, 1), w, qv
    )
    m_cx = over_tensor(m_x, 1)
    cot_near = padded(lax.dynamic_index_in_dim(after(cot, w), y, 0, False))

    first = (m_cy, m_cx, m_c[0], m_c[1])
    second = (m_y, m_x, win_t, wdown)
    s2, n2, gb3, branch, dn2, gwt_a, gwd_a, gb_a = mlp_first(
        ids, s1, o_own, over_tensor(o_send, 1), cot_near, cot_far, w, b, bout, gain, shift, first
    )
    out_near, far, g2, g_own, g_send, gwt_b, gwd_b, gb_b, sums2 = mlp_second(
        ids, s2, n2, gb3, branch, dn2, b, bdown[None], gain, second, clips.shape
    )

    g_got = over_tensor(g_send, 1)
    keep_t = gwt_b + over_tensor(gwt_a, 1)
    keep_d = gwd_b + over_tensor(gwd_a, 1)
    g_got, keep_t, keep_d = lax.optimization_barrier((g_got, keep_t, keep_d))
    got_t = over_tensor(keep_t[0], 2)
    mine_d, send_d = pick(keep_d, 1)
    got_d = over_dp(send_d, 1)
    out_got = over_tensor(after(far, got_t), 2)

    g2p, dn_own, dn_send, dqkv1 = temporal_back(ids, g_own, g_got, q1, k1, v1, lse1, w)
    dn_got = over_tensor(dn_send, 1)
    mine_t, send_t = pick(keep_t[1] + got_t, 0)
    mine_d = mine_d + got_d
    g2p, mine_t, send_t, mine_d = lax.optimization_barrier((g2p, mine_t, send_t, mine_d))
    got_t = over_dp(send_t, 1)
    got_d = over_tensor(mine_d[0], 2)
    gs1, gk1, sums1 = weight_grads(ids, dqkv1, o1p, n1p, g2p)
    mlp_sum = jnp.concatenate([mine_t + got_t, mine_d[1] + got_d])
    dn_got, gs1, mlp_sum = lax.optimization_barrier((dn_got, gs1, mlp_sum))
    groups = [[i for i in range(dp) if i % 2 == p] for p in range(2)]
    if dp > 2:
        mlp_sum = lax.psum(mlp_sum, "dp", axis_index_groups=groups)
    got1 = over_tensor(gs1, 1)
    kept = (s1, dn_own, dn_got, g2, q0, k0, v0, lse0, w, gain, shift)
    g0_far, sums_f, *rest = spatial_back(ids, clips_far, *kept, False)
    mine1, send1 = pick(gk1 + got1, 1)
    rest[0], mine1, send1, out_got = lax.optimization_barrier((rest[0], mine1, send1, out_got))
    got_x = over_dp(send1[0], 1)
    got_y = over_tensor(mine1[1], 2)
    got_xy = lax.ppermute(
        send1[1], ("dp", "tensor"), [(i, ((i // 4) ^ 1) * 4 + (i % 4 ^ 2)) for i in range(4 * dp)]
    )
    grad_near, sums_n, dqkv0, n0, gb0 = spatial_back(ids, clips, *kept, True, rest)
    t1 = (mine1[0] + got_x) + (got_y + got_xy)
    gb0, t1, mlp_sum = lax.optimization_barrier((gb0, t1, mlp_sum))
    gs0, gk0, sums_b = weight_grads(ids, dqkv0, o0, n0, gb0)

    bits = [1 << k for k in range(1, dp.bit_length() - 1)]
    z1 = over_dp(t1, bits[0]) if bits else jnp.zeros_like(t1)
    gs0, gk0, z1 = lax.optimization_barrier((gs0, gk0, z1))
    t1 = t1 + z1
    for bit in bits[1:]:
        t1 = t1 + over_dp(t1, bit)
    got0 = over_tensor(gs0, 1)
    output = both_clips(ids, out_near, after(out_got, gs0))
    keep0 = (gk0 + got0).reshape(2, 2, 2, e, width)
    mine0, send0 = (v[:, 0] for v in pick(keep0, 1))
    got_y = over_tensor(jnp.stack([mine0[1, 0], send0[1, 0]]), 2)
    got_x = over_dp(send0[:, 1], 1)
    mlp_got = over_dp(mlp_sum, 1)
    output, got_y, got_x, t1 = lax.optimization_barrier((output, got_y, got_x, t1))
    in_got = over_tensor(after(g0_far, got_y), 2)
    got_a = over_dp(send0[0, 0] + got_y[1], 1)
    got_b = over_tensor(mine0[1, 1] + got_x[1], 2)
    t0 = jnp.stack([mine0[0, 0] + got_y[0] + got_a, mine0[0, 1] + got_x[0] + got_b])
    sums0 = sums_f + sums_n
    rep = jnp.stack(
        [sums0[0], sums0[2], sums2[0], sums0[1], sums0[3], sums2[1], sums0[4], sums2[2], sums2[3]]
    )
    rep = jnp.pad(rep, ((0, 7), (0, 0)))
    qvs = jnp.stack([sums_b[0, 0], sums_b[2, 0], sums1[0, 0], sums1[2, 0]])
    qvs = qvs.reshape(4, 4, e).transpose(1, 0, 2).reshape(4, 1, 4 * e)
    hid = jnp.stack([gb_b[1], gb_a[1], gb_b[0], gb_a[0]])
    rel = jnp.concatenate([qvs, hid, jnp.zeros((4, 6, width), F32)], axis=1)
    f0, f1, rel, rep = finish(t0, t1, rel, rep, dp)
    input_grad = both_clips(ids, grad_near, after(in_got, f0))
    gqkv, gout, gwin, gwd = to_results(ids, f0, f1, mlp_sum, mlp_got)
    gqkv = gqkv.transpose(0, 1, 3, 2)
    return (
        output,
        input_grad,
        rep[0:3],
        rep[3:6],
        gqkv,
        rel[0].reshape(2, 2, e),
        gout,
        rep[6:8],
        gwin,
        rel[1],
        gwd,
        rep[8],
    )


def solution(mesh):
    placed = (
        P("dp", "tensor", None, None),
        P("dp", "tensor", None, None),
        P(),
        P(),
        P(None, None, None, "tensor"),
        P(None, None, "tensor"),
        P(None, "tensor", None),
        P(),
        P(None, "tensor"),
        P("tensor"),
        P("tensor", None),
        P(),
    )
    return jax.shard_map(
        shards,
        mesh=mesh,
        in_specs=placed,
        out_specs=(
            P("dp", "tensor", None, None),
            P("dp", "tensor", None, None),
            P(),
            P(),
            P(None, None, None, "tensor"),
            P(None, None, "tensor"),
            P(None, "tensor", None),
            P(),
            P(None, "tensor"),
            P("tensor"),
            P("tensor", None),
            P(),
        ),
        check_vma=False,
    )
```

time: 627 us -> 505 us (0.81)
  waiting for transfers between devices: 90.9 us -> 42.4 us
  local copies, waits for them, and re-layouts: 76.4 us -> 31.7 us
  other arithmetic: 68.7 us -> 26.7 us
  Pallas kernels: 343 us -> 353 us
    ppermute x33 -> x21, waiting for transfers between devices: 57 us -> 14.3 us  [over_tensor(): return lax.ppermute(v, 'tensor', [(i, i ^ bit) for i in range(4)])]
    unnamed x133 -> x48, local copies, waits for them, and re-layouts: 25.2 us -> 7.54 us
    select_n x13 -> x1, other arithmetic: 15.3 us -> 1.14 us  [shards(): m_a, m_b = (jnp.where(z == 0, m_q, m_z), jnp.where(z == 0, m_z, m_q))]
    slice x28 -> x4, local copies, waits for them, and re-layouts: 13.7 us -> 1.06 us  [the longest x1 0.93 us: shards(): qv = b[:, 0].reshape(4, 4, e).transpose(1, 0, 2).reshape(4, width)]
    another operation x18 -> x4, other arithmetic: 15.9 us -> 3.86 us  [the longest x3 2.99 us: shards(): jnp.stack([mine0[0, 0] + got_y[0] + got_a, mine0[0, 1] + got_x[0] + got_b])]
    pallas_call x11 -> x15, Pallas kernels: 343 us -> 353 us  [the longest x13 258 us: call(): pl.pallas_call(body, grid_spec=pltpu.PrefetchScalarGridSpec(num_scalar_pr...]
    ppermute x8 -> x10, waiting for transfers between devices: 34 us -> 25 us  [over_dp(): return lax.ppermute(v, 'dp', [(i, i ^ bit) for i in range(dp)])]
    ppermute x33 -> x21, starting transfers between devices: 18.7 us -> 10.8 us  [over_tensor(): return lax.ppermute(v, 'tensor', [(i, i ^ bit) for i in range(4)])]
  transfers between devices with their start and end apart: 42 -> 33, of which waited for: 12 -> 11; matrix products, arithmetic and copies ran while one was open for 19% -> 8% of each run, Pallas kernels for 48% -> 52%
where the time goes in v4:
time: 505 us; the launch traced here: 495 us
  Pallas kernels  353 us (70%)
  waiting for transfers between devices  42.4 us (8%)
  local copies, waits for them, and re-layouts  31.7 us (6%)
  other arithmetic  26.7 us (5%)
  starting transfers between devices  25.8 us (5%)
  between operations  15.1 us (3%)
    pallas_call x13, Pallas kernels, call(): pl.pallas_call(body, grid_spec=pltpu.PrefetchScalarGridSpec(num_scalar_pr...  258 us
    pallas_call x1, Pallas kernels, start(): pl.pallas_call(start_body, in_specs=[ANY, ANY, pl.BlockSpec(memory_space=...  49.2 us
    pallas_call x1, Pallas kernels, finish(): pl.pallas_call(functools.partial(finish_body, dp), in_specs=[vm] * 4, out...  46.4 us
    ppermute x10, waiting for transfers between devices, over_dp(): return lax.ppermute(v, 'dp', [(i, i ^ bit) for i in range(dp)])  25 us
    ppermute x21, waiting for transfers between devices, over_tensor(): return lax.ppermute(v, 'tensor', [(i, i ^ bit) for i in range(4)])  14.3 us
    ppermute x10, starting transfers between devices, over_dp(): return lax.ppermute(v, 'dp', [(i, i ^ bit) for i in range(dp)])  13.4 us
    ppermute x21, starting transfers between devices, over_tensor(): return lax.ppermute(v, 'tensor', [(i, i ^ bit) for i in range(4)])  10.8 us
  transfers between devices with their start and end apart: 33, of which 11 were waited for; matrix products, arithmetic and copies ran while one was open for 8% of the time, Pallas kernels for 52%

profile of v4, /device:TPU:0, one launch (start us, length us, event | category | flops | bytes accessed | tf_op | source)
XLA Modules:
  0.0 495.0 jit_solution(4804508911948138028)
XLA Ops:
  7.3 2.5 copy.36
  14.4 1.7 copy.35.clips.x
  17.1 2.5 pad.11
  20.3 49.2 %start.1 = (bf16[2,4,4,192,768]{4,3,2,1,0:T(8,128)(2,1)}, bf16[4,196,768]{2,1,0:T(8,128)(2,1)}, f32[4,8,768]{2,1,0:T(8,128)}) custom-call(bf16[2,3,192,768]{3,2,1,0:T(8,128)(2,1)} %bitcast.108, bf16[2,192,768]{2,1,0:T(8,128)(2,1)} %wout.1, f32[8,768]{1,0:T(8,128)} %maximum_maximum_fusion.1.bias, bf16[2,4,196,768]{3,2,1,0:T(8,128)(2,1)} %copy.35.clips.x), custom_call_target="tpu_custom_call" | custom-call | flops 54999998464 | bytes 5000000 | tf_op jit(solution)/shard_map/start/pallas_call | solution.py:243
  71.3 13.8 %spatial.2 = (f32[8,208,768]{2,1,0:T(8,128)}, bf16[8,104,768]{2,1,0:T(8,128)(2,1)}, bf16[8,104,768]{2,1,0:T(8,128)(2,1)}, bf16[8,208,768]{2,1,0:T(8,128)(2,1)}, ...) custom-call(s32[1]{0:T(128)} %bitcast.ids, ...), custom_call_target="tpu_custom_call" | custom-call | flops 13200000000 | bytes 1200000 | tf_op jit(solution)/shard_map/spatial/pallas_call | solution.py:134
  86.4 13.8 %spatial.3 = (f32[8,208,768]{2,1,0:T(8,128)}, bf16[8,104,768]{2,1,0:T(8,128)(2,1)}, bf16[8,104,768]{2,1,0:T(8,128)(2,1)}, bf16[8,208,768]{2,1,0:T(8,128)(2,1)}, ...) custom-call(s32[1]{0:T(128)} %bitcast.ids, ...), custom_call_target="tpu_custom_call", output_to_operand_aliasing={{0}: (7, {}), {1}: (8, {}), {2}: (9, {}), {3}: (10, {}), {4... | custom-call | flops 13200000000 | bytes 1200000 | tf_op jit(solution)/shard_map/spatial/pallas_call | solution.py:134
  100.8 1.8 collective-permute-start.4
  105.1 23.1 %temporal.1 = (bf16[13,128,768]{2,1,0:T(8,128)(2,1)}, bf16[1664,768]{1,0:T(8,128)(2,1)}, bf16[1664,768]{1,0:T(8,128)(2,1)}, bf16[1664,768]{1,0:T(8,128)(2,1)}, b...) custom-call(s32[1]{0:T(128)} %bitcast.ids, ...), custom_call_target="tpu_custom_call" | custom-call | flops 24199999488 | bytes 2200000 | tf_op jit(solution)/shard_map/temporal/pallas_call | solution.py:134
  128.8 4.1 collective-permute-done.6.refs_1_
  135.2 1.4 collective-permute-done.7.refs_1_
  136.6 43.4 %mlp_first.1 = (f32[1664,768]{1,0:T(8,128)}, bf16[1664,768]{1,0:T(8,128)(2,1)}, bf16[1664,768]{1,0:T(8,128)(2,1)}, f32[1664,768]{1,0:T(8,128)}, f32[1664,768]{1,...) custom-call(s32[1]{0:T(128)} %bitcast.ids, f32[1664,768]{1,0:T(8,128)} %bitcast.112, ...), custom_call_target="tpu_custom_call" | custom-call | flops 36300001280 | bytes 3300000 | tf_op jit(solution)/shard_map/mlp_first/pallas_call | solution.py:134
  180.6 44.7 %mlp_second.1 = (f32[4,196,768]{2,1,0:T(8,128)}, bf16[4,208,768]{2,1,0:T(8,128)(2,1)}, f32[8,208,768]{2,1,0:T(8,128)}, bf16[8,104,768]{2,1,0:T(8,128)(2,1)}, bf1...) custom-call(s32[1]{0:T(128)} %bitcast.ids, ...), custom_call_target="tpu_custom_call" | custom-call | flops 36300001280 | bytes 3300000 | tf_op jit(solution)/shard_map/mlp_second/pallas_call | solution.py:134
  225.4 1.4 copy-done.8
  226.9 3.1 add.120
  230.0 2.2 add.119
  235.0 1.6 collective-permute-start.15
  236.6 31.6 %temporal_back.1 = (bf16[13,128,768]{2,1,0:T(8,128)(2,1)}, bf16[8,13,8,768]{3,2,1,0:T(8,128)(2,1)}, bf16[8,13,8,768]{3,2,1,0:T(8,128)(2,1)}, bf16[3,1664,768]{2,1,0:T(8,128)(2,1)}) custom-call(s32[1]{0:T(128)} %bitcast.ids, bf16[8,13,8,768]{3,2,1,0:T(8,128)(2,1)} %bitcast.124, bf16[8,13,8,768]{3,2,1,0:T(8,128)(2,1)} %bitcast.13.got, ...), custom_call_target="tpu_custom_call" | custom-call | flops 37399998464 | bytes 3400000 | tf_op jit(solution)/shard_map/temporal_back/pallas_call | solution.py:134
  268.2 1.4 bitcast_add_fusion
  270.7 1.5 dynamic-slice_add_fusion
  273.6 1.5 collective-permute-start.17
  275.1 13.5 %weight_grads.2 = (bf16[2,4,192,768]{3,2,1,0:T(8,128)(2,1)}, bf16[2,4,192,768]{3,2,1,0:T(8,128)(2,1)}, f32[4,1,768]{2,1,0:T(1,128)}) custom-call(s32[1]{0:T(128)} %bitcast.ids, bf16[3,1664,768]{2,1,0:T(8,128)(2,1)} %get-tuple-element.167.dqkv, bf16[1664,768]{1,0:T(8,128)(2,1)} %bitcast.117, bf16[1664,768]{1,0:T(8,128)(2,1)} %bitcast.116, ...), custom_call_target="tpu_custom_call" | custom-call | flops 14300000256 | bytes 1300000 | tf_op jit(solution)/shard_map/weight_grads/pallas_call | solution.py:134
  290.4 1.6 collective-permute-start.19
  292.1 22.0 %spatial_back.2 = (bf16[4,208,768]{2,1,0:T(8,128)(2,1)}, f32[8,768]{1,0:T(8,128)}, bf16[3,8,208,768]{3,2,1,0:T(8,128)(2,1)}, bf16[8,208,768]{2,1,0:T(8,128)(2,1)}, bf16[8,208,768]{2,1,0:T(8,128)(2,1)}) custom-call(s32[1]{0:T(128)} %bitcast.ids, bf16[4,196,768]{2,1,0:T(8,128)(2,1)} %get-tuple-element.125.x, f32[8,208,768]{2,1,0:T(8,128)} %get-tuple-element.136.s1, ...), custom_call_target="tpu_custom_call" | custom-call | flops 22000001024 | bytes 2000000 | tf_op jit(solution)/shard_map/spatial_back/pallas_call | solution.py:134
  314.1 2.2 add.127
  316.5 4.7 collective-permute-done.19.got
  322.1 1.6 collective-permute-start.20
  323.7 1.5 collective-permute-start.22
  325.7 22.3 %spatial_back.3 = (f32[4,196,768]{2,1,0:T(8,128)}, f32[8,768]{1,0:T(8,128)}, bf16[3,8,208,768]{3,2,1,0:T(8,128)(2,1)}, bf16[8,208,768]{2,1,0:T(8,128)(2,1)}, bf16[8,208,768]{2,1,0:T(8,128)(2,1)}) custom-call(s32[1]{0:T(128)} %bitcast.ids, bf16[2,4,196,768]{3,2,1,0:T(8,128)(2,1)} %copy.35.clips.x, ...), custom_call_target="tpu_custom_call", output_to_operand_aliasing={{2}: (13, {}), {3}: (14, {}), {4}: (15, {})} | custom-call | flops 22000001024 | bytes 2000000 | tf_op jit(solution)/shard_map/spatial_back/pallas_call | solution.py:134
  348.1 3.0 collective-permute-done.22
  351.1 1.4 collective-permute-done.21
  354.8 13.6 %weight_grads.3 = (bf16[2,4,192,768]{3,2,1,0:T(8,128)(2,1)}, bf16[2,4,192,768]{3,2,1,0:T(8,128)(2,1)}, f32[4,1,768]{2,1,0:T(1,128)}) custom-call(s32[1]{0:T(128)} %bitcast.ids, bf16[3,1664,768]{2,1,0:T(8,128)(2,1)} %bitcast.111, bf16[1664,768]{1,0:T(8,128)(2,1)} %bitcast.121, bf16[1664,768]{1,0:T(8,128)(2,1)} %bitcast.118, bf16[1664,768]{1,0:T(8,128)(2,1)} %bitcast.119), custom_call_target="tpu_custom_call" | custom-call | flops 14300000256 | bytes 1300000 | tf_op jit(solution)/shard_map/weight_grads/pallas_call | solution.py:134
  370.6 2.7 collective-permute-start.27
  373.9 2.2 add.133
  378.7 1.5 collective-permute-start.26
  380.2 4.7 both_clips.2
  384.9 15.0 %collective-permute-done.27 = bf16[2,192,768]{2,1,0:T(8,128)(2,1)S(1)} collective-permute-done((bf16[2,192,768]{2,1,0:T(8,128)(2,1)S(1)}, bf16[2,192,768]{2,1,0:T(8,128)(2,1)S(1)}, u32[]{:S(2)}, u32[]{:S(2)}) %collective-permute-start.27) | collective-permute-done | bytes 589856 | tf_op jit(solution)/shard_map/ppermute | solution.py:1009
  401.9 1.8 collective-permute-start.29
  404.7 5.9 %collective-permute-done.29 = bf16[192,768]{1,0:T(8,128)(2,1)S(1)} collective-permute-done((bf16[192,768]{1,0:T(8,128)(2,1)S(1)}, bf16[192,768]{1,0:T(8,128)(2,1)S(1)}, u32[]{:S(2)}, u32[]{:S(2)}) %collective-permute-start.29) | collective-permute-done | bytes 294944 | tf_op jit(solution)/shard_map/ppermute | solution.py:1009
  412.5 1.5 collective-permute-start.31
  414.7 1.7 collective-permute-start.28
  416.5 5.3 %collective-permute-done.30 = bf16[192,768]{1,0:T(8,128)(2,1)S(1)} collective-permute-done((bf16[192,768]{1,0:T(8,128)(2,1)S(1)}, bf16[192,768]{1,0:T(8,128)(2,1)S(1)}, u32[]{:S(2)}, u32[]{:S(2)}) %collective-permute-start.30) | collective-permute-done | bytes 294944 | tf_op jit(solution)/shard_map/ppermute | solution.py:1006
  423.7 46.4 %finish.1 = (bf16[4,192,768]{2,1,0:T(8,128)(2,1)}, bf16[4,192,768]{2,1,0:T(8,128)(2,1)}, f32[8,768]{1,0:T(8,128)}, f32[16,768]{1,0:T(8,128)}) custom-call(bf16[2,192,768]{2,1,0:T(8,128)(2,1)} %pad_maximum_fusion.4.t0, bf16[2,192,768]{2,1,0:T(8,128)(2,1)} %add.137.t1, f32[4,8,768]{2,1,0:T(8,128)} %maximum_maximum_fusion.rel, f32[16,768]{1,0:T(8,128)} %pad.13.rep), custom_call_target="tpu_custom_call" | custom-call | flops 44000002048 | bytes 4000000 | tf_op jit(solution)/shard_map/finish/pallas_call | solution.py:967
  470.1 1.4 slice_reduce_fusion.2
  472.2 1.3 slice.183
  473.5 1.3 slice_reduce_fusion.1
  474.9 1.4 fusion.11
  476.3 6.5 %to_results.1 = (f32[2,3,192,768]{3,2,1,0:T(8,128)}, f32[2,192,768]{2,1,0:T(8,128)}, f32[768,768]{1,0:T(8,128)}, f32[768,768]{1,0:T(8,128)}) custom-call(s32[1]{0:T(128)} %bitcast.ids, bf16[4,192,768]{2,1,0:T(8,128)(2,1)} %get-tuple-element.222.f0, bf16[4,192,768]{2,1,0:T(8,128)(2,1)} %get-tuple-element.225.f1, ...), custom_call_target="tpu_custom_call" | custom-call | flops 5500000256 | bytes 500000 | tf_op jit(solution)/shard_map/to_results/pallas_call | solution.py:134
  482.8 4.9 both_clips.3
  (154 shorter events, 40.7 us)
Async XLA Ops:
  7.2 4.6 copy-start
  7.2 346.4 %all-reduce.5.cloned.1.call-start = ((), (), s32[]{:S(2)}) async-start(), calls=%async_computation | async-start | bytes 2359296 | tf_op jit(solution)/shard_map/psum | solution.py:1085
  69.5 15.9 %collective-permute-start = (bf16[384,768]{1,0:T(8,128)(2,1)}, bf16[384,768]{1,0:T(8,128)(2,1)S(1)}, u32[]{:S(2)}, u32[]{:S(2)}) collective-permute-start(bf16[384,768]{1,0:T(8,128)(2,1)} %pad_maximum_fusion.2), channel_id=1, source_target_pairs={{0,2},{1,3},{2,0},{3,1},{4,6},{5,7},{6,4},{7,5},{8,10},{9,11},{10,... | collective-permute-start | bytes 1769480 | tf_op jit(solution)/shard_map/ppermute | solution.py:1006
  85.4 17.2 %collective-permute-start.1 = (bf16[384,768]{1,0:T(8,128)(2,1)S(1)}, bf16[384,768]{1,0:T(8,128)(2,1)}, u32[]{:S(2)}, u32[]{:S(2)}) collective-permute-start(bf16[384,768]{1,0:T(8,128)(2,1)S(1)} %collective-permute-done), channel_id=1, source_target_pairs={{0,8},{4,12},{8,0},{12,4},{16,24},{20,28},{24,16},{28,20},{1,9},{5... | collective-permute-start | bytes 1769480 | tf_op jit(solution)/shard_map/ppermute | solution.py:1009
  100.2 4.9 collective-permute-start.2
  100.3 28.5 %collective-permute-start.8 = (bf16[768,768]{1,0:T(8,128)(2,1)}, bf16[768,768]{1,0:T(8,128)(2,1)}, u32[]{:S(2)}, u32[]{:S(2)}) collective-permute-start(bf16[768,768]{1,0:T(8,128)(2,1)} %bitcast.11.refs_2_), channel_id=1, source_target_pairs={{0,1},{1,0},{2,3},{3,2},{4,5},{5,4},{6,7},{7,6},{8,9},{9,8},{10,11... | collective-permute-start | bytes 3538952 | tf_op jit(solution)/shard_map/ppermute | solution.py:1006
  100.8 34.4 %collective-permute-start.4 = (bf16[4,208,768]{2,1,0:T(8,128)(2,1)}, bf16[4,208,768]{2,1,0:T(8,128)(2,1)}, u32[]{:S(2)}, u32[]{:S(2)}) collective-permute-start(bf16[4,208,768]{2,1,0:T(8,128)(2,1)} %pad.11), channel_id=1, source_target_pairs={{0,2},{1,3},{2,0},{3,1},{4,6},{5,7},{6,4},{7,5},{8,10},{9,11},{10,... | collective-permute-start | bytes 3833864 | tf_op jit(solution)/shard_map/ppermute | solution.py:1006
  104.9 28.0 %collective-permute-start.6 = (bf16[768,768]{1,0:T(8,128)(2,1)}, bf16[768,768]{1,0:T(8,128)(2,1)}, u32[]{:S(2)}, u32[]{:S(2)}) collective-permute-start(bf16[768,768]{1,0:T(8,128)(2,1)} %pad_maximum_fusion.refs_0_), channel_id=1, source_target_pairs={{0,4},{4,0},{8,12},{12,8},{16,20},{20,16},{24,28},{28,24},{1,5},{5... | collective-permute-start | bytes 3538952 | tf_op jit(solution)/shard_map/ppermute | solution.py:1009
  128.2 7.1 %collective-permute-start.3 = (bf16[8,104,768]{2,1,0:T(8,128)(2,1)}, bf16[8,104,768]{2,1,0:T(8,128)(2,1)}, u32[]{:S(2)}, u32[]{:S(2)}) collective-permute-start(bf16[8,104,768]{2,1,0:T(8,128)(2,1)} %bitcast.110), channel_id=1, source_target_pairs={{0,1},{1,0},{2,3},{3,2},{4,5},{5,4},{6,7},{7,6},{8,9},{9,8},{10,11... | collective-permute-start | bytes 3833864 | tf_op jit(solution)/shard_map/ppermute | solution.py:1006
  128.2 7.0 %collective-permute-start.9 = (bf16[768,768]{1,0:T(8,128)(2,1)}, bf16[768,768]{1,0:T(8,128)(2,1)}, u32[]{:S(2)}, u32[]{:S(2)}) collective-permute-start(bf16[768,768]{1,0:T(8,128)(2,1)} %refs_3_.1), channel_id=1, source_target_pairs={{0,1},{1,0},{2,3},{3,2},{4,5},{5,4},{6,7},{7,6},{8,9},{9,8},{10,11... | collective-permute-start | bytes 3538952 | tf_op jit(solution)/shard_map/ppermute | solution.py:1006
  128.7 6.5 %collective-permute-start.5 = (bf16[768,768]{1,0:T(8,128)(2,1)}, bf16[768,768]{1,0:T(8,128)(2,1)}, u32[]{:S(2)}, u32[]{:S(2)}) collective-permute-start(bf16[768,768]{1,0:T(8,128)(2,1)} %pad_maximum_fusion.refs_0_), channel_id=1, source_target_pairs={{0,1},{1,0},{2,3},{3,2},{4,5},{5,4},{6,7},{7,6},{8,9},{9,8},{10,11... | collective-permute-start | bytes 3538952 | tf_op jit(solution)/shard_map/ppermute | solution.py:1006
  132.9 3.7 collective-permute-start.7
  180.0 45.4 %collective-permute-start.12 = (bf16[2,768,768]{2,1,0:T(8,128)(2,1)}, bf16[2,768,768]{2,1,0:T(8,128)(2,1)S(1)}, u32[]{:S(2)}, u32[]{:S(2)}) collective-permute-start(bf16[2,768,768]{2,1,0:T(8,128)(2,1)} %get-tuple-element.159), channel_id=1, source_target_pairs={{0,1},{1,0},{2,3},{3,2},{4,5},{5,4},{6,7},{7,6},{8,9},{9,8},{10,11... | collective-permute-start | bytes 7077896 | tf_op jit(solution)/shard_map/ppermute | solution.py:1006
  180.2 49.7 %collective-permute-start.11 = (bf16[2,768,768]{2,1,0:T(8,128)(2,1)}, bf16[2,768,768]{2,1,0:T(8,128)(2,1)}, u32[]{:S(2)}, u32[]{:S(2)}) collective-permute-start(bf16[2,768,768]{2,1,0:T(8,128)(2,1)} %get-tuple-element.157), channel_id=1, source_target_pairs={{0,1},{1,0},{2,3},{3,2},{4,5},{5,4},{6,7},{7,6},{8,9},{9,8},{10,11... | collective-permute-start | bytes 7077896 | tf_op jit(solution)/shard_map/ppermute | solution.py:1006
  225.2 7.0 %collective-permute-start.10 = (bf16[8,104,768]{2,1,0:T(8,128)(2,1)}, bf16[8,104,768]{2,1,0:T(8,128)(2,1)}, u32[]{:S(2)}, u32[]{:S(2)}) collective-permute-start(bf16[8,104,768]{2,1,0:T(8,128)(2,1)} %get-tuple-element.155), channel_id=1, source_target_pairs={{0,1},{1,0},{2,3},{3,2},{4,5},{5,4},{6,7},{7,6},{8,9},{9,8},{10,11... | collective-permute-start | bytes 3833864 | tf_op jit(solution)/shard_map/ppermute | solution.py:1006
  226.9 3.1 copy-start.7
  232.2 2.8 copy-start.2
  233.4 34.8 %collective-permute-start.14 = (bf16[768,768]{1,0:T(8,128)(2,1)}, bf16[768,768]{1,0:T(8,128)(2,1)S(1)}, u32[]{:S(2)}, u32[]{:S(2)}) collective-permute-start(bf16[768,768]{1,0:T(8,128)(2,1)} %slice_bitcast_fusion), channel_id=1, source_target_pairs={{0,2},{1,3},{2,0},{3,1},{4,6},{5,7},{6,4},{7,5},{8,10},{9,11},{10,... | collective-permute-start | bytes 3538952 | tf_op jit(solution)/shard_map/ppermute | solution.py:1006
  235.0 35.6 %collective-permute-start.15 = (bf16[2,384,768]{2,1,0:T(8,128)(2,1)}, bf16[2,384,768]{2,1,0:T(8,128)(2,1)}, u32[]{:S(2)}, u32[]{:S(2)}) collective-permute-start(bf16[2,384,768]{2,1,0:T(8,128)(2,1)} %constant_dynamic-slice_fusion.2), channel_id=1, source_target_pairs={{0,4},{4,0},{8,12},{12,8},{16,20},{20,16},{24,28},{28,24},{1,5},{5... | collective-permute-start | bytes 3538952 | tf_op jit(solution)/shard_map/ppermute | solution.py:1009
  268.2 22.3 %collective-permute-start.13 = (bf16[8,104,768]{2,1,0:T(8,128)(2,1)}, bf16[8,104,768]{2,1,0:T(8,128)(2,1)}, u32[]{:S(2)}, u32[]{:S(2)}) collective-permute-start(bf16[8,104,768]{2,1,0:T(8,128)(2,1)} %bitcast.109), channel_id=1, source_target_pairs={{0,1},{1,0},{2,3},{3,2},{4,5},{5,4},{6,7},{7,6},{8,9},{9,8},{10,11... | collective-permute-start | bytes 3833864 | tf_op jit(solution)/shard_map/ppermute | solution.py:1006
  272.2 16.4 %collective-permute-start.16 = (bf16[384,768]{1,0:T(8,128)(2,1)}, bf16[384,768]{1,0:T(8,128)(2,1)S(1)}, u32[]{:S(2)}, u32[]{:S(2)}) collective-permute-start(bf16[384,768]{1,0:T(8,128)(2,1)} %get-tuple-element.176), channel_id=1, source_target_pairs={{0,4},{4,0},{8,12},{12,8},{16,20},{20,16},{24,28},{28,24},{1,5},{5... | collective-permute-start | bytes 1769480 | tf_op jit(solution)/shard_map/ppermute | solution.py:1009
  273.6 15.7 %collective-permute-start.17 = (bf16[384,768]{1,0:T(8,128)(2,1)}, bf16[384,768]{1,0:T(8,128)(2,1)S(1)}, u32[]{:S(2)}, u32[]{:S(2)}) collective-permute-start(bf16[384,768]{1,0:T(8,128)(2,1)} %slice_bitcast_fusion.5), channel_id=1, source_target_pairs={{0,2},{1,3},{2,0},{3,1},{4,6},{5,7},{6,4},{7,5},{8,10},{9,11},{10,... | collective-permute-start | bytes 1769480 | tf_op jit(solution)/shard_map/ppermute | solution.py:1006
  275.1 13.5 %copy-start.9 = (bf16[384,768]{1,0:T(8,128)(2,1)S(1)}, bf16[384,768]{1,0:T(8,128)(2,1)}, u32[]{:S(2)}) copy-start(bf16[384,768]{1,0:T(8,128)(2,1)} %get-tuple-element.175) | copy-start | bytes 1769476
  290.4 23.6 %collective-permute-start.18 = (bf16[2,4,192,768]{3,2,1,0:T(8,128)(2,1)}, bf16[2,4,192,768]{3,2,1,0:T(8,128)(2,1)}, u32[]{:S(2)}, u32[]{:S(2)}) collective-permute-start(bf16[2,4,192,768]{3,2,1,0:T(8,128)(2,1)} %get-tuple-element.186), channel_id=1, source_target_pairs={{0,1},{1,0},{2,3},{3,2},{4,5},{5,4},{6,7},{7,6},{8,9},{9,8},{10,11... | collective-permute-start | bytes 7077896 | tf_op jit(solution)/shard_map/ppermute | solution.py:1006
  290.4 30.8 %collective-permute-start.19 = (bf16[4,208,768]{2,1,0:T(8,128)(2,1)}, bf16[4,208,768]{2,1,0:T(8,128)(2,1)}, u32[]{:S(2)}, u32[]{:S(2)}) collective-permute-start(bf16[4,208,768]{2,1,0:T(8,128)(2,1)} %get-tuple-element.188), channel_id=1, source_target_pairs={{0,2},{1,3},{2,0},{3,1},{4,6},{5,7},{6,4},{7,5},{8,10},{9,11},{10,... | collective-permute-start | bytes 3833864 | tf_op jit(solution)/shard_map/ppermute | solution.py:1006
  292.1 22.0 %copy-start.6 = (bf16[2,4,192,768]{3,2,1,0:T(8,128)(2,1)S(1)}, bf16[2,4,192,768]{3,2,1,0:T(8,128)(2,1)}, u32[]{:S(2)}) copy-start(bf16[2,4,192,768]{3,2,1,0:T(8,128)(2,1)} %get-tuple-element.185) | copy-start | bytes 7077892
  322.1 25.9 %collective-permute-start.20 = (bf16[2,192,768]{2,1,0:T(8,128)(2,1)}, bf16[2,192,768]{2,1,0:T(8,128)(2,1)S(1)}, u32[]{:S(2)}, u32[]{:S(2)}) collective-permute-start(bf16[2,192,768]{2,1,0:T(8,128)(2,1)} %get-tuple-element.245), channel_id=1, source_target_pairs={{0,4},{4,0},{8,12},{12,8},{16,20},{20,16},{24,28},{28,24},{1,5},{5... | collective-permute-start | bytes 1769480 | tf_op jit(solution)/shard_map/ppermute | solution.py:1009
  323.7 27.4 %collective-permute-start.22 = (bf16[2,192,768]{2,1,0:T(8,128)(2,1)S(1)}, bf16[2,192,768]{2,1,0:T(8,128)(2,1)S(1)}, u32[]{:S(2)}, u32[]{:S(2)}) collective-permute-start(bf16[2,192,768]{2,1,0:T(8,128)(2,1)S(1)} %get-tuple-element.244), channel_id=1, source_target_pairs={{0,6},{1,7},{2,4},{3,5},{4,2},{5,3},{6,0},{7,1},{8,14},{9,15},{10,... | collective-permute-start | bytes 1769480 | tf_op jit(solution)/shard_map/ppermute | solution.py:1093
  325.2 27.2 %collective-permute-start.21 = (bf16[2,192,768]{2,1,0:T(8,128)(2,1)S(1)}, bf16[2,192,768]{2,1,0:T(8,128)(2,1)}, u32[]{:S(2)}, u32[]{:S(2)}) collective-permute-start(bf16[2,192,768]{2,1,0:T(8,128)(2,1)S(1)} %slice_bitcast_fusion.3), channel_id=1, source_target_pairs={{0,2},{1,3},{2,0},{3,1},{4,6},{5,7},{6,4},{7,5},{8,10},{9,11},{10,... | collective-permute-start | bytes 1769480 | tf_op jit(solution)/shard_map/ppermute | solution.py:1006
  353.6 14.7 %collective-permute-start.23 = (bf16[2,192,768]{2,1,0:T(8,128)(2,1)S(1)}, bf16[2,192,768]{2,1,0:T(8,128)(2,1)S(1)}, u32[]{:S(2)}, u32[]{:S(2)}) collective-permute-start(bf16[2,192,768]{2,1,0:T(8,128)(2,1)S(1)} %fusion), channel_id=1, source_target_pairs={{0,8},{4,12},{8,0},{12,4},{16,24},{20,28},{24,16},{28,20},{1,9},{5... | collective-permute-start | bytes 1769480 | tf_op jit(solution)/shard_map/ppermute | solution.py:1009
  354.7 14.4 %copy-start.13 = (f32[8,768]{1,0:T(8,128)S(1)}, f32[8,768]{1,0:T(8,128)}, u32[]{:S(2)}) copy-start(f32[8,768]{1,0:T(8,128)} %get-tuple-element.221) | copy-start | bytes 73732
  354.7 14.4 %copy-start.15 = (f32[2,1,768]{2,1,0:T(1,128)S(1)}, f32[2,1,768]{2,1,0:T(1,128)}, u32[]{:S(2)}) copy-start(f32[2,1,768]{2,1,0:T(1,128)} %get-tuple-element.217) | copy-start | bytes 18436
  354.7 14.5 %copy-start.14 = (f32[2,1,768]{2,1,0:T(1,128)S(1)}, f32[2,1,768]{2,1,0:T(1,128)}, u32[]{:S(2)}) copy-start(f32[2,1,768]{2,1,0:T(1,128)} %get-tuple-element.218) | copy-start | bytes 18436
  354.7 14.5 %copy-start.19 = (f32[4,1,768]{2,1,0:T(1,128)S(1)}, f32[4,1,768]{2,1,0:T(1,128)}, u32[]{:S(2)}) copy-start(f32[4,1,768]{2,1,0:T(1,128)} %get-tuple-element.216) | copy-start | bytes 36868
  354.7 14.7 %copy-start.11 = (f32[8,768]{1,0:T(8,128)S(1)}, f32[8,768]{1,0:T(8,128)}, u32[]{:S(2)}) copy-start(f32[8,768]{1,0:T(8,128)} %get-tuple-element.219) | copy-start | bytes 73732
  354.7 14.7 %copy-start.12 = (f32[8,768]{1,0:T(8,128)S(1)}, f32[8,768]{1,0:T(8,128)}, u32[]{:S(2)}) copy-start(f32[8,768]{1,0:T(8,128)} %get-tuple-element.220) | copy-start | bytes 73732
  369.1 4.7 collective-permute-start.24
  370.6 29.3 %collective-permute-start.27 = (bf16[2,192,768]{2,1,0:T(8,128)(2,1)S(1)}, bf16[2,192,768]{2,1,0:T(8,128)(2,1)S(1)}, u32[]{:S(2)}, u32[]{:S(2)}) collective-permute-start(bf16[2,192,768]{2,1,0:T(8,128)(2,1)S(1)} %add.136), channel_id=1, source_target_pairs={{0,16},{4,20},{8,24},{12,28},{16,0},{20,4},{24,8},{28,12},{1,17},{... | collective-permute-start | bytes 1769480 | tf_op jit(solution)/shard_map/ppermute | solution.py:1009
  378.2 22.7 %collective-permute-start.25 = (bf16[2,192,768]{2,1,0:T(8,128)(2,1)}, bf16[2,192,768]{2,1,0:T(8,128)(2,1)}, u32[]{:S(2)}, u32[]{:S(2)}) collective-permute-start(bf16[2,192,768]{2,1,0:T(8,128)(2,1)} %pad_maximum_fusion.3), channel_id=1, source_target_pairs={{0,2},{1,3},{2,0},{3,1},{4,6},{5,7},{6,4},{7,5},{8,10},{9,11},{10,... | collective-permute-start | bytes 1769480 | tf_op jit(solution)/shard_map/ppermute | solution.py:1006
  378.7 22.2 %collective-permute-start.26 = (bf16[2,192,768]{2,1,0:T(8,128)(2,1)}, bf16[2,192,768]{2,1,0:T(8,128)(2,1)}, u32[]{:S(2)}, u32[]{:S(2)}) collective-permute-start(bf16[2,192,768]{2,1,0:T(8,128)(2,1)} %slice_bitcast_fusion.1), channel_id=1, source_target_pairs={{0,4},{4,0},{8,12},{12,8},{16,20},{20,16},{24,28},{28,24},{1,5},{5... | collective-permute-start | bytes 1769480 | tf_op jit(solution)/shard_map/ppermute | solution.py:1009
  384.9 19.6 %copy-start.20 = (f32[4,1,768]{2,1,0:T(1,128)S(1)}, f32[4,1,768]{2,1,0:T(1,128)}, u32[]{:S(2)}) copy-start(f32[4,1,768]{2,1,0:T(1,128)} %get-tuple-element.215) | copy-start | bytes 36868
  384.9 25.7 %copy-start.4 = (bf16[2,2,192,768]{3,2,1,0:T(8,128)(2,1)S(1)}, bf16[2,2,192,768]{3,2,1,0:T(8,128)(2,1)}, u32[]{:S(2)}) copy-start(bf16[2,2,192,768]{3,2,1,0:T(8,128)(2,1)} %copy-done.3) | copy-start | bytes 3538948
  401.9 12.1 %copy-start.22 = (f32[8]{0:T(128)S(1)}, f32[8]{0:T(128)}, u32[]{:S(2)}) copy-start(f32[8]{0:T(128)} %copy-done.21) | copy-start | bytes 100
  401.9 8.7 %collective-permute-start.29 = (bf16[192,768]{1,0:T(8,128)(2,1)S(1)}, bf16[192,768]{1,0:T(8,128)(2,1)S(1)}, u32[]{:S(2)}, u32[]{:S(2)}) collective-permute-start(bf16[192,768]{1,0:T(8,128)(2,1)S(1)} %fusion.5), channel_id=1, source_target_pairs={{0,4},{4,0},{8,12},{12,8},{16,20},{20,16},{24,28},{28,24},{1,5},{5... | collective-permute-start | bytes 884744 | tf_op jit(solution)/shard_map/ppermute | solution.py:1009
  411.8 10.0 %collective-permute-start.30 = (bf16[192,768]{1,0:T(8,128)(2,1)S(1)}, bf16[192,768]{1,0:T(8,128)(2,1)S(1)}, u32[]{:S(2)}, u32[]{:S(2)}) collective-permute-start(bf16[192,768]{1,0:T(8,128)(2,1)S(1)} %get-tuple-element.243), channel_id=1, source_target_pairs={{0,2},{1,3},{2,0},{3,1},{4,6},{5,7},{6,4},{7,5},{8,10},{9,11},{10,... | collective-permute-start | bytes 884744 | tf_op jit(solution)/shard_map/ppermute | solution.py:1006
  412.5 63.8 %collective-permute-start.31 = (bf16[768,768]{1,0:T(8,128)(2,1)}, bf16[768,768]{1,0:T(8,128)(2,1)}, u32[]{:S(2)}, u32[]{:S(2)}) collective-permute-start(bf16[768,768]{1,0:T(8,128)(2,1)} %all-reduce.5.cloned.1.call-done.m), channel_id=1, source_target_pairs={{0,4},{4,0},{8,12},{12,8},{16,20},{20,16},{24,28},{28,24},{1,5},{5... | collective-permute-start | bytes 3538952 | tf_op jit(solution)/shard_map/ppermute | solution.py:1009
  414.7 68.0 %collective-permute-start.28 = (bf16[4,208,768]{2,1,0:T(8,128)(2,1)}, bf16[4,208,768]{2,1,0:T(8,128)(2,1)}, u32[]{:S(2)}, u32[]{:S(2)}) collective-permute-start(bf16[4,208,768]{2,1,0:T(8,128)(2,1)} %get-tuple-element.212), channel_id=1, source_target_pairs={{0,2},{1,3},{2,0},{3,1},{4,6},{5,7},{6,4},{7,5},{8,10},{9,11},{10,... | collective-permute-start | bytes 3833864 | tf_op jit(solution)/shard_map/ppermute | solution.py:1006
  482.8 4.9 copy-start.1
  (8 other events, 11.7 us)
Sparse Core Ops, SparseCore 0:
  292.2 55.8 all-reduce.4

commit v5 on v4

--- a/solution.py
+++ b/solution.py
@@ -1102,8 +1102,9 @@
     z1 = over_dp(t1, bits[0]) if bits else jnp.zeros_like(t1)
     gs0, gk0, z1 = lax.optimization_barrier((gs0, gk0, z1))
     t1 = t1 + z1
+    ta, tb = t1[0], t1[1]
     for bit in bits[1:]:
-        t1 = t1 + over_dp(t1, bit)
+        ta = ta + over_dp(ta, bit)
     got0 = over_tensor(gs0, 1)
     output = both_clips(ids, out_near, after(out_got, gs0))
     keep0 = (gk0 + got0).reshape(2, 2, 2, e, width)
@@ -1111,10 +1112,14 @@
     got_y = over_tensor(jnp.stack([mine0[1, 0], send0[1, 0]]), 2)
     got_x = over_dp(send0[:, 1], 1)
     mlp_got = over_dp(mlp_sum, 1)
-    output, got_y, got_x, t1 = lax.optimization_barrier((output, got_y, got_x, t1))
+    output, got_y, got_x, ta, tb = lax.optimization_barrier((output, got_y, got_x, ta, tb))
+    for bit in bits[1:]:
+        tb = tb + over_dp(tb, bit)
     in_got = over_tensor(after(g0_far, got_y), 2)
     got_a = over_dp(send0[0, 0] + got_y[1], 1)
     got_b = over_tensor(mine0[1, 1] + got_x[1], 2)
+    got_a, got_b, tb = lax.optimization_barrier((got_a, got_b, tb))
+    t1 = jnp.stack([ta, tb])
     t0 = jnp.stack([mine0[0, 0] + got_y[0] + got_a, mine0[0, 1] + got_x[0] + got_b])
     sums0 = sums_f + sums_n
     rep = jnp.stack(

time: 505 us -> 499 us (0.988)
  waiting for transfers between devices: 42.4 us -> 30.4 us
    ppermute x10 -> x11, waiting for transfers between devices: 25 us -> 14.1 us  [over_dp(): return lax.ppermute(v, 'dp', [(i, i ^ bit) for i in range(dp)])]
    ppermute x10 -> x11, starting transfers between devices: 13.4 us -> 12.5 us  [over_dp(): return lax.ppermute(v, 'dp', [(i, i ^ bit) for i in range(dp)])]
  transfers between devices with their start and end apart: 33 -> 34, of which waited for: 11 -> 11; matrix products, arithmetic and copies ran while one was open for 8% -> 10% of each run, Pallas kernels for 52% -> 53%
where the time goes in v5:
time: 499 us; the launch traced here: 489 us
  Pallas kernels  355 us (71%)
  local copies, waits for them, and re-layouts  34.4 us (7%)
  waiting for transfers between devices  30.4 us (6%)
  other arithmetic  29.5 us (6%)
  starting transfers between devices  24.6 us (5%)
  between operations  15.2 us (3%)
    pallas_call x13, Pallas kernels, call(): pl.pallas_call(body, grid_spec=pltpu.PrefetchScalarGridSpec(num_scalar_pr...  257 us
    pallas_call x1, Pallas kernels, start(): pl.pallas_call(start_body, in_specs=[ANY, ANY, pl.BlockSpec(memory_space=...  49.2 us
    pallas_call x1, Pallas kernels, finish(): pl.pallas_call(functools.partial(finish_body, dp), in_specs=[vm] * 4, out...  48.1 us
    ppermute x11, waiting for transfers between devices, over_dp(): return lax.ppermute(v, 'dp', [(i, i ^ bit) for i in range(dp)])  14.1 us
    ppermute x21, waiting for transfers between devices, over_tensor(): return lax.ppermute(v, 'tensor', [(i, i ^ bit) for i in range(4)])  13.3 us
    ppermute x11, starting transfers between devices, over_dp(): return lax.ppermute(v, 'dp', [(i, i ^ bit) for i in range(dp)])  12.5 us
    ppermute x21, starting transfers between devices, over_tensor(): return lax.ppermute(v, 'tensor', [(i, i ^ bit) for i in range(4)])  10.6 us
  transfers between devices with their start and end apart: 34, of which 11 were waited for; matrix products, arithmetic and copies ran while one was open for 10% of the time, Pallas kernels for 53%

profile of v5, /device:TPU:0, one launch (start us, length us, event | category | flops | bytes accessed | tf_op | source)
XLA Modules:
  0.0 488.9 jit_solution(14030405827611375503)
XLA Ops:
  7.3 2.5 copy.36
  14.4 1.8 copy.35.clips.x
  17.1 2.4 pad.11
  20.3 49.2 %start.1 = (bf16[2,4,4,192,768]{4,3,2,1,0:T(8,128)(2,1)}, bf16[4,196,768]{2,1,0:T(8,128)(2,1)}, f32[4,8,768]{2,1,0:T(8,128)}) custom-call(bf16[2,3,192,768]{3,2,1,0:T(8,128)(2,1)} %bitcast.118, bf16[2,192,768]{2,1,0:T(8,128)(2,1)} %wout.1, f32[8,768]{1,0:T(8,128)} %maximum_maximum_fusion.1.bias, bf16[2,4,196,768]{3,2,1,0:T(8,128)(2,1)} %copy.35.clips.x), custom_call_target="tpu_custom_call" | custom-call | flops 54999998464 | bytes 5000000 | tf_op jit(solution)/shard_map/start/pallas_call | solution.py:243
  71.3 13.8 %spatial.2 = (f32[8,208,768]{2,1,0:T(8,128)}, bf16[8,104,768]{2,1,0:T(8,128)(2,1)}, bf16[8,104,768]{2,1,0:T(8,128)(2,1)}, bf16[8,208,768]{2,1,0:T(8,128)(2,1)}, ...) custom-call(s32[1]{0:T(128)} %bitcast.ids, ...), custom_call_target="tpu_custom_call" | custom-call | flops 13200000000 | bytes 1200000 | tf_op jit(solution)/shard_map/spatial/pallas_call | solution.py:134
  86.4 13.8 %spatial.3 = (f32[8,208,768]{2,1,0:T(8,128)}, bf16[8,104,768]{2,1,0:T(8,128)(2,1)}, bf16[8,104,768]{2,1,0:T(8,128)(2,1)}, bf16[8,208,768]{2,1,0:T(8,128)(2,1)}, ...) custom-call(s32[1]{0:T(128)} %bitcast.ids, ...), custom_call_target="tpu_custom_call", output_to_operand_aliasing={{0}: (7, {}), {1}: (8, {}), {2}: (9, {}), {3}: (10, {}), {4... | custom-call | flops 13200000000 | bytes 1200000 | tf_op jit(solution)/shard_map/spatial/pallas_call | solution.py:134
  100.8 1.8 collective-permute-start.4
  105.1 23.1 %temporal.1 = (bf16[13,128,768]{2,1,0:T(8,128)(2,1)}, bf16[1664,768]{1,0:T(8,128)(2,1)}, bf16[1664,768]{1,0:T(8,128)(2,1)}, bf16[1664,768]{1,0:T(8,128)(2,1)}, b...) custom-call(s32[1]{0:T(128)} %bitcast.ids, ...), custom_call_target="tpu_custom_call" | custom-call | flops 24199999488 | bytes 2200000 | tf_op jit(solution)/shard_map/temporal/pallas_call | solution.py:134
  128.8 4.1 collective-permute-done.6.refs_1_
  135.2 1.4 collective-permute-done.7.refs_1_
  136.6 43.4 %mlp_first.1 = (f32[1664,768]{1,0:T(8,128)}, bf16[1664,768]{1,0:T(8,128)(2,1)}, bf16[1664,768]{1,0:T(8,128)(2,1)}, f32[1664,768]{1,0:T(8,128)}, f32[1664,768]{1,...) custom-call(s32[1]{0:T(128)} %bitcast.ids, f32[1664,768]{1,0:T(8,128)} %bitcast.122, ...), custom_call_target="tpu_custom_call" | custom-call | flops 36300001280 | bytes 3300000 | tf_op jit(solution)/shard_map/mlp_first/pallas_call | solution.py:134
  180.6 44.6 %mlp_second.1 = (f32[4,196,768]{2,1,0:T(8,128)}, bf16[4,208,768]{2,1,0:T(8,128)(2,1)}, f32[8,208,768]{2,1,0:T(8,128)}, bf16[8,104,768]{2,1,0:T(8,128)(2,1)}, bf1...) custom-call(s32[1]{0:T(128)} %bitcast.ids, ...), custom_call_target="tpu_custom_call" | custom-call | flops 36300001280 | bytes 3300000 | tf_op jit(solution)/shard_map/mlp_second/pallas_call | solution.py:134
  225.4 1.4 copy-done.12
  226.8 3.1 add.123
  229.9 2.2 add.122
  234.9 1.6 collective-permute-start.15
  236.5 31.6 %temporal_back.1 = (bf16[13,128,768]{2,1,0:T(8,128)(2,1)}, bf16[8,13,8,768]{3,2,1,0:T(8,128)(2,1)}, bf16[8,13,8,768]{3,2,1,0:T(8,128)(2,1)}, bf16[3,1664,768]{2,1,0:T(8,128)(2,1)}) custom-call(s32[1]{0:T(128)} %bitcast.ids, bf16[8,13,8,768]{3,2,1,0:T(8,128)(2,1)} %bitcast.134, bf16[8,13,8,768]{3,2,1,0:T(8,128)(2,1)} %bitcast.13.got, ...), custom_call_target="tpu_custom_call" | custom-call | flops 37399998464 | bytes 3400000 | tf_op jit(solution)/shard_map/temporal_back/pallas_call | solution.py:134
  268.2 1.4 bitcast_add_fusion
  270.7 1.5 dynamic-slice_add_fusion
  273.6 1.5 collective-permute-start.17
  275.1 13.5 %weight_grads.2 = (bf16[2,4,192,768]{3,2,1,0:T(8,128)(2,1)}, bf16[2,4,192,768]{3,2,1,0:T(8,128)(2,1)}, f32[4,1,768]{2,1,0:T(1,128)}) custom-call(s32[1]{0:T(128)} %bitcast.ids, bf16[3,1664,768]{2,1,0:T(8,128)(2,1)} %get-tuple-element.171.dqkv, bf16[1664,768]{1,0:T(8,128)(2,1)} %bitcast.127, bf16[1664,768]{1,0:T(8,128)(2,1)} %bitcast.126, ...), custom_call_target="tpu_custom_call" | custom-call | flops 14300000256 | bytes 1300000 | tf_op jit(solution)/shard_map/weight_grads/pallas_call | solution.py:134
  290.4 1.6 collective-permute-start.19
  292.1 21.9 %spatial_back.2 = (bf16[4,208,768]{2,1,0:T(8,128)(2,1)}, f32[8,768]{1,0:T(8,128)}, bf16[3,8,208,768]{3,2,1,0:T(8,128)(2,1)}, bf16[8,208,768]{2,1,0:T(8,128)(2,1)}, bf16[8,208,768]{2,1,0:T(8,128)(2,1)}) custom-call(s32[1]{0:T(128)} %bitcast.ids, bf16[4,196,768]{2,1,0:T(8,128)(2,1)} %get-tuple-element.129.x, f32[8,208,768]{2,1,0:T(8,128)} %get-tuple-element.140.s1, ...), custom_call_target="tpu_custom_call" | custom-call | flops 22000001024 | bytes 2000000 | tf_op jit(solution)/shard_map/spatial_back/pallas_call | solution.py:134
  314.0 2.2 add.130
  316.4 4.8 collective-permute-done.19.got
  322.1 1.6 collective-permute-start.20
  323.7 1.5 collective-permute-start.22
  325.7 22.3 %spatial_back.3 = (f32[4,196,768]{2,1,0:T(8,128)}, f32[8,768]{1,0:T(8,128)}, bf16[3,8,208,768]{3,2,1,0:T(8,128)(2,1)}, bf16[8,208,768]{2,1,0:T(8,128)(2,1)}, bf16[8,208,768]{2,1,0:T(8,128)(2,1)}) custom-call(s32[1]{0:T(128)} %bitcast.ids, bf16[2,4,196,768]{3,2,1,0:T(8,128)(2,1)} %copy.35.clips.x, ...), custom_call_target="tpu_custom_call", output_to_operand_aliasing={{2}: (13, {}), {3}: (14, {}), {4}: (15, {})} | custom-call | flops 22000001024 | bytes 2000000 | tf_op jit(solution)/shard_map/spatial_back/pallas_call | solution.py:134
  348.0 3.0 collective-permute-done.22
  352.4 1.4 fusion
  354.9 13.3 %weight_grads.3 = (bf16[2,4,192,768]{3,2,1,0:T(8,128)(2,1)}, bf16[2,4,192,768]{3,2,1,0:T(8,128)(2,1)}, f32[4,1,768]{2,1,0:T(1,128)}) custom-call(s32[1]{0:T(128)} %bitcast.ids, bf16[3,1664,768]{2,1,0:T(8,128)(2,1)} %bitcast.121, bf16[1664,768]{1,0:T(8,128)(2,1)} %bitcast.131, bf16[1664,768]{1,0:T(8,128)(2,1)} %bitcast.128, bf16[1664,768]{1,0:T(8,128)(2,1)} %bitcast.129), custom_call_target="tpu_custom_call" | custom-call | flops 14300000256 | bytes 1300000 | tf_op jit(solution)/shard_map/weight_grads/pallas_call | solution.py:134
  370.7 1.4 add.139
  372.8 2.6 collective-permute-start.27
  375.4 2.2 add.136
  380.3 1.5 collective-permute-start.26
  381.8 4.8 both_clips.2
  386.6 3.0 collective-permute-done.27
  389.7 5.7 %collective-permute-done.25 = bf16[2,192,768]{2,1,0:T(8,128)(2,1)S(1)} collective-permute-done((bf16[2,192,768]{2,1,0:T(8,128)(2,1)}, bf16[2,192,768]{2,1,0:T(8,128)(2,1)S(1)}, u32[]{:S(2)}, u32[]{:S(2)}) %collective-permute-start.25) | collective-permute-done | bytes 589856 | tf_op jit(solution)/shard_map/ppermute | solution.py:1006
  396.1 1.7 fusion.4
  397.8 1.5 collective-permute-start.30
  399.3 1.7 fusion.5
  401.0 1.7 collective-permute-start.29
  404.5 6.6 %collective-permute-done.31 = bf16[192,768]{1,0:T(8,128)(2,1)} collective-permute-done((bf16[192,768]{1,0:T(8,128)(2,1)S(1)}, bf16[192,768]{1,0:T(8,128)(2,1)}, u32[]{:S(2)}, u32[]{:S(2)}) %collective-permute-start.31) | collective-permute-done | bytes 294944 | tf_op jit(solution)/shard_map/ppermute | solution.py:1009
  415.9 48.1 %finish.1 = (bf16[4,192,768]{2,1,0:T(8,128)(2,1)}, bf16[4,192,768]{2,1,0:T(8,128)(2,1)}, f32[8,768]{1,0:T(8,128)}, f32[16,768]{1,0:T(8,128)}) custom-call(bf16[2,192,768]{2,1,0:T(8,128)(2,1)} %pad_maximum_fusion.4.t0, bf16[2,192,768]{2,1,0:T(8,128)(2,1)} %pad_maximum_fusion.5.t1, f32[4,8,768]{2,1,0:T(8,128)} %maximum_maximum_fusion.rel, f32[16,768]{1,0:T(8,128)} %pad.13.rep), custom_call_target="tpu_custom_call" | custom-call | flops 44000002048 | bytes 4000000 | tf_op jit(solution)/shard_map/finish/pallas_call | solution.py:967
  464.0 1.4 slice_reduce_fusion.2
  468.8 1.4 fusion.12
  470.2 6.5 %to_results.1 = (f32[2,3,192,768]{3,2,1,0:T(8,128)}, f32[2,192,768]{2,1,0:T(8,128)}, f32[768,768]{1,0:T(8,128)}, f32[768,768]{1,0:T(8,128)}) custom-call(s32[1]{0:T(128)} %bitcast.ids, bf16[4,192,768]{2,1,0:T(8,128)(2,1)} %get-tuple-element.230.f0, bf16[4,192,768]{2,1,0:T(8,128)(2,1)} %get-tuple-element.233.f1, ...), custom_call_target="tpu_custom_call" | custom-call | flops 5500000256 | bytes 500000 | tf_op jit(solution)/shard_map/to_results/pallas_call | solution.py:134
  476.7 4.9 %both_clips.3 = f32[2,196,4,768]{3,2,1,0:T(4,128)} custom-call(s32[1]{0:T(128)} %bitcast.ids, f32[4,196,768]{2,1,0:T(8,128)} %get-tuple-element.213.near, bf16[4,208,768]{2,1,0:T(8,128)(2,1)} %collective-permute-done.28.got), custom_call_target="tpu_custom_call" | custom-call | flops 6600000000 | bytes 600000 | tf_op jit(solution)/shard_map/both_clips/pallas_call | solution.py:134
  (171 shorter events, 43.7 us)
Async XLA Ops:
  7.2 346.6 %all-reduce.5.cloned.1.call-start = ((), (), s32[]{:S(2)}) async-start(), calls=%async_computation | async-start | bytes 2359296 | tf_op jit(solution)/shard_map/psum | solution.py:1085
  69.5 15.9 %collective-permute-start = (bf16[384,768]{1,0:T(8,128)(2,1)}, bf16[384,768]{1,0:T(8,128)(2,1)S(1)}, u32[]{:S(2)}, u32[]{:S(2)}) collective-permute-start(bf16[384,768]{1,0:T(8,128)(2,1)} %pad_maximum_fusion.2), channel_id=1, source_target_pairs={{0,2},{1,3},{2,0},{3,1},{4,6},{5,7},{6,4},{7,5},{8,10},{9,11},{10,... | collective-permute-start | bytes 1769480 | tf_op jit(solution)/shard_map/ppermute | solution.py:1006
  85.4 17.2 %collective-permute-start.1 = (bf16[384,768]{1,0:T(8,128)(2,1)S(1)}, bf16[384,768]{1,0:T(8,128)(2,1)}, u32[]{:S(2)}, u32[]{:S(2)}) collective-permute-start(bf16[384,768]{1,0:T(8,128)(2,1)S(1)} %collective-permute-done), channel_id=1, source_target_pairs={{0,8},{4,12},{8,0},{12,4},{16,24},{20,28},{24,16},{28,20},{1,9},{5... | collective-permute-start | bytes 1769480 | tf_op jit(solution)/shard_map/ppermute | solution.py:1009
  100.2 4.9 collective-permute-start.2
  100.3 28.4 %collective-permute-start.8 = (bf16[768,768]{1,0:T(8,128)(2,1)}, bf16[768,768]{1,0:T(8,128)(2,1)}, u32[]{:S(2)}, u32[]{:S(2)}) collective-permute-start(bf16[768,768]{1,0:T(8,128)(2,1)} %bitcast.11.refs_2_), channel_id=1, source_target_pairs={{0,1},{1,0},{2,3},{3,2},{4,5},{5,4},{6,7},{7,6},{8,9},{9,8},{10,11... | collective-permute-start | bytes 3538952 | tf_op jit(solution)/shard_map/ppermute | solution.py:1006
  100.8 34.4 %collective-permute-start.4 = (bf16[4,208,768]{2,1,0:T(8,128)(2,1)}, bf16[4,208,768]{2,1,0:T(8,128)(2,1)}, u32[]{:S(2)}, u32[]{:S(2)}) collective-permute-start(bf16[4,208,768]{2,1,0:T(8,128)(2,1)} %pad.11), channel_id=1, source_target_pairs={{0,2},{1,3},{2,0},{3,1},{4,6},{5,7},{6,4},{7,5},{8,10},{9,11},{10,... | collective-permute-start | bytes 3833864 | tf_op jit(solution)/shard_map/ppermute | solution.py:1006
  104.9 28.0 %collective-permute-start.6 = (bf16[768,768]{1,0:T(8,128)(2,1)}, bf16[768,768]{1,0:T(8,128)(2,1)}, u32[]{:S(2)}, u32[]{:S(2)}) collective-permute-start(bf16[768,768]{1,0:T(8,128)(2,1)} %pad_maximum_fusion.refs_0_), channel_id=1, source_target_pairs={{0,4},{4,0},{8,12},{12,8},{16,20},{20,16},{24,28},{28,24},{1,5},{5... | collective-permute-start | bytes 3538952 | tf_op jit(solution)/shard_map/ppermute | solution.py:1009
  128.1 7.1 %collective-permute-start.3 = (bf16[8,104,768]{2,1,0:T(8,128)(2,1)}, bf16[8,104,768]{2,1,0:T(8,128)(2,1)}, u32[]{:S(2)}, u32[]{:S(2)}) collective-permute-start(bf16[8,104,768]{2,1,0:T(8,128)(2,1)} %bitcast.120), channel_id=1, source_target_pairs={{0,1},{1,0},{2,3},{3,2},{4,5},{5,4},{6,7},{7,6},{8,9},{9,8},{10,11... | collective-permute-start | bytes 3833864 | tf_op jit(solution)/shard_map/ppermute | solution.py:1006
  128.2 7.0 %collective-permute-start.9 = (bf16[768,768]{1,0:T(8,128)(2,1)}, bf16[768,768]{1,0:T(8,128)(2,1)}, u32[]{:S(2)}, u32[]{:S(2)}) collective-permute-start(bf16[768,768]{1,0:T(8,128)(2,1)} %refs_3_.1), channel_id=1, source_target_pairs={{0,1},{1,0},{2,3},{3,2},{4,5},{5,4},{6,7},{7,6},{8,9},{9,8},{10,11... | collective-permute-start | bytes 3538952 | tf_op jit(solution)/shard_map/ppermute | solution.py:1006
  128.7 6.5 %collective-permute-start.5 = (bf16[768,768]{1,0:T(8,128)(2,1)}, bf16[768,768]{1,0:T(8,128)(2,1)}, u32[]{:S(2)}, u32[]{:S(2)}) collective-permute-start(bf16[768,768]{1,0:T(8,128)(2,1)} %pad_maximum_fusion.refs_0_), channel_id=1, source_target_pairs={{0,1},{1,0},{2,3},{3,2},{4,5},{5,4},{6,7},{7,6},{8,9},{9,8},{10,11... | collective-permute-start | bytes 3538952 | tf_op jit(solution)/shard_map/ppermute | solution.py:1006
  132.9 3.7 collective-permute-start.7
  180.0 45.4 %collective-permute-start.12 = (bf16[2,768,768]{2,1,0:T(8,128)(2,1)}, bf16[2,768,768]{2,1,0:T(8,128)(2,1)S(1)}, u32[]{:S(2)}, u32[]{:S(2)}) collective-permute-start(bf16[2,768,768]{2,1,0:T(8,128)(2,1)} %get-tuple-element.163), channel_id=1, source_target_pairs={{0,1},{1,0},{2,3},{3,2},{4,5},{5,4},{6,7},{7,6},{8,9},{9,8},{10,11... | collective-permute-start | bytes 7077896 | tf_op jit(solution)/shard_map/ppermute | solution.py:1006
  180.2 49.7 %collective-permute-start.11 = (bf16[2,768,768]{2,1,0:T(8,128)(2,1)}, bf16[2,768,768]{2,1,0:T(8,128)(2,1)}, u32[]{:S(2)}, u32[]{:S(2)}) collective-permute-start(bf16[2,768,768]{2,1,0:T(8,128)(2,1)} %get-tuple-element.161), channel_id=1, source_target_pairs={{0,1},{1,0},{2,3},{3,2},{4,5},{5,4},{6,7},{7,6},{8,9},{9,8},{10,11... | collective-permute-start | bytes 7077896 | tf_op jit(solution)/shard_map/ppermute | solution.py:1006
  225.2 7.0 %collective-permute-start.10 = (bf16[8,104,768]{2,1,0:T(8,128)(2,1)}, bf16[8,104,768]{2,1,0:T(8,128)(2,1)}, u32[]{:S(2)}, u32[]{:S(2)}) collective-permute-start(bf16[8,104,768]{2,1,0:T(8,128)(2,1)} %get-tuple-element.159), channel_id=1, source_target_pairs={{0,1},{1,0},{2,3},{3,2},{4,5},{5,4},{6,7},{7,6},{8,9},{9,8},{10,11... | collective-permute-start | bytes 3833864 | tf_op jit(solution)/shard_map/ppermute | solution.py:1006
  233.3 34.8 %collective-permute-start.14 = (bf16[768,768]{1,0:T(8,128)(2,1)}, bf16[768,768]{1,0:T(8,128)(2,1)S(1)}, u32[]{:S(2)}, u32[]{:S(2)}) collective-permute-start(bf16[768,768]{1,0:T(8,128)(2,1)} %slice_bitcast_fusion), channel_id=1, source_target_pairs={{0,2},{1,3},{2,0},{3,1},{4,6},{5,7},{6,4},{7,5},{8,10},{9,11},{10,... | collective-permute-start | bytes 3538952 | tf_op jit(solution)/shard_map/ppermute | solution.py:1006
  234.9 35.7 %collective-permute-start.15 = (bf16[2,384,768]{2,1,0:T(8,128)(2,1)}, bf16[2,384,768]{2,1,0:T(8,128)(2,1)}, u32[]{:S(2)}, u32[]{:S(2)}) collective-permute-start(bf16[2,384,768]{2,1,0:T(8,128)(2,1)} %constant_dynamic-slice_fusion.2), channel_id=1, source_target_pairs={{0,4},{4,0},{8,12},{12,8},{16,20},{20,16},{24,28},{28,24},{1,5},{5... | collective-permute-start | bytes 3538952 | tf_op jit(solution)/shard_map/ppermute | solution.py:1009
  268.1 22.3 %collective-permute-start.13 = (bf16[8,104,768]{2,1,0:T(8,128)(2,1)}, bf16[8,104,768]{2,1,0:T(8,128)(2,1)}, u32[]{:S(2)}, u32[]{:S(2)}) collective-permute-start(bf16[8,104,768]{2,1,0:T(8,128)(2,1)} %bitcast.119), channel_id=1, source_target_pairs={{0,1},{1,0},{2,3},{3,2},{4,5},{5,4},{6,7},{7,6},{8,9},{9,8},{10,11... | collective-permute-start | bytes 3833864 | tf_op jit(solution)/shard_map/ppermute | solution.py:1006
  272.2 16.4 %collective-permute-start.16 = (bf16[384,768]{1,0:T(8,128)(2,1)}, bf16[384,768]{1,0:T(8,128)(2,1)S(1)}, u32[]{:S(2)}, u32[]{:S(2)}) collective-permute-start(bf16[384,768]{1,0:T(8,128)(2,1)} %get-tuple-element.180), channel_id=1, source_target_pairs={{0,4},{4,0},{8,12},{12,8},{16,20},{20,16},{24,28},{28,24},{1,5},{5... | collective-permute-start | bytes 1769480 | tf_op jit(solution)/shard_map/ppermute | solution.py:1009
  273.6 15.7 %collective-permute-start.17 = (bf16[384,768]{1,0:T(8,128)(2,1)}, bf16[384,768]{1,0:T(8,128)(2,1)S(1)}, u32[]{:S(2)}, u32[]{:S(2)}) collective-permute-start(bf16[384,768]{1,0:T(8,128)(2,1)} %slice_bitcast_fusion.5), channel_id=1, source_target_pairs={{0,2},{1,3},{2,0},{3,1},{4,6},{5,7},{6,4},{7,5},{8,10},{9,11},{10,... | collective-permute-start | bytes 1769480 | tf_op jit(solution)/shard_map/ppermute | solution.py:1006
  275.1 13.5 %copy-start.13 = (bf16[384,768]{1,0:T(8,128)(2,1)S(1)}, bf16[384,768]{1,0:T(8,128)(2,1)}, u32[]{:S(2)}) copy-start(bf16[384,768]{1,0:T(8,128)(2,1)} %get-tuple-element.179) | copy-start | bytes 1769476
  290.4 23.6 %collective-permute-start.18 = (bf16[2,4,192,768]{3,2,1,0:T(8,128)(2,1)}, bf16[2,4,192,768]{3,2,1,0:T(8,128)(2,1)}, u32[]{:S(2)}, u32[]{:S(2)}) collective-permute-start(bf16[2,4,192,768]{3,2,1,0:T(8,128)(2,1)} %get-tuple-element.190), channel_id=1, source_target_pairs={{0,1},{1,0},{2,3},{3,2},{4,5},{5,4},{6,7},{7,6},{8,9},{9,8},{10,11... | collective-permute-start | bytes 7077896 | tf_op jit(solution)/shard_map/ppermute | solution.py:1006
  290.4 30.8 %collective-permute-start.19 = (bf16[4,208,768]{2,1,0:T(8,128)(2,1)}, bf16[4,208,768]{2,1,0:T(8,128)(2,1)}, u32[]{:S(2)}, u32[]{:S(2)}) collective-permute-start(bf16[4,208,768]{2,1,0:T(8,128)(2,1)} %get-tuple-element.192), channel_id=1, source_target_pairs={{0,2},{1,3},{2,0},{3,1},{4,6},{5,7},{6,4},{7,5},{8,10},{9,11},{10,... | collective-permute-start | bytes 3833864 | tf_op jit(solution)/shard_map/ppermute | solution.py:1006
  292.1 22.0 %copy-start.10 = (bf16[2,4,192,768]{3,2,1,0:T(8,128)(2,1)S(1)}, bf16[2,4,192,768]{3,2,1,0:T(8,128)(2,1)}, u32[]{:S(2)}) copy-start(bf16[2,4,192,768]{3,2,1,0:T(8,128)(2,1)} %get-tuple-element.189) | copy-start | bytes 7077892
  322.1 25.9 %collective-permute-start.20 = (bf16[2,192,768]{2,1,0:T(8,128)(2,1)}, bf16[2,192,768]{2,1,0:T(8,128)(2,1)S(1)}, u32[]{:S(2)}, u32[]{:S(2)}) collective-permute-start(bf16[2,192,768]{2,1,0:T(8,128)(2,1)} %get-tuple-element.253), channel_id=1, source_target_pairs={{0,4},{4,0},{8,12},{12,8},{16,20},{20,16},{24,28},{28,24},{1,5},{5... | collective-permute-start | bytes 1769480 | tf_op jit(solution)/shard_map/ppermute | solution.py:1009
  323.7 27.4 %collective-permute-start.22 = (bf16[2,192,768]{2,1,0:T(8,128)(2,1)S(1)}, bf16[2,192,768]{2,1,0:T(8,128)(2,1)S(1)}, u32[]{:S(2)}, u32[]{:S(2)}) collective-permute-start(bf16[2,192,768]{2,1,0:T(8,128)(2,1)S(1)} %get-tuple-element.252), channel_id=1, source_target_pairs={{0,6},{1,7},{2,4},{3,5},{4,2},{5,3},{6,0},{7,1},{8,14},{9,15},{10,... | collective-permute-start | bytes 1769480 | tf_op jit(solution)/shard_map/ppermute | solution.py:1093
  325.2 27.2 %collective-permute-start.21 = (bf16[2,192,768]{2,1,0:T(8,128)(2,1)S(1)}, bf16[2,192,768]{2,1,0:T(8,128)(2,1)}, u32[]{:S(2)}, u32[]{:S(2)}) collective-permute-start(bf16[2,192,768]{2,1,0:T(8,128)(2,1)S(1)} %slice_bitcast_fusion.3), channel_id=1, source_target_pairs={{0,2},{1,3},{2,0},{3,1},{4,6},{5,7},{6,4},{7,5},{8,10},{9,11},{10,... | collective-permute-start | bytes 1769480 | tf_op jit(solution)/shard_map/ppermute | solution.py:1006
  353.8 14.4 %collective-permute-start.23 = (bf16[2,192,768]{2,1,0:T(8,128)(2,1)S(1)}, bf16[2,192,768]{2,1,0:T(8,128)(2,1)S(1)}, u32[]{:S(2)}, u32[]{:S(2)}) collective-permute-start(bf16[2,192,768]{2,1,0:T(8,128)(2,1)S(1)} %fusion), channel_id=1, source_target_pairs={{0,8},{4,12},{8,0},{12,4},{16,24},{20,28},{24,16},{28,20},{1,9},{5... | collective-permute-start | bytes 1769480 | tf_op jit(solution)/shard_map/ppermute | solution.py:1009
  354.9 13.5 %copy-start.20 = (f32[8,768]{1,0:T(8,128)S(1)}, f32[8,768]{1,0:T(8,128)}, u32[]{:S(2)}) copy-start(f32[8,768]{1,0:T(8,128)} %get-tuple-element.229) | copy-start | bytes 73732
  354.9 13.5 %copy-start.22 = (f32[2,1,768]{2,1,0:T(1,128)S(1)}, f32[2,1,768]{2,1,0:T(1,128)}, u32[]{:S(2)}) copy-start(f32[2,1,768]{2,1,0:T(1,128)} %get-tuple-element.225) | copy-start | bytes 18436
  354.9 13.5 %copy-start.21 = (f32[2,1,768]{2,1,0:T(1,128)S(1)}, f32[2,1,768]{2,1,0:T(1,128)}, u32[]{:S(2)}) copy-start(f32[2,1,768]{2,1,0:T(1,128)} %get-tuple-element.226) | copy-start | bytes 18436
  354.9 13.6 %copy-start.26 = (f32[4,1,768]{2,1,0:T(1,128)S(1)}, f32[4,1,768]{2,1,0:T(1,128)}, u32[]{:S(2)}) copy-start(f32[4,1,768]{2,1,0:T(1,128)} %get-tuple-element.224) | copy-start | bytes 36868
  354.9 13.8 %copy-start.18 = (f32[8,768]{1,0:T(8,128)S(1)}, f32[8,768]{1,0:T(8,128)}, u32[]{:S(2)}) copy-start(f32[8,768]{1,0:T(8,128)} %get-tuple-element.227) | copy-start | bytes 73732
  354.9 13.7 %copy-start.19 = (f32[8,768]{1,0:T(8,128)S(1)}, f32[8,768]{1,0:T(8,128)}, u32[]{:S(2)}) copy-start(f32[8,768]{1,0:T(8,128)} %get-tuple-element.228) | copy-start | bytes 73732
  368.3 7.1 %collective-permute-start.24 = (bf16[2,4,192,768]{3,2,1,0:T(8,128)(2,1)}, bf16[2,4,192,768]{3,2,1,0:T(8,128)(2,1)}, u32[]{:S(2)}, u32[]{:S(2)}) collective-permute-start(bf16[2,4,192,768]{3,2,1,0:T(8,128)(2,1)} %get-tuple-element.208), channel_id=1, source_target_pairs={{0,1},{1,0},{2,3},{3,2},{4,5},{5,4},{6,7},{7,6},{8,9},{9,8},{10,11... | collective-permute-start | bytes 7077896 | tf_op jit(solution)/shard_map/ppermute | solution.py:1006
  370.7 4.8 copy-start.9
  372.8 16.8 %collective-permute-start.27 = (bf16[192,768]{1,0:T(8,128)(2,1)}, bf16[192,768]{1,0:T(8,128)(2,1)S(1)}, u32[]{:S(2)}, u32[]{:S(2)}) collective-permute-start(bf16[192,768]{1,0:T(8,128)(2,1)} %get-tuple-element.259), channel_id=1, source_target_pairs={{0,16},{4,20},{8,24},{12,28},{16,0},{20,4},{24,8},{28,12},{1,17},{... | collective-permute-start | bytes 884744 | tf_op jit(solution)/shard_map/ppermute | solution.py:1009
  377.9 18.3 %copy-start.3 = (bf16[2,2,192,768]{3,2,1,0:T(8,128)(2,1)}, bf16[2,2,192,768]{3,2,1,0:T(8,128)(2,1)S(1)}, u32[]{:S(2)}) copy-start(bf16[2,2,192,768]{3,2,1,0:T(8,128)(2,1)S(1)} %get-tuple-element.246) | copy-start | bytes 3538948
  379.8 15.6 %collective-permute-start.25 = (bf16[2,192,768]{2,1,0:T(8,128)(2,1)}, bf16[2,192,768]{2,1,0:T(8,128)(2,1)S(1)}, u32[]{:S(2)}, u32[]{:S(2)}) collective-permute-start(bf16[2,192,768]{2,1,0:T(8,128)(2,1)} %pad_maximum_fusion.3), channel_id=1, source_target_pairs={{0,2},{1,3},{2,0},{3,1},{4,6},{5,7},{6,4},{7,5},{8,10},{9,11},{10,... | collective-permute-start | bytes 1769480 | tf_op jit(solution)/shard_map/ppermute | solution.py:1006
  380.3 15.4 %collective-permute-start.26 = (bf16[2,192,768]{2,1,0:T(8,128)(2,1)}, bf16[2,192,768]{2,1,0:T(8,128)(2,1)}, u32[]{:S(2)}, u32[]{:S(2)}) collective-permute-start(bf16[2,192,768]{2,1,0:T(8,128)(2,1)} %slice_bitcast_fusion.1), channel_id=1, source_target_pairs={{0,4},{4,0},{8,12},{12,8},{16,20},{20,16},{24,28},{28,24},{1,5},{5... | collective-permute-start | bytes 1769480 | tf_op jit(solution)/shard_map/ppermute | solution.py:1009
  381.8 7.8 %copy-start.7 = (bf16[2,192,768]{2,1,0:T(8,128)(2,1)S(1)}, bf16[2,192,768]{2,1,0:T(8,128)(2,1)}, u32[]{:S(2)}) copy-start(bf16[2,192,768]{2,1,0:T(8,128)(2,1)} %copy-done.6) | copy-start | bytes 1769476
  386.6 16.6 %copy-start.28 = (f32[8]{0:T(128)S(1)}, f32[8]{0:T(128)}, u32[]{:S(2)}) copy-start(f32[8]{0:T(128)} %copy-done.27) | copy-start | bytes 100
  395.8 15.3 %collective-permute-start.31 = (bf16[192,768]{1,0:T(8,128)(2,1)S(1)}, bf16[192,768]{1,0:T(8,128)(2,1)}, u32[]{:S(2)}, u32[]{:S(2)}) collective-permute-start(bf16[192,768]{1,0:T(8,128)(2,1)S(1)} %get-tuple-element.218), channel_id=1, source_target_pairs={{0,16},{4,20},{8,24},{12,28},{16,0},{20,4},{24,8},{28,12},{1,17},{... | collective-permute-start | bytes 884744 | tf_op jit(solution)/shard_map/ppermute | solution.py:1009
  397.8 14.3 %collective-permute-start.30 = (bf16[192,768]{1,0:T(8,128)(2,1)}, bf16[192,768]{1,0:T(8,128)(2,1)S(1)}, u32[]{:S(2)}, u32[]{:S(2)}) collective-permute-start(bf16[192,768]{1,0:T(8,128)(2,1)} %fusion.4), channel_id=1, source_target_pairs={{0,2},{1,3},{2,0},{3,1},{4,6},{5,7},{6,4},{7,5},{8,10},{9,11},{10,... | collective-permute-start | bytes 884744 | tf_op jit(solution)/shard_map/ppermute | solution.py:1006
  401.0 12.8 %copy-start.4 = (bf16[2,2,192,768]{3,2,1,0:T(8,128)(2,1)S(1)}, bf16[2,2,192,768]{3,2,1,0:T(8,128)(2,1)}, u32[]{:S(2)}) copy-start(bf16[2,2,192,768]{3,2,1,0:T(8,128)(2,1)} %copy-done.3) | copy-start | bytes 3538948
  401.0 11.1 %collective-permute-start.29 = (bf16[192,768]{1,0:T(8,128)(2,1)}, bf16[192,768]{1,0:T(8,128)(2,1)S(1)}, u32[]{:S(2)}, u32[]{:S(2)}) collective-permute-start(bf16[192,768]{1,0:T(8,128)(2,1)} %fusion.5), channel_id=1, source_target_pairs={{0,4},{4,0},{8,12},{12,8},{16,20},{20,16},{24,28},{28,24},{1,5},{5... | collective-permute-start | bytes 884744 | tf_op jit(solution)/shard_map/ppermute | solution.py:1009
  402.9 67.4 %collective-permute-start.32 = (bf16[768,768]{1,0:T(8,128)(2,1)}, bf16[768,768]{1,0:T(8,128)(2,1)}, u32[]{:S(2)}, u32[]{:S(2)}) collective-permute-start(bf16[768,768]{1,0:T(8,128)(2,1)} %all-reduce.5.cloned.1.call-done.m), channel_id=1, source_target_pairs={{0,4},{4,0},{8,12},{12,8},{16,20},{20,16},{24,28},{28,24},{1,5},{5... | collective-permute-start | bytes 3538952 | tf_op jit(solution)/shard_map/ppermute | solution.py:1009
  404.0 72.8 %collective-permute-start.28 = (bf16[4,208,768]{2,1,0:T(8,128)(2,1)}, bf16[4,208,768]{2,1,0:T(8,128)(2,1)}, u32[]{:S(2)}, u32[]{:S(2)}) collective-permute-start(bf16[4,208,768]{2,1,0:T(8,128)(2,1)} %get-tuple-element.216), channel_id=1, source_target_pairs={{0,2},{1,3},{2,0},{3,1},{4,6},{5,7},{6,4},{7,5},{8,10},{9,11},{10,... | collective-permute-start | bytes 3833864 | tf_op jit(solution)/shard_map/ppermute | solution.py:1006
  476.7 4.9 %copy-start.1 = (bf16[2,4,196,768]{3,1,2,0:T(4,128)(2,1)S(1)}, bf16[2,4,196,768]{3,1,2,0:T(4,128)(2,1)}, u32[]{:S(2)}) copy-start(bf16[2,4,196,768]{3,1,2,0:T(4,128)(2,1)} %param.13) | copy-start | bytes 7225348
  (15 other events, 29.6 us)
Sparse Core Ops, SparseCore 0:
  292.2 55.7 all-reduce.4
